TPU v7x, 512 devices: a whole 4x8x8 slice. The times are simulated.
512 devices in a mesh: gr: 32 (over y, x), gc: 16 (over z, core).
Axes of the slice: x: 4, y: 8, z: 8, core: 2. Of those that a mesh axis runs over, the one named last changes fastest.
Arguments:
- features: bfloat16 [16, 32, 512, 128], P('gc', 'gr'), may hold values from -6 to 6
- out_grad: bfloat16 [32, 16, 512, 128], P('gr', 'gc'), may hold values from -6 to 6
- weight: bfloat16 [128, 128], replicated, may hold values from -0.5 to 0.5
- block_values: bfloat16 [32, 16, 128, 128, 128], P('gr', 'gc'), may hold values from 0 to 0.03491211
- block_slot: int32 [32, 16, 128], P('gr', 'gc'), may hold values from 0 to 2047, as said below
- live_count: int32 [32, 16], P('gr', 'gc'), may hold values from 32 to 128, as said below
- row_need: int32 [32, 16, 16, 2], P('gr', 'gc'), may hold values from 0 to 3, as said below
- col_need: int32 [32, 16, 32, 2], P('gr', 'gc'), may hold values from 0 to 3, as said below
Outputs:
- activated: bfloat16 [32, 16, 512, 128], P('gr', 'gc')
- weight_grad: float32 [128, 128], replicated
- input_grad: bfloat16 [16, 32, 512, 128], P('gc', 'gr')
Inputs may be any that keep to these rules, and one draw needn't show every extreme that they name: `block_slot`: within one tile the 128 entries are distinct. `live_count`: each tile holds 128, 64 or 32 live slots; some tile holds 128 in every draw. `row_need`: the 2 entries for one tile and one owner are distinct. `col_need`: the 2 entries for one tile and one owner are distinct.
All inputs are finite; a program needn't handle non-finite values.
Results may differ from a plain program's by a relative error of at most 0.0069.
Values may be sent and summed in bfloat16 or wider, within the bound.
No kernel may reach another device: no remote copies, remote signals or barrier semaphores. Data moves between devices by JAX's collectives and lax.ppermute only.
A program may use at most 64 MiB of HBM per device.

v0:
```python
import jax
import jax.numpy as jnp
from jax import lax
from jax.sharding import PartitionSpec as P


def add_blocks(arrived, asked, per_dev):
    onehot = (jnp.arange(per_dev)[:, None] == asked[None, :]).astype(jnp.bfloat16)
    return jnp.dot(onehot, arrived, preferred_element_type=jnp.float32)


def on_device(features, out_grad, weight, block_values, block_slot, live_count, row_need, col_need):
    n_rows = lax.axis_size("gr")
    n_cols = lax.axis_size("gc")
    values = block_values[0, 0]
    slot_total = values.shape[0]
    blk = values.shape[1]
    local = features.shape[2]
    width = features.shape[3]
    per_dev = local // blk
    cap = row_need.shape[3]
    col_slots = n_rows * cap
    row_slots = n_cols * cap
    slots = block_slot[0, 0]
    live = jnp.arange(slot_total) < live_count[0, 0]
    row_of = slots // col_slots
    col_of = slots % col_slots
    row_target = jnp.where(live, row_of, row_slots)
    col_target = jnp.where(live, col_of, col_slots)
    row_asked = lax.all_to_all(row_need, "gc", split_axis=2, concat_axis=0, tiled=True).reshape(
        row_slots
    )
    col_asked = lax.all_to_all(col_need, "gr", split_axis=2, concat_axis=0, tiled=True).reshape(
        col_slots
    )
    gathered = lax.all_gather(features, "gr", axis=1, tiled=True).reshape(
        n_rows, per_dev, blk, width
    )
    picked = gathered[jnp.arange(n_rows)[:, None], col_need[0, 0]].reshape(col_slots, blk, width)
    terms = jnp.einsum("bmk,bkf->bmf", values, picked[col_of], preferred_element_type=jnp.float32)
    partial_value = jax.ops.segment_sum(terms, row_target, num_segments=row_slots + 1)[
        :row_slots
    ].astype(jnp.bfloat16)
    arrived = lax.all_to_all(
        partial_value.reshape(n_cols, cap, blk, width),
        "gc",
        split_axis=0,
        concat_axis=0,
        tiled=True,
    )
    aggregated = add_blocks(arrived.reshape(row_slots, blk * width), row_asked, per_dev)
    aggregated = aggregated.astype(jnp.bfloat16).reshape(local, width)
    pre = jnp.dot(aggregated, weight, preferred_element_type=jnp.float32)
    sig = jax.nn.sigmoid(pre)
    activated = (pre * sig).astype(jnp.bfloat16)
    upstream = out_grad[0, 0].astype(jnp.float32)
    grad_pre = (upstream * sig * (1.0 + pre * (1.0 - sig))).astype(jnp.bfloat16)
    local_term = lax.dot_general(
        aggregated, grad_pre, (((0,), (0,)), ((), ())), preferred_element_type=jnp.float32
    )
    node_total = local * n_rows * n_cols
    weight_grad = lax.psum(local_term, ("gr", "gc")) * float(node_total) ** (-0.5)
    back_rows = lax.dot_general(
        grad_pre, weight, (((1,), (1,)), ((), ())), preferred_element_type=jnp.float32
    )
    back_rows = back_rows.astype(jnp.bfloat16)
    gathered_rows = lax.all_gather(back_rows.reshape(1, local, width), "gc", axis=0, tiled=True)
    gathered_rows = gathered_rows.reshape(n_cols, per_dev, blk, width)
    picked_rows = gathered_rows[jnp.arange(n_cols)[:, None], row_need[0, 0]].reshape(
        row_slots, blk, width
    )
    back_terms = jnp.einsum(
        "bmk,bmf->bkf", values, picked_rows[row_of], preferred_element_type=jnp.float32
    )
    partial_back = jax.ops.segment_sum(back_terms, col_target, num_segments=col_slots + 1)[
        :col_slots
    ].astype(jnp.bfloat16)
    returned = lax.all_to_all(
        partial_back.reshape(n_rows, cap, blk, width), "gr", split_axis=0, concat_axis=0, tiled=True
    )
    input_grad = add_blocks(returned.reshape(col_slots, blk * width), col_asked, per_dev)
    input_grad = input_grad.astype(jnp.bfloat16).reshape(1, 1, local, width)
    return (activated.reshape(1, 1, local, width), weight_grad, input_grad)


def solution(mesh):
    placed = (
        P("gc", "gr", None, None),
        P("gr", "gc", None, None),
        P(),
        P("gr", "gc", None, None, None),
        P("gr", "gc", None),
        P("gr", "gc"),
        P("gr", "gc", None, None),
        P("gr", "gc", None, None),
    )
    return jax.shard_map(
        on_device,
        mesh=mesh,
        in_specs=placed,
        out_specs=(P("gr", "gc", None, None), P(), P("gc", "gr", None, None)),
        check_vma=False,
    )
```

profile of v0, /device:TPU:1, one launch (start us, length us, event | category | flops | bytes accessed | tf_op | source)
XLA Modules:
  0.0 572.5 jit_solution(11141833442630652047)
XLA Ops:
  7.2 0.7 all-gather.4.cloned.1.call-update
  7.9 1.4 copy.25
  9.3 11.8 %all-to-all-start = ((s32[1,1,16,2]{3,1,0,2:T(1,128)}), s32[1,1,16,2]{3,1,0,2:T(1,128)S(1)}, u32[]{:S(2)}, u32[]{:S(2)}) async-start(s32[1,1,16,2]{3,1,0,2:T(1,128)} %copy.25), calls=%async_computation | async-start | bytes 16384 | tf_op jit(solution)/shard_map/all_to_all | solution.py:30
  21.7 0.7 fusion.19
  23.3 76.9 %all-gather.4.cloned.1.call-done = bf16[1,32,512,128]{3,2,0,1:T(8,128)(2,1)} async-done(((bf16[1,1,512,128]{3,2,0,1:T(8,128)(2,1)}), bf16[1,32,512,128]{3,2,0,1:T(8,128)(2,1)}) %all-gather.4.cloned.1.call-update) | async-done | bytes 4194320 | tf_op jit(solution)/shard_map/all_gather | solution.py:36
  100.2 3.1 gather_fusion
  103.3 3.1 gather_fusion.1
  106.4 9.8 %fusion.4 = f32[128,128,128]{1,2,0:T(8,128)} fusion(bf16[128,128,128]{2,1,0:T(8,128)(2,1)} %gather_fusion.1, bf16[1,1,128,128,128]{4,3,2,1,0:T(8,128)(2,1)} %param.11), kind=kOutput, calls=%fused_computation.13 | convolution fusion | flops 536870912 | bytes 16777216 | tf_op jit(solution)/shard_map/bmk,bkf->bmf/dot_general | solution.py:40
  116.1 9.0 %copy.29 = f32[128,128,128]{2,1,0:T(8,128)} copy(f32[128,128,128]{1,2,0:T(8,128)} %fusion.4) | data formatting | bytes 16777216 | tf_op jit(solution)/shard_map/bmk,bkf->bmf/dot_general | solution.py:40
  125.4 17.0 %scatter_fusion = f32[33,128,128]{2,1,0:T(8,128)S(1)} fusion(f32[33,128,128]{2,1,0:T(8,128)S(1)} %broadcast_in_dim.13, s32[128]{0:T(128)S(1)} %get-tuple-element.10, f32[128,128,128]{2,1,0:T(8,128)} %copy.29), kind=kCustom, calls=%fused_computation.4 | custom fusion | flops 2097152 | bytes 25166336 | tf_op jit(solution)/shard_map/scatter-add | solution.py:41
  142.4 1.1 slice.23
  143.6 11.6 %all-to-all-start.1 = ((bf16[16,2,128,128]{3,2,1,0:T(8,128)(2,1)}), bf16[16,2,128,128]{3,2,1,0:T(8,128)(2,1)S(1)}, u32[]{:S(2)}, u32[]{:S(2)}) async-start(bf16[16,2,128,128]{3,2,1,0:T(8,128)(2,1)} %bitcast.9), calls=%async_computation.1 | async-start | bytes 2097152 | tf_op jit(solution)/shard_map/all_to_all | solution.py:44
  156.5 26.6 %all-to-all-done.1 = bf16[16,2,128,128]{3,2,1,0:T(8,128)(2,1)S(1)} async-done(((bf16[16,2,128,128]{3,2,1,0:T(8,128)(2,1)}), bf16[16,2,128,128]{3,2,1,0:T(8,128)(2,1)S(1)}, u32[]{:S(2)}, u32[]{:S(2)}) %all-to-all-start.1) | async-done | bytes 1048608 | tf_op jit(solution)/shard_map/all_to_all | solution.py:44
  183.2 0.7 convolution_convert_fusion.1
  184.0 0.9 fusion.15
  184.9 0.8 convolution_convert_fusion.2
  185.8 0.7 copy.30
  186.5 5.2 all-to-all-start.2
  191.9 29.9 %all-gather.6.cloned.1.call-done = bf16[8192,128]{1,0:T(8,128)(2,1)} async-done(((bf16[512,128]{1,0:T(8,128)(2,1)}), bf16[8192,128]{1,0:T(8,128)(2,1)}) %all-gather.6.cloned.1.call-update) | async-done | bytes 2097168 | tf_op jit(solution)/shard_map/all_gather | solution.py:67
  221.8 2.3 gather_fusion.2
  224.2 3.0 gather_fusion.3
  227.2 8.2 %fusion.7 = f32[128,128,128]{1,2,0:T(8,128)} fusion(bf16[128,128,128]{2,1,0:T(8,128)(2,1)} %gather_fusion.3, bf16[1,1,128,128,128]{4,3,2,1,0:T(8,128)(2,1)} %param.11), kind=kOutput, calls=%fused_computation.14 | convolution fusion | flops 536870912 | bytes 16777216 | tf_op jit(solution)/shard_map/bmk,bmf->bkf/dot_general | solution.py:72
  235.5 9.0 %copy.33 = f32[128,128,128]{2,1,0:T(8,128)} copy(f32[128,128,128]{1,2,0:T(8,128)} %fusion.7) | data formatting | bytes 16777216 | tf_op jit(solution)/shard_map/bmk,bmf->bkf/dot_general | solution.py:72
  244.5 2.5 broadcast_in_dim.16
  247.0 28.1 %scatter_fusion.1 = f32[65,128,128]{2,1,0:T(8,128)} fusion(f32[65,128,128]{2,1,0:T(8,128)} %broadcast_in_dim.16, s32[128]{0:T(128)S(1)} %get-tuple-element.8, f32[128,128,128]{2,1,0:T(8,128)} %copy.33), kind=kCustom, calls=%fused_computation.5 | custom fusion | flops 2097152 | bytes 25166336 | tf_op jit(solution)/shard_map/scatter-add | solution.py:75
  275.1 3.9 slice.22
  279.0 8.8 %all-to-all-start.3 = ((bf16[32,2,128,128]{3,2,1,0:T(8,128)(2,1)}), bf16[32,2,128,128]{3,2,1,0:T(8,128)(2,1)S(1)}, u32[]{:S(2)}, u32[]{:S(2)}) async-start(bf16[32,2,128,128]{3,2,1,0:T(8,128)(2,1)} %bitcast.17), calls=%async_computation.3 | async-start | bytes 4194304 | tf_op jit(solution)/shard_map/all_to_all | solution.py:78
  288.0 0.9 fusion.29
  289.6 272.8 %all-reduce.2.cloned.1.call-done = f32[128,128]{1,0:T(8,128)} async-done(((f32[128,128]{1,0:T(8,128)}), f32[128,128]{1,0:T(8,128)}) %all-reduce.2.cloned.1.call-update) | async-done | bytes 65552 | tf_op jit(solution)/shard_map/psum | solution.py:62
  562.4 1.5 broadcast_multiply_fusion
  563.9 1.2 convolution_convert_fusion
  565.2 0.8 reshape.282
  (34 shorter events, 3.7 us)
Async XLA Ops:
  7.2 176.8 %copy-start = (bf16[128,128]{1,0:T(8,128)(2,1)S(1)}, bf16[128,128]{1,0:T(8,128)(2,1)}, u32[]{:S(2)}) copy-start(bf16[128,128]{1,0:T(8,128)(2,1)} %param.10) | copy-start | bytes 98308
  7.2 93.0 %all-gather.4.cloned.1.call-start = ((), (), s32[]{:S(2)}) async-start(), calls=%async_computation.4 | async-start | bytes 4325376 | tf_op jit(solution)/shard_map/all_gather | solution.py:36
  9.3 134.3 %all-to-all-start = ((s32[1,1,16,2]{3,1,0,2:T(1,128)}), s32[1,1,16,2]{3,1,0,2:T(1,128)S(1)}, u32[]{:S(2)}, u32[]{:S(2)}) async-start(s32[1,1,16,2]{3,1,0,2:T(1,128)} %copy.25), calls=%async_computation | async-start | bytes 16384 | tf_op jit(solution)/shard_map/all_to_all | solution.py:30
  142.4 41.6 %copy-start.4 = (bf16[1,1,512,128]{3,2,1,0:T(8,128)(2,1)S(1)}, bf16[1,1,512,128]{3,2,1,0:T(8,128)(2,1)}, u32[]{:S(2)}) copy-start(bf16[1,1,512,128]{3,2,1,0:T(8,128)(2,1)} %param.9) | copy-start | bytes 393220
  142.4 43.4 %copy-start.2 = (s32[1,1,32,2]{2,3,1,0:T(2,128)S(1)}, s32[1,1,32,2]{2,3,1,0:T(2,128)}, u32[]{:S(2)}) copy-start(s32[1,1,32,2]{2,3,1,0:T(2,128)} %param.15) | copy-start | bytes 772
  142.4 49.3 %copy-start.3 = (s32[1,1,16,2]{2,3,1,0:T(2,128)S(1)}, s32[1,1,16,2]{2,3,1,0:T(2,128)}, u32[]{:S(2)}) copy-start(s32[1,1,16,2]{2,3,1,0:T(2,128)} %param.14) | copy-start | bytes 388
  143.6 39.6 %all-to-all-start.1 = ((bf16[16,2,128,128]{3,2,1,0:T(8,128)(2,1)}), bf16[16,2,128,128]{3,2,1,0:T(8,128)(2,1)S(1)}, u32[]{:S(2)}, u32[]{:S(2)}) async-start(bf16[16,2,128,128]{3,2,1,0:T(8,128)(2,1)} %bitcast.9), calls=%async_computation.1 | async-start | bytes 2097152 | tf_op jit(solution)/shard_map/all_to_all | solution.py:44
  155.2 66.7 %all-gather.6.cloned.1.call-start = ((), (), s32[]{:S(2)}) async-start(), calls=%async_computation.6 | async-start | bytes 2228224 | tf_op jit(solution)/shard_map/all_gather | solution.py:67
  186.5 92.5 %all-to-all-start.2 = ((s32[1,1,32,2]{3,1,0,2:T(1,128)}), s32[1,1,32,2]{3,1,0,2:T(1,128)S(1)}, u32[]{:S(2)}, u32[]{:S(2)}) async-start(s32[1,1,32,2]{3,1,0,2:T(1,128)} %copy.30), calls=%async_computation.2 | async-start | bytes 32768 | tf_op jit(solution)/shard_map/all_to_all | solution.py:33
  275.1 290.8 %copy-start.1 = (bf16[128,128]{1,0:T(8,128)(2,1)S(1)}, bf16[128,128]{1,0:T(8,128)(2,1)}, u32[]{:S(2)}) copy-start(bf16[128,128]{1,0:T(8,128)(2,1)} %param.10) | copy-start | bytes 98308
  279.0 284.9 %all-to-all-start.3 = ((bf16[32,2,128,128]{3,2,1,0:T(8,128)(2,1)}), bf16[32,2,128,128]{3,2,1,0:T(8,128)(2,1)S(1)}, u32[]{:S(2)}, u32[]{:S(2)}) async-start(bf16[32,2,128,128]{3,2,1,0:T(8,128)(2,1)} %bitcast.17), calls=%async_computation.3 | async-start | bytes 4194304 | tf_op jit(solution)/shard_map/all_to_all | solution.py:78
  287.9 274.5 %all-reduce.2.cloned.1.call-start = ((), (), s32[]{:S(2)}) async-start(), calls=%async_computation.5 | async-start | bytes 131072 | tf_op jit(solution)/shard_map/psum | solution.py:62
Sparse Core Ops, SparseCore 0:
  11.2 88.9 all-gather.3
  185.9 35.8 all-gather.5
  294.3 268.1 all-reduce.1
where the time goes:
time: 575 us; the launch traced here: 573 us
  waiting for transfers between devices  407 us (71%)
  other arithmetic  49.3 us (9%)
  local copies, waits for them, and re-layouts  41.5 us (7%)
  starting transfers between devices  37.6 us (7%)
  matrix products  22.5 us (4%)
  between operations  14.6 us (3%)
    psum x1, waiting for transfers between devices, on_device(): lax.psum(local_term, ('gr', 'gc')) * float(node_total) ** (-0.5)  273 us
    all_gather x1, waiting for transfers between devices, on_device(): lax.all_gather(features, 'gr', axis=1, tiled=True)  76.9 us
    all_gather x1, waiting for transfers between devices, on_device(): lax.all_gather(back_rows.reshape(1, local, width), 'gc', axis=0, tiled=True)  29.9 us
    scatter-add x1, other arithmetic, on_device(): jax.ops.segment_sum(back_terms, col_target, num_segments=col_slots + 1)  28.1 us
    all_to_all x1, waiting for transfers between devices, on_device(): lax.all_to_all(partial_value.reshape(n_cols, cap, blk, width), 'gc', spli...  26.6 us
    scatter-add x1, other arithmetic, on_device(): jax.ops.segment_sum(terms, row_target, num_segments=row_slots + 1)  17 us
    all_to_all x1, starting transfers between devices, on_device(): lax.all_to_all(row_need, 'gc', split_axis=2, concat_axis=0, tiled=True)  11.8 us
    all_to_all x1, starting transfers between devices, on_device(): lax.all_to_all(partial_value.reshape(n_cols, cap, blk, width), 'gc', spli...  11.6 us
  transfers between devices with their start and end apart: 7, of which 4 were waited for; matrix products, arithmetic and copies ran while one was open for 19% of the time, Pallas kernels for 0%

commit v1 on v0

v1 whole, which is shorter than its diff:
```python
import jax
import jax.numpy as jnp
from jax import lax
from jax.experimental import pallas as pl
from jax.experimental.pallas import tpu as pltpu
from jax.sharding import PartitionSpec as P

F32 = jnp.float32
BF16 = jnp.bfloat16
EXTRA = 16
GROUP = 8

VMEM = pl.BlockSpec(memory_space=pltpu.VMEM)
SMEM = pl.BlockSpec(memory_space=pltpu.SMEM)


def call(kernel, out_shape, in_specs, scratch=(), flops=0, moved=0):
    many = isinstance(out_shape, (tuple, list))
    return pl.pallas_call(
        kernel,
        out_shape=out_shape,
        in_specs=in_specs,
        out_specs=tuple(VMEM for _ in out_shape) if many else VMEM,
        scratch_shapes=list(scratch),
        cost_estimate=pl.CostEstimate(flops=flops, bytes_accessed=moved, transcendentals=0),
        compiler_params=pltpu.CompilerParams(vmem_limit_bytes=48 * 1024 * 1024),
    )


def pick_kernel(asked, feats, out):
    n, _, _ = out.shape
    blk = out.shape[1] // 2

    def step(r, carry):
        for k in range(2):
            start = pl.multiple_of(asked[r, k] * blk, blk)
            out[r, k * blk : (k + 1) * blk, :] = feats[pl.ds(start, blk), :]
        return carry

    lax.fori_loop(0, n, step, 0, unroll=4)


def forward_kernel(col_slots, slots, live, row_need, values, arrived, out, acc):
    n, _, width = out.shape
    blk = values.shape[1]
    acc[...] = jnp.zeros_like(acc)

    def group(g, carry):
        for u in range(GROUP):
            b = g * GROUP + u
            slot = slots[0, b]
            row = slot // col_slots
            col = slot % col_slots
            feats = arrived[col // 2, pl.ds(pl.multiple_of((col % 2) * blk, blk), blk), :]
            acc[row] += jnp.dot(values[b], feats, preferred_element_type=F32)
        return carry

    lax.fori_loop(0, live[0, 0] // GROUP, group, 0)
    sub = lax.broadcasted_iota(jnp.int32, (EXTRA, width), 0)
    for c in range(n):
        for k in range(2):
            out[c, k * blk : (k + 1) * blk, :] = acc[2 * c + k].astype(BF16)
        ids = jnp.where(sub < EXTRA // 2, row_need[c, 0], row_need[c, 1])
        out[c, 2 * blk :, :] = ids.astype(F32).astype(BF16)


def middle_kernel(arrived, weight, upstream, act, out, agg, back):
    n, rows, width = arrived.shape
    blk = (rows - EXTRA) // 2
    per_dev = upstream.shape[0] // blk
    ids = []
    for c in range(n):
        tail = arrived[c, 2 * blk :, :].astype(F32)
        ids.append((tail[0:1, :], tail[EXTRA // 2 : EXTRA // 2 + 1, :]))
    w = weight[...]
    total = jnp.zeros((width, width), F32)
    for q in range(per_dev):
        acc = jnp.zeros((blk, width), F32)
        for c in range(n):
            for k in range(2):
                term = arrived[c, k * blk : (k + 1) * blk, :].astype(F32)
                acc = acc + jnp.where(ids[c][k] == float(q), term, 0.0)
        a = acc.astype(BF16)
        pre = jnp.dot(a, w, preferred_element_type=F32)
        sig = jax.nn.sigmoid(pre)
        act[q * blk : (q + 1) * blk, :] = (pre * sig).astype(BF16)
        up = upstream[q * blk : (q + 1) * blk, :].astype(F32)
        grad = (up * sig * (1.0 + pre * (1.0 - sig))).astype(BF16)
        total = total + lax.dot_general(a, grad, (((0,), (0,)), ((), ())), preferred_element_type=F32)
        back[q] = lax.dot_general(
            grad, w, (((1,), (1,)), ((), ())), preferred_element_type=F32
        ).astype(BF16)
    high = total.astype(BF16).astype(F32)
    low = total - high
    step = width // n
    for c in range(n):
        for k in range(2):
            chosen = back[0]
            for q in range(1, per_dev):
                chosen = jnp.where(ids[c][k].astype(BF16) == float(q), back[q], chosen)
            out[c, k * blk : (k + 1) * blk, :] = chosen
        pair = [high[c * step : (c + 1) * step, :], low[c * step : (c + 1) * step, :]]
        out[c, 2 * blk :, :] = jnp.concatenate(pair, axis=0).astype(BF16)


def backward_kernel(col_slots, slots, live, values, arrived, out, acc):
    blk = values.shape[1]
    acc[...] = jnp.zeros_like(acc)

    def group(g, carry):
        for u in range(GROUP):
            b = g * GROUP + u
            slot = slots[0, b]
            row = slot // col_slots
            col = slot % col_slots
            grads = arrived[row // 2, pl.ds(pl.multiple_of((row % 2) * blk, blk), blk), :]
            acc[col] += lax.dot_general(
                values[b], grads, (((0,), (0,)), ((), ())), preferred_element_type=F32
            )
        return carry

    lax.fori_loop(0, live[0, 0] // GROUP, group, 0)
    for r in range(out.shape[0]):
        for k in range(2):
            out[r, k * blk : (k + 1) * blk, :] = acc[2 * r + k].astype(BF16)


def final_kernel(asked, arrived, out, acc):
    n, rows, _ = arrived.shape
    blk = rows // 2
    acc[...] = jnp.zeros_like(acc)

    def step(r, carry):
        for k in range(2):
            term = arrived[r, k * blk : (k + 1) * blk, :].astype(F32)
            acc[asked[r, k]] += term
        return carry

    lax.fori_loop(0, n, step, 0, unroll=2)
    for q in range(acc.shape[0]):
        out[q * blk : (q + 1) * blk, :] = acc[q].astype(BF16)


def on_device(features, out_grad, weight, block_values, block_slot, live_count, row_need, col_need):
    import functools

    n_rows = lax.axis_size("gr")
    n_cols = lax.axis_size("gc")
    values = block_values[0, 0]
    slot_total, blk, _ = values.shape
    local, width = features.shape[2:]
    cap = row_need.shape[3]
    per_dev = local // blk
    col_slots = n_rows * cap
    row_slots = n_cols * cap
    slots = block_slot[0]
    step = width // n_cols
    work = 2 * slot_total * blk * blk * width

    need = jnp.pad(col_need[0, 0], ((0, 0), (0, 128 - cap))).reshape(n_rows, 1, 128)
    asked = lax.all_to_all(need, "gr", split_axis=0, concat_axis=0, tiled=True)
    asked = asked.reshape(n_rows, 128)
    chosen = call(
        pick_kernel,
        jax.ShapeDtypeStruct((n_rows, cap * blk, width), BF16),
        [SMEM, VMEM],
        moved=4 << 20,
    )(asked, features[0, 0])
    arrived = lax.all_to_all(chosen, "gr", split_axis=0, concat_axis=0, tiled=True)
    partial = call(
        functools.partial(forward_kernel, col_slots),
        jax.ShapeDtypeStruct((n_cols, cap * blk + EXTRA, width), BF16),
        [SMEM, SMEM, SMEM, VMEM, VMEM],
        [pltpu.VMEM((row_slots, blk, width), F32)],
        flops=work,
        moved=8 << 20,
    )(slots, live_count, row_need[0, 0], values, arrived)
    partial = lax.all_to_all(partial, "gc", split_axis=0, concat_axis=0, tiled=True)
    activated, back = call(
        middle_kernel,
        (
            jax.ShapeDtypeStruct((local, width), BF16),
            jax.ShapeDtypeStruct((n_cols, cap * blk + EXTRA, width), BF16),
        ),
        [VMEM, VMEM, VMEM],
        [pltpu.VMEM((per_dev, blk, width), BF16), pltpu.VMEM((per_dev, blk, width), BF16)],
        flops=work // 8,
        moved=4 << 20,
    )(partial, weight, out_grad[0, 0])
    back = lax.all_to_all(back, "gc", split_axis=0, concat_axis=0, tiled=True)
    tail = back[:, cap * blk :, :].astype(F32).sum(0)
    tail = tail[:step] + tail[step:]
    tail = jnp.broadcast_to(tail[None], (n_rows, step, width))
    tail = lax.all_to_all(tail, "gr", split_axis=0, concat_axis=0, tiled=True).sum(0)
    tail = jnp.broadcast_to(tail[None], (n_cols, step, width))
    tail = lax.all_to_all(tail, "gc", split_axis=0, concat_axis=0, tiled=True)
    node_total = local * n_rows * n_cols
    weight_grad = tail.reshape(width, width) * float(node_total) ** (-0.5)
    returned = call(
        functools.partial(backward_kernel, col_slots),
        jax.ShapeDtypeStruct((n_rows, cap * blk, width), BF16),
        [SMEM, SMEM, VMEM, VMEM],
        [pltpu.VMEM((col_slots, blk, width), F32)],
        flops=work,
        moved=8 << 20,
    )(slots, live_count, values, back)
    returned = lax.all_to_all(returned, "gr", split_axis=0, concat_axis=0, tiled=True)
    input_grad = call(
        final_kernel,
        jax.ShapeDtypeStruct((local, width), BF16),
        [SMEM, VMEM],
        [pltpu.VMEM((per_dev, blk, width), F32)],
        moved=4 << 20,
    )(asked, returned)
    return (
        activated.reshape(1, 1, local, width),
        weight_grad,
        input_grad.reshape(1, 1, local, width),
    )


def solution(mesh):
    placed = (
        P("gc", "gr", None, None),
        P("gr", "gc", None, None),
        P(),
        P("gr", "gc", None, None, None),
        P("gr", "gc", None),
        P("gr", "gc"),
        P("gr", "gc", None, None),
        P("gr", "gc", None, None),
    )
    return jax.shard_map(
        on_device,
        mesh=mesh,
        in_specs=placed,
        out_specs=(P("gr", "gc", None, None), P(), P("gc", "gr", None, None)),
        check_vma=False,
    )
```

time: 575 us -> 247 us (0.43)
  waiting for transfers between devices: 407 us -> 97.2 us
  blocking collectives: 0 us -> 111 us
  other arithmetic: 49.3 us -> 0.69 us
  local copies, waits for them, and re-layouts: 41.5 us -> 5.07 us
  starting transfers between devices: 37.6 us -> 13 us
  matrix products: 22.5 us -> 0 us
  Pallas kernels: 0 us -> 18.6 us
  between operations: 14.6 us -> 1.39 us
    psum x1 -> x0, waiting for transfers between devices: 273 us -> none  [on_device(): lax.psum(local_term, ('gr', 'gc')) * float(node_total) ** (-0.5)]
    all_to_all x0 -> x4, blocking collectives: none -> 111 us  [the longest x1 43.1 us: on_device(): lax.all_to_all(partial, 'gc', split_axis=0, concat_axis=0, tiled=True)]
    all_gather x2 -> x0, waiting for transfers between devices: 107 us -> none  [the longest x1 76.9 us: on_device(): lax.all_gather(features, 'gr', axis=1, tiled=True)]
    all_to_all x4 -> x3, waiting for transfers between devices: 26.6 us -> 97.2 us  [the longest x1 50.9 us: on_device(): lax.all_to_all(returned, 'gr', split_axis=0, concat_axis=0, tiled=True)]
    scatter-add x2 -> x0, other arithmetic: 45.2 us -> none  [the longest x1 28.1 us: on_device(): jax.ops.segment_sum(back_terms, col_target, num_segments=col_slots + 1)]
    all_to_all x4 -> x3, starting transfers between devices: 37.5 us -> 13 us  [the longest x1 4.83 us: on_device(): tail = lax.all_to_all(tail, 'gc', split_axis=0, concat_axis=0, tiled=True)]
    dot_general x7 -> x0, matrix products: 22.5 us -> none  [the longest x1 9.76 us: on_device(): jnp.einsum('bmk,bkf->bmf', values, picked[col_of], preferred_element_type...]
    pallas_call x0 -> x5, Pallas kernels: none -> 18.6 us  [the longest x1 7.08 us: on_device(): call(functools.partial(backward_kernel, col_slots), jax.ShapeDtypeStruct(...]
  transfers between devices with their start and end apart: 7 -> 3, of which waited for: 4 -> 2; matrix products, arithmetic and copies ran while one was open for 19% -> 0% of each run, Pallas kernels for 0% -> 3%
where the time goes in v1:
time: 247 us
  blocking collectives  111 us (45%)
  waiting for transfers between devices  97.2 us (39%)
  Pallas kernels  18.6 us (8%)
  starting transfers between devices  13 us (5%)
  local copies, waits for them, and re-layouts  5.07 us (2%)
    all_to_all x1, waiting for transfers between devices, on_device(): lax.all_to_all(returned, 'gr', split_axis=0, concat_axis=0, tiled=True)  50.9 us
    all_to_all x1, waiting for transfers between devices, on_device(): lax.all_to_all(chosen, 'gr', split_axis=0, concat_axis=0, tiled=True)  46.3 us
    all_to_all x1, blocking collectives, on_device(): lax.all_to_all(partial, 'gc', split_axis=0, concat_axis=0, tiled=True)  43.1 us
    all_to_all x1, blocking collectives, on_device(): back = lax.all_to_all(back, 'gc', split_axis=0, concat_axis=0, tiled=True)  32.8 us
    all_to_all x1, blocking collectives, on_device(): asked = lax.all_to_all(need, 'gr', split_axis=0, concat_axis=0, tiled=True)  18.9 us
    all_to_all x1, blocking collectives, on_device(): lax.all_to_all(tail, 'gr', split_axis=0, concat_axis=0, tiled=True).sum(0)  16.6 us
    pallas_call x1, Pallas kernels, on_device(): call(functools.partial(backward_kernel, col_slots), jax.ShapeDtypeStruct(...  7.08 us
    pallas_call x1, Pallas kernels, on_device(): call(functools.partial(forward_kernel, col_slots), jax.ShapeDtypeStruct((...  6.53 us
  transfers between devices with their start and end apart: 3, of which 2 were waited for; matrix products, arithmetic and copies ran while one was open for 0% of the time, Pallas kernels for 3%

profile of v1, /device:TPU:1, one launch (start us, length us, event | category | flops | bytes accessed | tf_op | source)
XLA Modules:
  0.0 247.5 jit_solution(15270705123743135373)
XLA Ops:
  0.6 0.7 pad_bitcast_fusion
  1.3 0.1 copy.15
  1.4 18.9 %all_to_all.35 = s32[32,1,128]{2,1,0:T(1,128)S(1)} all-to-all(s32[32,1,128]{2,1,0:T(1,128)S(1)} %copy.15), channel_id=1, replica_groups=mesh['gr'=32,'gc'=16] {'gr'}, dimensions={0} | all-to-all | bytes 32768 | tf_op jit(solution)/shard_map/all_to_all | solution.py:161
  20.3 0.0 copy-start.2
  20.3 0.9 copy-done.2
  21.2 1.0 shard_map.103
  22.2 0.0 copy-start
  22.2 1.3 copy-done
  23.5 4.1 %all-to-all-start.1 = ((bf16[32,256,128]{2,1,0:T(8,128)(2,1)}), bf16[32,256,128]{2,1,0:T(8,128)(2,1)S(1)}, u32[]{:S(2)}, u32[]{:S(2)}) async-start(bf16[32,256,128]{2,1,0:T(8,128)(2,1)} %copy-done), calls=%async_computation.1 | async-start | bytes 4194304 | tf_op jit(solution)/shard_map/all_to_all | solution.py:169
  28.3 0.0 copy-done.6
  28.3 0.1 copy.16.row_need
  28.4 46.3 %all-to-all-done.1.arrived = bf16[32,256,128]{2,1,0:T(8,128)(2,1)S(1)} async-done(((bf16[32,256,128]{2,1,0:T(8,128)(2,1)}), bf16[32,256,128]{2,1,0:T(8,128)(2,1)S(1)}, u32[]{:S(2)}, u32[]{:S(2)}) %all-to-all-start.1) | async-done | bytes 2097184 | tf_op jit(solution)/shard_map/all_to_all | solution.py:169
  74.7 0.0 copy-done.5
  74.7 6.5 %shard_map.104 = bf16[16,272,128]{2,1,0:T(8,128)(2,1)S(1)} custom-call(s32[1,128]{1,0:T(1,128)S(1)} %bitcast.17, s32[1,1]{1,0:T(1,128)S(6)} %copy.17.live, s32[16,2]{1,0:T(8,128)S(1)} %copy.16.row_need, bf16[128,128,128]{2,1,0:T(8,128)(2,1)} %bitcast.19, bf16[32,256,128]{2,1,0:T(8,128)(2,1)S(1)} %all-to-all-done.1.arrived), custom_call_target="tpu_custom_call" | custom-call | flops 536870912 | bytes 8388608 | tf_op jit(solution)/shard_map/pallas_call | solution.py:170
  81.2 0.0 copy-start.3
  81.3 0.0 copy-start.4
  81.3 43.1 %all_to_all.36.arrived = bf16[16,272,128]{2,1,0:T(8,128)(2,1)S(1)} all-to-all(bf16[16,272,128]{2,1,0:T(8,128)(2,1)S(1)} %shard_map.104), channel_id=1, replica_groups=mesh['gr'=32,'gc'=16] {'gc'}, dimensions={0} | all-to-all | bytes 2228224 | tf_op jit(solution)/shard_map/all_to_all | solution.py:178
  124.4 0.0 copy-done.3
  124.4 0.0 copy-done.4
  124.4 2.1 shard_map.105
  126.5 32.8 %all_to_all.37.arrived = bf16[16,272,128]{2,1,0:T(8,128)(2,1)S(1)} all-to-all(bf16[16,272,128]{2,1,0:T(8,128)(2,1)S(1)} %get-tuple-element.6), channel_id=1, replica_groups=mesh['gr'=32,'gc'=16] {'gc'}, dimensions={0} | all-to-all | bytes 2228224 | tf_op jit(solution)/shard_map/all_to_all | solution.py:190
  159.3 16.6 %all_to_all.38 = f32[32,8,128]{2,1,0:T(8,128)S(1)} all-to-all(f32[32,8,128]{2,1,0:T(8,128)S(1)} %broadcast_in_dim.4), channel_id=1, replica_groups=mesh['gr'=32,'gc'=16] {'gr'}, dimensions={0} | all-to-all | bytes 262144 | tf_op jit(solution)/shard_map/all_to_all | solution.py:194
  176.0 0.6 broadcast_in_dim.5
  176.6 4.8 %all-to-all-start.5 = ((f32[16,8,128]{2,1,0:T(8,128)}), f32[16,8,128]{2,1,0:T(8,128)S(1)}, u32[]{:S(2)}, u32[]{:S(2)}) async-start(f32[16,8,128]{2,1,0:T(8,128)} %broadcast_in_dim.5), calls=%async_computation.5 | async-start | bytes 131072 | tf_op jit(solution)/shard_map/all_to_all | solution.py:196
  181.5 7.1 %shard_map.106 = bf16[32,256,128]{2,1,0:T(8,128)(2,1)S(1)} custom-call(s32[1,128]{1,0:T(1,128)S(1)} %bitcast.18, s32[1,1]{1,0:T(1,128)S(6)} %copy.17.live, bf16[128,128,128]{2,1,0:T(8,128)(2,1)} %bitcast.20, bf16[16,272,128]{2,1,0:T(8,128)(2,1)S(1)} %all_to_all.37.arrived), custom_call_target="tpu_custom_call" | custom-call | flops 536870912 | bytes 8388608 | tf_op jit(solution)/shard_map/pallas_call | solution.py:199
  188.5 0.0 copy-start.1
  188.6 1.3 copy-done.1
  189.9 0.0 all-to-all-done.5
  189.9 4.0 %all-to-all-start.6 = ((bf16[32,256,128]{2,1,0:T(8,128)(2,1)}), bf16[32,256,128]{2,1,0:T(8,128)(2,1)S(1)}, u32[]{:S(2)}, u32[]{:S(2)}) async-start(bf16[32,256,128]{2,1,0:T(8,128)(2,1)} %copy-done.1), calls=%async_computation.6 | async-start | bytes 4194304 | tf_op jit(solution)/shard_map/all_to_all | solution.py:207
  193.9 0.6 multiply_bitcast_fusion
  194.6 50.9 %all-to-all-done.6.arrived = bf16[32,256,128]{2,1,0:T(8,128)(2,1)S(1)} async-done(((bf16[32,256,128]{2,1,0:T(8,128)(2,1)}), bf16[32,256,128]{2,1,0:T(8,128)(2,1)S(1)}, u32[]{:S(2)}, u32[]{:S(2)}) %all-to-all-start.6) | async-done | bytes 2097184 | tf_op jit(solution)/shard_map/all_to_all | solution.py:207
  245.5 2.0 shard_map.107
  (6 shorter events, 0.1 us)
Async XLA Ops:
  20.3 0.9 copy-start.2
  22.2 1.3 copy-start
  23.5 4.8 %copy-start.6 = (s32[1,1,16,2]{2,3,1,0:T(2,128)S(1)}, s32[1,1,16,2]{2,3,1,0:T(2,128)}, u32[]{:S(2)}) copy-start(s32[1,1,16,2]{2,3,1,0:T(2,128)} %param.14) | copy-start | bytes 388
  23.5 51.2 %copy-start.5 = (s32[1,1,128]{2,1,0:T(1,128)S(1)}, s32[1,1,128]{2,1,0:T(1,128)}, u32[]{:S(2)}) copy-start(s32[1,1,128]{2,1,0:T(1,128)} %param.12) | copy-start | bytes 1540
  23.5 51.2 %all-to-all-start.1 = ((bf16[32,256,128]{2,1,0:T(8,128)(2,1)}), bf16[32,256,128]{2,1,0:T(8,128)(2,1)S(1)}, u32[]{:S(2)}, u32[]{:S(2)}) async-start(bf16[32,256,128]{2,1,0:T(8,128)(2,1)} %copy-done), calls=%async_computation.1 | async-start | bytes 4194304 | tf_op jit(solution)/shard_map/all_to_all | solution.py:169
  81.2 43.2 %copy-start.3 = (bf16[1,1,512,128]{3,2,1,0:T(8,128)(2,1)S(1)}, bf16[1,1,512,128]{3,2,1,0:T(8,128)(2,1)}, u32[]{:S(2)}) copy-start(bf16[1,1,512,128]{3,2,1,0:T(8,128)(2,1)} %param.9) | copy-start | bytes 393220
  81.3 43.2 %copy-start.4 = (bf16[128,128]{1,0:T(8,128)(2,1)S(1)}, bf16[128,128]{1,0:T(8,128)(2,1)}, u32[]{:S(2)}) copy-start(bf16[128,128]{1,0:T(8,128)(2,1)} %weight.1) | copy-start | bytes 98308
  176.6 13.3 %all-to-all-start.5 = ((f32[16,8,128]{2,1,0:T(8,128)}), f32[16,8,128]{2,1,0:T(8,128)S(1)}, u32[]{:S(2)}, u32[]{:S(2)}) async-start(f32[16,8,128]{2,1,0:T(8,128)} %broadcast_in_dim.5), calls=%async_computation.5 | async-start | bytes 131072 | tf_op jit(solution)/shard_map/all_to_all | solution.py:196
  188.5 1.3 copy-start.1
  189.9 55.6 %all-to-all-start.6 = ((bf16[32,256,128]{2,1,0:T(8,128)(2,1)}), bf16[32,256,128]{2,1,0:T(8,128)(2,1)S(1)}, u32[]{:S(2)}, u32[]{:S(2)}) async-start(bf16[32,256,128]{2,1,0:T(8,128)(2,1)} %copy-done.1), calls=%async_computation.6 | async-start | bytes 4194304 | tf_op jit(solution)/shard_map/all_to_all | solution.py:207

commit v2 on v1

v2 whole, which is shorter than its diff:
```python
import functools

import jax
import jax.numpy as jnp
from jax import lax
from jax.experimental import pallas as pl
from jax.experimental.pallas import tpu as pltpu
from jax.sharding import PartitionSpec as P

F32 = jnp.float32
BF16 = jnp.bfloat16
EXTRA = 16
GROUP = 8
BATCH = 2

VMEM = pl.BlockSpec(memory_space=pltpu.VMEM)
SMEM = pl.BlockSpec(memory_space=pltpu.SMEM)
HBM = pl.BlockSpec(memory_space=pltpu.HBM)


def call(kernel, out_shape, in_specs, scratch=(), flops=0, moved=0, out_spec=VMEM, grant=48):
    many = isinstance(out_shape, (tuple, list))
    return pl.pallas_call(
        kernel,
        out_shape=out_shape,
        in_specs=in_specs,
        out_specs=tuple(out_spec for _ in out_shape) if many else out_spec,
        scratch_shapes=list(scratch),
        cost_estimate=pl.CostEstimate(flops=flops, bytes_accessed=moved, transcendentals=0),
        compiler_params=pltpu.CompilerParams(vmem_limit_bytes=grant << 20),
    )


def pick_kernel(asked, feats, out, sems):
    n = out.shape[0]
    blk = out.shape[1] // 2

    def copy(r, k):
        start = pl.multiple_of(asked[r, k] * blk, blk)
        return pltpu.make_async_copy(
            feats.at[pl.ds(start, blk), :], out.at[r, pl.ds(k * blk, blk), :], sems.at[r, k]
        )

    for r in range(n):
        for k in range(2):
            copy(r, k).start()
    for r in range(n):
        for k in range(2):
            copy(r, k).wait()


def load_groups(live, source, values, sems):
    groups = live[0, 0] // GROUP

    def load(g):
        part = pl.ds(pl.multiple_of(g * GROUP, GROUP), GROUP)
        return pltpu.make_async_copy(source.at[part], values.at[part], sems.at[g])

    def start(g, carry):
        load(g).start()
        return carry

    lax.fori_loop(0, groups, start, 0)
    return groups, load


def forward_kernel(
    col_slots, slots, live, row_need, source, arrived, out, values, acc, sems
):
    n, _, width = out.shape
    blk = values.shape[1]
    groups, load = load_groups(live, source, values, sems)
    acc[...] = jnp.zeros_like(acc)

    def group(g, carry):
        load(g).wait()
        for first in range(0, GROUP, BATCH):
            terms = []
            for u in range(first, first + BATCH):
                b = g * GROUP + u
                slot = slots[0, b]
                col = slot % col_slots
                feats = arrived[col // 2, pl.ds(pl.multiple_of((col % 2) * blk, blk), blk), :]
                term = jnp.dot(values[b], feats, preferred_element_type=F32)
                terms.append((slot // col_slots, term))
            for row, term in terms:
                acc[row] += term
        return carry

    lax.fori_loop(0, groups, group, 0)
    sub = lax.broadcasted_iota(jnp.int32, (EXTRA, width), 0)
    for c in range(n):
        for k in range(2):
            out[c, k * blk : (k + 1) * blk, :] = acc[2 * c + k].astype(BF16)
        ids = jnp.where(sub < EXTRA // 2, row_need[c, 0], row_need[c, 1])
        out[c, 2 * blk :, :] = ids.astype(F32).astype(BF16)


def middle_kernel(arrived, weight, upstream, act, out, local_term, back):
    n, rows, width = arrived.shape
    blk = (rows - EXTRA) // 2
    per_dev = upstream.shape[0] // blk
    ids = []
    for c in range(n):
        tail = arrived[c, 2 * blk :, :].astype(F32)
        ids.append((tail[0:1, :], tail[EXTRA // 2 : EXTRA // 2 + 1, :]))
    w = weight[...]
    total = jnp.zeros((width, width), F32)
    for q in range(per_dev):
        acc = jnp.zeros((blk, width), F32)
        for c in range(n):
            for k in range(2):
                term = arrived[c, k * blk : (k + 1) * blk, :].astype(F32)
                acc = acc + jnp.where(ids[c][k] == float(q), term, 0.0)
        a = acc.astype(BF16)
        pre = jnp.dot(a, w, preferred_element_type=F32)
        sig = jax.nn.sigmoid(pre)
        act[q * blk : (q + 1) * blk, :] = (pre * sig).astype(BF16)
        up = upstream[q * blk : (q + 1) * blk, :].astype(F32)
        grad = (up * sig * (1.0 + pre * (1.0 - sig))).astype(BF16)
        total = total + lax.dot_general(a, grad, (((0,), (0,)), ((), ())), preferred_element_type=F32)
        back[q] = lax.dot_general(
            grad, w, (((1,), (1,)), ((), ())), preferred_element_type=F32
        ).astype(BF16)
    local_term[...] = total
    for c in range(n):
        for k in range(2):
            chosen = back[0]
            for q in range(1, per_dev):
                chosen = jnp.where(ids[c][k].astype(BF16) == float(q), back[q], chosen)
            out[c, k * blk : (k + 1) * blk, :] = chosen


def backward_kernel(
    col_slots, slots, live, source, arrived, out, values, acc, held, load_sems, sems
):
    blk = values.shape[1]
    groups, load = load_groups(live, source, values, load_sems)
    acc[...] = jnp.zeros_like(acc)

    def group(g, carry):
        load(g).wait()
        for first in range(0, GROUP, BATCH):
            terms = []
            for u in range(first, first + BATCH):
                b = g * GROUP + u
                slot = slots[0, b]
                row = slot // col_slots
                grads = arrived[row // 2, pl.ds(pl.multiple_of((row % 2) * blk, blk), blk), :]
                term = lax.dot_general(
                    values[b], grads, (((0,), (0,)), ((), ())), preferred_element_type=F32
                )
                terms.append((slot % col_slots, term))
            for col, term in terms:
                acc[col] += term
        return carry

    lax.fori_loop(0, groups, group, 0)
    n = out.shape[0]

    def copy(r):
        return pltpu.make_async_copy(held.at[r], out.at[r], sems.at[r])

    for r in range(n):
        for k in range(2):
            held[r, k * blk : (k + 1) * blk, :] = acc[2 * r + k].astype(BF16)
        if r:
            copy(r - 1).start()
    copy(n - 1).start()
    for r in range(n):
        copy(r).wait()


def final_kernel(asked, arrived, out, acc):
    n, rows, _ = arrived.shape
    blk = rows // 2
    acc[...] = jnp.zeros_like(acc)

    def step(r, carry):
        for k in range(2):
            term = arrived[r, k * blk : (k + 1) * blk, :].astype(F32)
            acc[asked[r, k]] += term
        return carry

    lax.fori_loop(0, n, step, 0, unroll=2)
    for q in range(acc.shape[0]):
        out[q * blk : (q + 1) * blk, :] = acc[q].astype(BF16)


def on_device(features, out_grad, weight, block_values, block_slot, live_count, row_need, col_need):
    n_rows = lax.axis_size("gr")
    n_cols = lax.axis_size("gc")
    values = block_values[0, 0]
    slot_total, blk, _ = values.shape
    local, width = features.shape[2:]
    cap = row_need.shape[3]
    per_dev = local // blk
    col_slots = n_rows * cap
    row_slots = n_cols * cap
    slots = block_slot[0]
    work = 2 * slot_total * blk * blk * width

    def swap(array, axis):
        return lax.all_to_all(array, axis, split_axis=0, concat_axis=0, tiled=True)

    def trade(array, axis, bit):
        pairs = [(i, i ^ bit) for i in range(lax.axis_size(axis))]
        return lax.ppermute(array, axis, pairs)

    def upper(axis, bit):
        return (lax.axis_index(axis) & bit) != 0

    need = jnp.pad(col_need[0, 0], ((0, 0), (0, 128 - cap))).reshape(n_rows, 1, 128)
    asked = swap(need, "gr").reshape(n_rows, 128)
    chosen = call(
        pick_kernel,
        jax.ShapeDtypeStruct((n_rows, cap * blk, width), BF16),
        [SMEM, VMEM],
        [pltpu.SemaphoreType.DMA((n_rows, cap))],
        moved=4 << 20,
        out_spec=HBM,
        grant=60,
    )(asked, features[0, 0])
    arrived = swap(chosen, "gr")
    partial = call(
        functools.partial(forward_kernel, col_slots),
        jax.ShapeDtypeStruct((n_cols, cap * blk + EXTRA, width), BF16),
        [SMEM, SMEM, SMEM, HBM, VMEM],
        [
            pltpu.VMEM(values.shape, BF16),
            pltpu.VMEM((row_slots, blk, width), F32),
            pltpu.SemaphoreType.DMA((slot_total // GROUP,)),
        ],
        flops=work,
        moved=8 << 20,
    )(slots, live_count, row_need[0, 0], values, arrived)
    partial = swap(partial, "gc")
    activated, back, term = call(
        middle_kernel,
        (
            jax.ShapeDtypeStruct((local, width), BF16),
            jax.ShapeDtypeStruct((n_cols, cap * blk, width), BF16),
            jax.ShapeDtypeStruct((width, width), F32),
        ),
        [VMEM, VMEM, VMEM],
        [pltpu.VMEM((per_dev, blk, width), BF16)],
        flops=work // 8,
        moved=4 << 20,
    )(partial, weight, out_grad[0, 0])
    back = swap(back, "gc")

    halved = []
    bit = 1
    while bit < n_rows:
        if len(halved) < 2:
            low, high = jnp.split(term, 2, axis=0)
            top = upper("gr", bit)
            term = jnp.where(top, high, low) + trade(jnp.where(top, low, high), "gr", bit)
            halved.append(bit)
        else:
            other = trade(term, "gr", bit)
            term = term + other
        bit *= 2
    bit = 1
    while bit < n_cols:
        term = term + trade(term, "gc", bit)
        bit *= 2
    for bit in reversed(halved):
        other = trade(term, "gr", bit)
        top = upper("gr", bit)
        term = jnp.concatenate([jnp.where(top, other, term), jnp.where(top, term, other)], axis=0)
    node_total = local * n_rows * n_cols
    weight_grad = term * float(node_total) ** (-0.5)

    returned = call(
        functools.partial(backward_kernel, col_slots),
        jax.ShapeDtypeStruct((n_rows, cap * blk, width), BF16),
        [SMEM, SMEM, HBM, VMEM],
        [
            pltpu.VMEM(values.shape, BF16),
            pltpu.VMEM((col_slots, blk, width), F32),
            pltpu.VMEM((n_rows, cap * blk, width), BF16),
            pltpu.SemaphoreType.DMA((slot_total // GROUP,)),
            pltpu.SemaphoreType.DMA((n_rows,)),
        ],
        flops=work,
        moved=8 << 20,
        out_spec=HBM,
        grant=59,
    )(slots, live_count, values, back)
    returned = swap(returned, "gr")
    input_grad = call(
        final_kernel,
        jax.ShapeDtypeStruct((local, width), BF16),
        [SMEM, VMEM],
        [pltpu.VMEM((per_dev, blk, width), F32)],
        moved=4 << 20,
    )(asked, returned)
    return (
        activated.reshape(1, 1, local, width),
        weight_grad,
        input_grad.reshape(1, 1, local, width),
    )


def solution(mesh):
    placed = (
        P("gc", "gr", None, None),
        P("gr", "gc", None, None),
        P(),
        P("gr", "gc", None, None, None),
        P("gr", "gc", None),
        P("gr", "gc"),
        P("gr", "gc", None, None),
        P("gr", "gc", None, None),
    )

    return jax.shard_map(
        on_device,
        mesh=mesh,
        in_specs=placed,
        out_specs=(P("gr", "gc", None, None), P(), P("gc", "gr", None, None)),
        check_vma=False,
    )
```

time: 247 us -> 276 us (1.12); the launches traced: 247 us -> 270 us
  starting transfers between devices: 13 us -> 49.2 us
  blocking collectives: 111 us -> 96.1 us
  local copies, waits for them, and re-layouts: 5.07 us -> 0.85 us
  waiting for transfers between devices: 97.2 us -> 101 us
    ppermute x0 -> x11, waiting for transfers between devices: none -> 54.7 us  [trade(): return lax.ppermute(array, axis, pairs)]
    all_to_all x3 -> x2, waiting for transfers between devices: 97.2 us -> 46 us  [swap(): return lax.all_to_all(array, axis, split_axis=0, concat_axis=0, tiled=True)]
    ppermute x0 -> x11, starting transfers between devices: none -> 40.2 us  [trade(): return lax.ppermute(array, axis, pairs)]
    all_to_all x4 -> x3, blocking collectives: 111 us -> 96.1 us  [swap(): return lax.all_to_all(array, axis, split_axis=0, concat_axis=0, tiled=True)]
    all_to_all x3 -> x2, starting transfers between devices: 13 us -> 9 us  [swap(): return lax.all_to_all(array, axis, split_axis=0, concat_axis=0, tiled=True)]
    unnamed x14 -> x10, local copies, waits for them, and re-layouts: 3.6 us -> 0.03 us
  transfers between devices with their start and end apart: 3 -> 13, of which waited for: 2 -> 12; matrix products, arithmetic and copies ran while one was open for 0% -> 0% of each run, Pallas kernels for 3% -> 0%
where the time goes in v2:
time: 276 us; the launch traced here: 270 us
  waiting for transfers between devices  101 us (37%)
  blocking collectives  96.1 us (35%)
  starting transfers between devices  49.2 us (18%)
  Pallas kernels  21.1 us (8%)
    all_to_all x3, blocking collectives, swap(): return lax.all_to_all(array, axis, split_axis=0, concat_axis=0, tiled=True)  96.1 us
    ppermute x11, waiting for transfers between devices, trade(): return lax.ppermute(array, axis, pairs)  54.7 us
    all_to_all x2, waiting for transfers between devices, swap(): return lax.all_to_all(array, axis, split_axis=0, concat_axis=0, tiled=True)  46 us
    ppermute x11, starting transfers between devices, trade(): return lax.ppermute(array, axis, pairs)  40.2 us
    all_to_all x2, starting transfers between devices, swap(): return lax.all_to_all(array, axis, split_axis=0, concat_axis=0, tiled=True)  9 us
    pallas_call x1, Pallas kernels, on_device(): call(functools.partial(backward_kernel, col_slots), jax.ShapeDtypeStruct(...  8.28 us
    pallas_call x1, Pallas kernels, on_device(): call(functools.partial(forward_kernel, col_slots), jax.ShapeDtypeStruct((...  5.92 us
  transfers between devices with their start and end apart: 13, of which 12 were waited for; matrix products, arithmetic and copies ran while one was open for 0% of the time, Pallas kernels for 0%

profile of v2, /device:TPU:1, one launch (start us, length us, event | category | flops | bytes accessed | tf_op | source)
XLA Modules:
  0.0 270.1 jit_solution(6375335602352616208)
XLA Ops:
  1.4 18.9 %all_to_all.25 = s32[32,1,128]{2,1,0:T(1,128)} all-to-all(s32[32,1,128]{2,1,0:T(1,128)S(1)} %copy.13), channel_id=1, replica_groups=mesh['gr'=32,'gc'=16] {'gr'}, dimensions={0} | all-to-all | bytes 32768 | tf_op jit(solution)/shard_map/all_to_all | solution.py:204
  20.2 2.8 %shard_map.103 = bf16[32,256,128]{2,1,0:T(8,128)(2,1)} custom-call(s32[32,128]{1,0:T(8,128)} %bitcast.11, bf16[512,128]{1,0:T(8,128)(2,1)} %bitcast.18), custom_call_target="tpu_custom_call" | custom-call | bytes 4194304 | tf_op jit(solution)/shard_map/pallas_call | solution.py:215
  23.1 4.0 %all-to-all-start.1 = ((bf16[32,256,128]{2,1,0:T(8,128)(2,1)}), bf16[32,256,128]{2,1,0:T(8,128)(2,1)S(1)}, u32[]{:S(2)}, u32[]{:S(2)}) async-start(bf16[32,256,128]{2,1,0:T(8,128)(2,1)} %shard_map.103), calls=%async_computation.1 | async-start | bytes 4194304 | tf_op jit(solution)/shard_map/all_to_all | solution.py:204
  27.9 46.0 %all-to-all-done.1.arrived = bf16[32,256,128]{2,1,0:T(8,128)(2,1)S(1)} async-done(((bf16[32,256,128]{2,1,0:T(8,128)(2,1)}), bf16[32,256,128]{2,1,0:T(8,128)(2,1)S(1)}, u32[]{:S(2)}, u32[]{:S(2)}) %all-to-all-start.1) | async-done | bytes 2097184 | tf_op jit(solution)/shard_map/all_to_all | solution.py:204
  73.9 5.9 %shard_map.104 = bf16[16,272,128]{2,1,0:T(8,128)(2,1)S(1)} custom-call(s32[1,128]{1,0:T(1,128)S(1)} %bitcast.15, s32[1,1]{1,0:T(1,128)S(6)} %copy.15.live, s32[16,2]{1,0:T(8,128)S(1)} %copy.14.row_need, bf16[128,128,128]{2,1,0:T(8,128)(2,1)} %bitcast.16, bf16[32,256,128]{2,1,0:T(8,128)(2,1)S(1)} %all-to-all-done.1.arrived), custom_call_target="tpu_custom_call" | custom-call | flops 536870912 | bytes 8388608 | tf_op jit(solution)/shard_map/pallas_call | solution.py:225
  79.8 45.4 %all_to_all.26.arrived = bf16[16,272,128]{2,1,0:T(8,128)(2,1)S(1)} all-to-all(bf16[16,272,128]{2,1,0:T(8,128)(2,1)S(1)} %shard_map.104), channel_id=1, replica_groups=mesh['gr'=32,'gc'=16] {'gc'}, dimensions={0} | all-to-all | bytes 2228224 | tf_op jit(solution)/shard_map/all_to_all | solution.py:204
  125.3 2.0 shard_map.105
  127.3 31.8 %all_to_all.27.arrived = bf16[16,256,128]{2,1,0:T(8,128)(2,1)} all-to-all(bf16[16,256,128]{2,1,0:T(8,128)(2,1)S(1)} %get-tuple-element.8), channel_id=1, replica_groups=mesh['gr'=32,'gc'=16] {'gc'}, dimensions={0} | all-to-all | bytes 2097152 | tf_op jit(solution)/shard_map/all_to_all | solution.py:204
  159.1 8.3 %shard_map.106 = bf16[32,256,128]{2,1,0:T(8,128)(2,1)} custom-call(s32[1,128]{1,0:T(1,128)} %bitcast.14, s32[1,1]{1,0:T(1,128)S(6)} %copy.15.live, bf16[128,128,128]{2,1,0:T(8,128)(2,1)} %bitcast.17, bf16[16,256,128]{2,1,0:T(8,128)(2,1)} %all_to_all.27.arrived), custom_call_target="tpu_custom_call" | custom-call | flops 536870912 | bytes 8388608 | tf_op jit(solution)/shard_map/pallas_call | solution.py:275
  167.4 5.0 %all-to-all-start.4 = ((bf16[32,256,128]{2,1,0:T(8,128)(2,1)}), bf16[32,256,128]{2,1,0:T(8,128)(2,1)S(1)}, u32[]{:S(2)}, u32[]{:S(2)}) async-start(bf16[32,256,128]{2,1,0:T(8,128)(2,1)} %shard_map.106), calls=%async_computation.4 | async-start | bytes 4194304 | tf_op jit(solution)/shard_map/all_to_all | solution.py:204
  172.4 3.1 %collective-permute-start = (f32[64,128]{1,0:T(8,128)S(1)}, f32[64,128]{1,0:T(8,128)S(1)}, u32[]{:S(2)}, u32[]{:S(2)}) collective-permute-start(f32[64,128]{1,0:T(8,128)S(1)} %slice_select_fusion), channel_id=1, source_target_pairs={{0,16},{16,0},{32,48},{48,32},{64,80},{80,64},{96,112},{112,96},{1... | collective-permute-start | bytes 98312 | tf_op jit(solution)/shard_map/ppermute | solution.py:208
  175.6 2.5 collective-permute-done
  178.1 4.3 %collective-permute-start.1 = (f32[32,128]{1,0:T(8,128)S(1)}, f32[32,128]{1,0:T(8,128)S(1)}, u32[]{:S(2)}, u32[]{:S(2)}) collective-permute-start(f32[32,128]{1,0:T(8,128)S(1)} %slice_select_fusion.1), channel_id=1, source_target_pairs={{0,32},{16,48},{32,0},{48,16},{64,96},{80,112},{96,64},{112,80},{1... | collective-permute-start | bytes 49160 | tf_op jit(solution)/shard_map/ppermute | solution.py:208
  182.3 2.0 collective-permute-done.1
  184.3 5.9 %collective-permute-start.2 = (f32[32,128]{1,0:T(8,128)S(1)}, f32[32,128]{1,0:T(8,128)S(1)}, u32[]{:S(2)}, u32[]{:S(2)}) collective-permute-start(f32[32,128]{1,0:T(8,128)S(1)} %select_add_fusion.1), channel_id=1, source_target_pairs={{0,64},{16,80},{32,96},{48,112},{64,0},{80,16},{96,32},{112,48},{1... | collective-permute-start | bytes 49160 | tf_op jit(solution)/shard_map/ppermute | solution.py:208
  190.3 29.5 %collective-permute-done.2 = f32[32,128]{1,0:T(8,128)S(1)} collective-permute-done((f32[32,128]{1,0:T(8,128)S(1)}, f32[32,128]{1,0:T(8,128)S(1)}, u32[]{:S(2)}, u32[]{:S(2)}) %collective-permute-start.2) | collective-permute-done | bytes 16416 | tf_op jit(solution)/shard_map/ppermute | solution.py:208
  219.8 2.6 collective-permute-start.3
  222.4 2.9 %collective-permute-done.3 = f32[32,128]{1,0:T(8,128)S(1)} collective-permute-done((f32[32,128]{1,0:T(8,128)S(1)}, f32[32,128]{1,0:T(8,128)S(1)}, u32[]{:S(2)}, u32[]{:S(2)}) %collective-permute-start.3) | collective-permute-done | bytes 16416 | tf_op jit(solution)/shard_map/ppermute | solution.py:208
  225.3 5.7 %collective-permute-start.4 = (f32[32,128]{1,0:T(8,128)S(1)}, f32[32,128]{1,0:T(8,128)S(1)}, u32[]{:S(2)}, u32[]{:S(2)}) collective-permute-start(f32[32,128]{1,0:T(8,128)S(1)} %add.32), channel_id=1, source_target_pairs={{0,256},{16,272},{32,288},{48,304},{64,320},{80,336},{96,352},{112... | collective-permute-start | bytes 49160 | tf_op jit(solution)/shard_map/ppermute | solution.py:208
  231.0 2.7 collective-permute-done.4
  233.7 4.0 %collective-permute-start.5 = (f32[32,128]{1,0:T(8,128)S(1)}, f32[32,128]{1,0:T(8,128)S(1)}, u32[]{:S(2)}, u32[]{:S(2)}) collective-permute-start(f32[32,128]{1,0:T(8,128)S(1)} %add.33), channel_id=1, source_target_pairs={{0,1},{1,0},{2,3},{3,2},{4,5},{5,4},{6,7},{7,6},{8,9},{9,8},{10,11... | collective-permute-start | bytes 49160 | tf_op jit(solution)/shard_map/ppermute | solution.py:208
  238.5 1.9 collective-permute-start.6
  240.4 2.6 collective-permute-done.6
  243.0 2.5 collective-permute-start.7
  245.5 2.9 %collective-permute-done.7 = f32[32,128]{1,0:T(8,128)S(1)} collective-permute-done((f32[32,128]{1,0:T(8,128)S(1)}, f32[32,128]{1,0:T(8,128)S(1)}, u32[]{:S(2)}, u32[]{:S(2)}) %collective-permute-start.7) | collective-permute-done | bytes 16416 | tf_op jit(solution)/shard_map/ppermute | solution.py:208
  248.3 3.2 %collective-permute-start.8 = (f32[32,128]{1,0:T(8,128)S(1)}, f32[32,128]{1,0:T(8,128)S(1)}, u32[]{:S(2)}, u32[]{:S(2)}) collective-permute-start(f32[32,128]{1,0:T(8,128)S(1)} %add.36), channel_id=1, source_target_pairs={{0,8},{1,9},{2,10},{3,11},{4,12},{5,13},{6,14},{7,15},{8,0},{9,1},... | collective-permute-start | bytes 49160 | tf_op jit(solution)/shard_map/ppermute | solution.py:208
  251.5 5.2 %collective-permute-done.8 = f32[32,128]{1,0:T(8,128)S(1)} collective-permute-done((f32[32,128]{1,0:T(8,128)S(1)}, f32[32,128]{1,0:T(8,128)S(1)}, u32[]{:S(2)}, u32[]{:S(2)}) %collective-permute-start.8) | collective-permute-done | bytes 16416 | tf_op jit(solution)/shard_map/ppermute | solution.py:208
  256.7 4.2 %collective-permute-start.9 = (f32[32,128]{1,0:T(8,128)S(1)}, f32[32,128]{1,0:T(8,128)S(1)}, u32[]{:S(2)}, u32[]{:S(2)}) collective-permute-start(f32[32,128]{1,0:T(8,128)S(1)} %add.37), channel_id=1, source_target_pairs={{0,32},{16,48},{32,0},{48,16},{64,96},{80,112},{96,64},{112,80},{1... | collective-permute-start | bytes 49160 | tf_op jit(solution)/shard_map/ppermute | solution.py:208
  261.0 1.7 collective-permute-done.9
  262.7 2.8 %collective-permute-start.10 = (f32[64,128]{1,0:T(8,128)S(1)}, f32[64,128]{1,0:T(8,128)S(1)}, u32[]{:S(2)}, u32[]{:S(2)}) collective-permute-start(f32[64,128]{1,0:T(8,128)S(1)} %pad_maximum_fusion), channel_id=1, source_target_pairs={{0,16},{16,0},{32,48},{48,32},{64,80},{80,64},{96,112},{112,96},{1... | collective-permute-start | bytes 98312 | tf_op jit(solution)/shard_map/ppermute | solution.py:208
  265.5 2.0 collective-permute-done.10
  268.1 2.0 shard_map.107
  (30 shorter events, 2.4 us)
Async XLA Ops:
  23.1 4.7 %copy-start.4 = (s32[1,1,16,2]{2,3,1,0:T(2,128)S(1)}, s32[1,1,16,2]{2,3,1,0:T(2,128)}, u32[]{:S(2)}) copy-start(s32[1,1,16,2]{2,3,1,0:T(2,128)} %param.14) | copy-start | bytes 388
  23.1 50.8 %copy-start.3 = (s32[1,1,128]{2,1,0:T(1,128)S(1)}, s32[1,1,128]{2,1,0:T(1,128)}, u32[]{:S(2)}) copy-start(s32[1,1,128]{2,1,0:T(1,128)} %param.12) | copy-start | bytes 1540
  23.1 50.8 %all-to-all-start.1 = ((bf16[32,256,128]{2,1,0:T(8,128)(2,1)}), bf16[32,256,128]{2,1,0:T(8,128)(2,1)S(1)}, u32[]{:S(2)}, u32[]{:S(2)}) async-start(bf16[32,256,128]{2,1,0:T(8,128)(2,1)} %shard_map.103), calls=%async_computation.1 | async-start | bytes 4194304 | tf_op jit(solution)/shard_map/all_to_all | solution.py:204
  79.8 45.5 %copy-start.1 = (bf16[1,1,512,128]{3,2,1,0:T(8,128)(2,1)S(1)}, bf16[1,1,512,128]{3,2,1,0:T(8,128)(2,1)}, u32[]{:S(2)}) copy-start(bf16[1,1,512,128]{3,2,1,0:T(8,128)(2,1)} %param.9) | copy-start | bytes 393220
  79.8 45.5 %copy-start.2 = (bf16[128,128]{1,0:T(8,128)(2,1)S(1)}, bf16[128,128]{1,0:T(8,128)(2,1)}, u32[]{:S(2)}) copy-start(bf16[128,128]{1,0:T(8,128)(2,1)} %weight.1) | copy-start | bytes 98308
  167.4 100.7 %copy-start = (s32[32,1,128]{2,1,0:T(1,128)S(1)}, s32[32,1,128]{2,1,0:T(1,128)}, u32[]{:S(2)}) copy-start(s32[32,1,128]{2,1,0:T(1,128)} %all_to_all.25) | copy-start | bytes 49156
  167.4 100.7 %all-to-all-start.4 = ((bf16[32,256,128]{2,1,0:T(8,128)(2,1)}), bf16[32,256,128]{2,1,0:T(8,128)(2,1)S(1)}, u32[]{:S(2)}, u32[]{:S(2)}) async-start(bf16[32,256,128]{2,1,0:T(8,128)(2,1)} %shard_map.106), calls=%async_computation.4 | async-start | bytes 4194304 | tf_op jit(solution)/shard_map/all_to_all | solution.py:204
  172.4 5.6 %collective-permute-start = (f32[64,128]{1,0:T(8,128)S(1)}, f32[64,128]{1,0:T(8,128)S(1)}, u32[]{:S(2)}, u32[]{:S(2)}) collective-permute-start(f32[64,128]{1,0:T(8,128)S(1)} %slice_select_fusion), channel_id=1, source_target_pairs={{0,16},{16,0},{32,48},{48,32},{64,80},{80,64},{96,112},{112,96},{1... | collective-permute-start | bytes 98312 | tf_op jit(solution)/shard_map/ppermute | solution.py:208
  178.1 6.3 %collective-permute-start.1 = (f32[32,128]{1,0:T(8,128)S(1)}, f32[32,128]{1,0:T(8,128)S(1)}, u32[]{:S(2)}, u32[]{:S(2)}) collective-permute-start(f32[32,128]{1,0:T(8,128)S(1)} %slice_select_fusion.1), channel_id=1, source_target_pairs={{0,32},{16,48},{32,0},{48,16},{64,96},{80,112},{96,64},{112,80},{1... | collective-permute-start | bytes 49160 | tf_op jit(solution)/shard_map/ppermute | solution.py:208
  184.3 35.4 %collective-permute-start.2 = (f32[32,128]{1,0:T(8,128)S(1)}, f32[32,128]{1,0:T(8,128)S(1)}, u32[]{:S(2)}, u32[]{:S(2)}) collective-permute-start(f32[32,128]{1,0:T(8,128)S(1)} %select_add_fusion.1), channel_id=1, source_target_pairs={{0,64},{16,80},{32,96},{48,112},{64,0},{80,16},{96,32},{112,48},{1... | collective-permute-start | bytes 49160 | tf_op jit(solution)/shard_map/ppermute | solution.py:208
  219.8 5.5 %collective-permute-start.3 = (f32[32,128]{1,0:T(8,128)S(1)}, f32[32,128]{1,0:T(8,128)S(1)}, u32[]{:S(2)}, u32[]{:S(2)}) collective-permute-start(f32[32,128]{1,0:T(8,128)S(1)} %add.31), channel_id=1, source_target_pairs={{0,128},{16,144},{32,160},{48,176},{64,192},{80,208},{96,224},{112... | collective-permute-start | bytes 49160 | tf_op jit(solution)/shard_map/ppermute | solution.py:208
  225.3 8.4 %collective-permute-start.4 = (f32[32,128]{1,0:T(8,128)S(1)}, f32[32,128]{1,0:T(8,128)S(1)}, u32[]{:S(2)}, u32[]{:S(2)}) collective-permute-start(f32[32,128]{1,0:T(8,128)S(1)} %add.32), channel_id=1, source_target_pairs={{0,256},{16,272},{32,288},{48,304},{64,320},{80,336},{96,352},{112... | collective-permute-start | bytes 49160 | tf_op jit(solution)/shard_map/ppermute | solution.py:208
  233.7 4.8 %collective-permute-start.5 = (f32[32,128]{1,0:T(8,128)S(1)}, f32[32,128]{1,0:T(8,128)S(1)}, u32[]{:S(2)}, u32[]{:S(2)}) collective-permute-start(f32[32,128]{1,0:T(8,128)S(1)} %add.33), channel_id=1, source_target_pairs={{0,1},{1,0},{2,3},{3,2},{4,5},{5,4},{6,7},{7,6},{8,9},{9,8},{10,11... | collective-permute-start | bytes 49160 | tf_op jit(solution)/shard_map/ppermute | solution.py:208
  238.5 4.5 %collective-permute-start.6 = (f32[32,128]{1,0:T(8,128)S(1)}, f32[32,128]{1,0:T(8,128)S(1)}, u32[]{:S(2)}, u32[]{:S(2)}) collective-permute-start(f32[32,128]{1,0:T(8,128)S(1)} %add.34), channel_id=1, source_target_pairs={{0,2},{1,3},{2,0},{3,1},{4,6},{5,7},{6,4},{7,5},{8,10},{9,11},{10,... | collective-permute-start | bytes 49160 | tf_op jit(solution)/shard_map/ppermute | solution.py:208
  243.0 5.4 %collective-permute-start.7 = (f32[32,128]{1,0:T(8,128)S(1)}, f32[32,128]{1,0:T(8,128)S(1)}, u32[]{:S(2)}, u32[]{:S(2)}) collective-permute-start(f32[32,128]{1,0:T(8,128)S(1)} %add.35), channel_id=1, source_target_pairs={{0,4},{1,5},{2,6},{3,7},{4,0},{5,1},{6,2},{7,3},{8,12},{9,13},{10,... | collective-permute-start | bytes 49160 | tf_op jit(solution)/shard_map/ppermute | solution.py:208
  248.3 8.4 %collective-permute-start.8 = (f32[32,128]{1,0:T(8,128)S(1)}, f32[32,128]{1,0:T(8,128)S(1)}, u32[]{:S(2)}, u32[]{:S(2)}) collective-permute-start(f32[32,128]{1,0:T(8,128)S(1)} %add.36), channel_id=1, source_target_pairs={{0,8},{1,9},{2,10},{3,11},{4,12},{5,13},{6,14},{7,15},{8,0},{9,1},... | collective-permute-start | bytes 49160 | tf_op jit(solution)/shard_map/ppermute | solution.py:208
  256.7 6.0 %collective-permute-start.9 = (f32[32,128]{1,0:T(8,128)S(1)}, f32[32,128]{1,0:T(8,128)S(1)}, u32[]{:S(2)}, u32[]{:S(2)}) collective-permute-start(f32[32,128]{1,0:T(8,128)S(1)} %add.37), channel_id=1, source_target_pairs={{0,32},{16,48},{32,0},{48,16},{64,96},{80,112},{96,64},{112,80},{1... | collective-permute-start | bytes 49160 | tf_op jit(solution)/shard_map/ppermute | solution.py:208
  262.7 4.8 %collective-permute-start.10 = (f32[64,128]{1,0:T(8,128)S(1)}, f32[64,128]{1,0:T(8,128)S(1)}, u32[]{:S(2)}, u32[]{:S(2)}) collective-permute-start(f32[64,128]{1,0:T(8,128)S(1)} %pad_maximum_fusion), channel_id=1, source_target_pairs={{0,16},{16,0},{32,48},{48,32},{64,80},{80,64},{96,112},{112,96},{1... | collective-permute-start | bytes 98312 | tf_op jit(solution)/shard_map/ppermute | solution.py:208

commit v3 on v2

--- a/solution.py
+++ b/solution.py
@@ -10,9 +10,14 @@
 F32 = jnp.float32
 BF16 = jnp.bfloat16
 EXTRA = 16
+NX = 4
 GROUP = 8
 BATCH = 2
-
+PICK_GRANT = 40
+BACKWARD_GRANT = 58
+FORWARD_GRANT = 40
+
+ANY = pl.BlockSpec(memory_space=pl.ANY)
 VMEM = pl.BlockSpec(memory_space=pltpu.VMEM)
 SMEM = pl.BlockSpec(memory_space=pltpu.SMEM)
 HBM = pl.BlockSpec(memory_space=pltpu.HBM)
@@ -31,22 +36,26 @@
     )
 
 
-def pick_kernel(asked, feats, out, sems):
-    n = out.shape[0]
-    blk = out.shape[1] // 2
-
-    def copy(r, k):
-        start = pl.multiple_of(asked[r, k] * blk, blk)
+def pick_kernel(me, *refs):
+    peers = NX - 1
+    tables, column, outs, sems = refs[:peers], refs[peers], refs[peers + 1 : -1], refs[-1]
+    n = column.shape[0]
+    blk = outs[0].shape[1] // 2
+    mine = me[0, 0] % NX
+
+    def copy(d, y, k):
+        start = pl.multiple_of(tables[d][0, 2 * (NX * y + mine) + k] * blk, blk)
         return pltpu.make_async_copy(
-            feats.at[pl.ds(start, blk), :], out.at[r, pl.ds(k * blk, blk), :], sems.at[r, k]
+            column.at[y, pl.ds(start, blk), :],
+            outs[d].at[y, pl.ds(k * blk, blk), :],
+            sems.at[d, y, k],
         )
 
-    for r in range(n):
-        for k in range(2):
-            copy(r, k).start()
-    for r in range(n):
-        for k in range(2):
-            copy(r, k).wait()
+    every = [(d, y, k) for d in range(peers) for y in range(n) for k in range(2)]
+    for place in every:
+        copy(*place).start()
+    for place in every:
+        copy(*place).wait()
 
 
 def load_groups(live, source, values, sems):
@@ -64,13 +73,33 @@
     return groups, load
 
 
-def forward_kernel(
-    col_slots, slots, live, row_need, source, arrived, out, values, acc, sems
-):
+def forward_kernel(col_slots, me, slots, live, row_need, need, source, column, *refs):
+    peers, (out, values, arrived, acc, sems, own_sems, peer_sems) = refs[: NX - 1], refs[NX - 1 :]
     n, _, width = out.shape
     blk = values.shape[1]
+    rows = column.shape[0]
+    mine = me[0, 0] % NX
+
+    def own(y, k):
+        start = pl.multiple_of(need[0, 2 * (NX * y + mine) + k] * blk, blk)
+        return pltpu.make_async_copy(
+            column.at[y, pl.ds(start, blk), :], arrived.at[0, 2 * y + k], own_sems.at[y, k]
+        )
+
+    def received(d):
+        return pltpu.make_async_copy(peers[d], arrived.at[d + 1], peer_sems.at[d])
+
+    every = [(y, k) for y in range(rows) for k in range(2)]
+    for d in range(NX - 1):
+        received(d).start()
+    for place in every:
+        own(*place).start()
     groups, load = load_groups(live, source, values, sems)
     acc[...] = jnp.zeros_like(acc)
+    for d in range(NX - 1):
+        received(d).wait()
+    for place in every:
+        own(*place).wait()
 
     def group(g, carry):
         load(g).wait()
@@ -80,7 +109,9 @@
                 b = g * GROUP + u
                 slot = slots[0, b]
                 col = slot % col_slots
-                feats = arrived[col // 2, pl.ds(pl.multiple_of((col % 2) * blk, blk), blk), :]
+                owner = col // 2
+                piece = (mine + NX - owner % NX) % NX
+                feats = arrived[piece, 2 * (owner // NX) + col % 2]
                 term = jnp.dot(values[b], feats, preferred_element_type=F32)
                 terms.append((slot // col_slots, term))
             for row, term in terms:
@@ -171,15 +202,18 @@
         copy(r).wait()
 
 
-def final_kernel(asked, arrived, out, acc):
+def final_kernel(me, asked, arrived, out, acc):
     n, rows, _ = arrived.shape
     blk = rows // 2
+    mine = me[0, 0]
     acc[...] = jnp.zeros_like(acc)
 
     def step(r, carry):
+        ring = (r % NX + NX - mine % NX) % NX
+        place = ((r // NX) ^ (mine // NX)) * NX + ring
         for k in range(2):
             term = arrived[r, k * blk : (k + 1) * blk, :].astype(F32)
-            acc[asked[r, k]] += term
+            acc[asked[place, 2 * mine + k]] += term
         return carry
 
     lax.fori_loop(0, n, step, 0, unroll=2)
@@ -210,30 +244,56 @@
     def upper(axis, bit):
         return (lax.axis_index(axis) & bit) != 0
 
-    need = jnp.pad(col_need[0, 0], ((0, 0), (0, 128 - cap))).reshape(n_rows, 1, 128)
-    asked = swap(need, "gr").reshape(n_rows, 128)
+    n_y = n_rows // NX
+    me = lax.axis_index("gr").astype(jnp.int32).reshape(1, 1)
+
+    def along_x(array, shift):
+        pairs = [(i, i - i % NX + (i + shift) % NX) for i in range(n_rows)]
+        return lax.ppermute(array, "gr", pairs)
+
+    column = lax.all_to_all(
+        jnp.broadcast_to(features[0, 0][None], (n_y, local, width)),
+        "gr",
+        split_axis=0,
+        concat_axis=0,
+        tiled=True,
+        axis_index_groups=[[NX * y + x for y in range(n_y)] for x in range(NX)],
+    )
+    need = jnp.pad(col_need[0, 0].reshape(1, -1), ((0, 0), (0, 128 - col_slots)))
+    tables = [along_x(need, -d) for d in range(1, NX)]
     chosen = call(
         pick_kernel,
-        jax.ShapeDtypeStruct((n_rows, cap * blk, width), BF16),
-        [SMEM, VMEM],
-        [pltpu.SemaphoreType.DMA((n_rows, cap))],
+        [jax.ShapeDtypeStruct((n_y, cap * blk, width), BF16) for _ in tables],
+        [SMEM, *[SMEM for _ in tables], VMEM],
+        [pltpu.SemaphoreType.DMA((NX - 1, n_y, cap))],
         moved=4 << 20,
-        out_spec=HBM,
-        grant=60,
-    )(asked, features[0, 0])
-    arrived = swap(chosen, "gr")
+        out_spec=ANY,
+        grant=PICK_GRANT,
+    )(me, *tables, column)
+    pieces = [along_x(chosen[d], d + 1) for d in range(NX - 1)]
+    pieces = [p.reshape(cap * n_y, blk, width) for p in pieces]
     partial = call(
         functools.partial(forward_kernel, col_slots),
         jax.ShapeDtypeStruct((n_cols, cap * blk + EXTRA, width), BF16),
-        [SMEM, SMEM, SMEM, HBM, VMEM],
+        [SMEM, SMEM, SMEM, SMEM, SMEM, HBM, ANY, *[ANY for _ in pieces]],
         [
             pltpu.VMEM(values.shape, BF16),
+            pltpu.VMEM((NX, cap * n_y, blk, width), BF16),
             pltpu.VMEM((row_slots, blk, width), F32),
             pltpu.SemaphoreType.DMA((slot_total // GROUP,)),
+            pltpu.SemaphoreType.DMA((n_y, cap)),
+            pltpu.SemaphoreType.DMA((NX - 1,)),
         ],
         flops=work,
         moved=8 << 20,
-    )(slots, live_count, row_need[0, 0], values, arrived)
+        grant=FORWARD_GRANT,
+    )(me, slots, live_count, row_need[0, 0], need, values, column, *pieces)
+    asked = jnp.concatenate([need, *tables], axis=0)
+    bit = 1
+    while bit < n_y:
+        other = trade(asked, "gr", bit * NX)
+        asked = jnp.concatenate([asked, other], axis=0)
+        bit *= 2
     partial = swap(partial, "gc")
     activated, back, term = call(
         middle_kernel,
@@ -286,16 +346,16 @@
         flops=work,
         moved=8 << 20,
         out_spec=HBM,
-        grant=59,
+        grant=BACKWARD_GRANT,
     )(slots, live_count, values, back)
     returned = swap(returned, "gr")
     input_grad = call(
         final_kernel,
         jax.ShapeDtypeStruct((local, width), BF16),
-        [SMEM, VMEM],
+        [SMEM, SMEM, VMEM],
         [pltpu.VMEM((per_dev, blk, width), F32)],
         moved=4 << 20,
-    )(asked, returned)
+    )(me, asked, returned)
     return (
         activated.reshape(1, 1, local, width),
         weight_grad,

time: 276 us -> 294 us (1.065)
  the two profiles are of different devices: /device:TPU:1 before, /device:TPU:4 now
where the time goes in v3:
time: 294 us; the launch traced here: 293 us
  waiting for transfers between devices  117 us (40%)
  starting transfers between devices  76 us (26%)
  blocking collectives  70.9 us (24%)
  Pallas kernels  22.5 us (8%)
  local copies, waits for them, and re-layouts  4.59 us (2%)
    ppermute x14, waiting for transfers between devices, trade(): return lax.ppermute(array, axis, pairs)  77.7 us
    all_to_all x2, blocking collectives, swap(): return lax.all_to_all(array, axis, split_axis=0, concat_axis=0, tiled=True)  70.9 us
    ppermute x14, starting transfers between devices, trade(): return lax.ppermute(array, axis, pairs)  44.4 us
    ppermute x6, waiting for transfers between devices, along_x(): return lax.ppermute(array, 'gr', pairs)  23.1 us
    ppermute x6, starting transfers between devices, along_x(): return lax.ppermute(array, 'gr', pairs)  19.5 us
    all_to_all x1, waiting for transfers between devices, on_device(): lax.all_to_all(jnp.broadcast_to(features[0, 0][None], (n_y, local, width)...  16 us
    pallas_call x1, Pallas kernels, on_device(): call(functools.partial(backward_kernel, col_slots), jax.ShapeDtypeStruct(...  8.3 us
    pallas_call x1, Pallas kernels, on_device(): call(functools.partial(forward_kernel, col_slots), jax.ShapeDtypeStruct((...  7.78 us
  transfers between devices with their start and end apart: 22, of which 18 were waited for; matrix products, arithmetic and copies ran while one was open for 0% of the time, Pallas kernels for 0%

profile of v3, /device:TPU:4, one launch (start us, length us, event | category | flops | bytes accessed | tf_op | source)
XLA Modules:
  0.0 293.2 jit_solution(9876852154323522926)
XLA Ops:
  2.7 7.1 %all-to-all-start = ((bf16[8,512,128]{2,1,0:T(8,128)(2,1)}), bf16[8,512,128]{2,1,0:T(8,128)(2,1)S(1)}, u32[]{:S(2)}, u32[]{:S(2)}) async-start(bf16[8,512,128]{2,1,0:T(8,128)(2,1)} %broadcast_in_dim.8), calls=%async_computation | async-start | bytes 2097152 | tf_op jit(solution)/shard_map/all_to_all | solution.py:254
  12.5 4.6 %collective-permute-start.1 = (s32[1,128]{1,0:T(1,128)S(1)}, s32[1,128]{1,0:T(1,128)S(1)}, u32[]{:S(2)}, u32[]{:S(2)}) collective-permute-start(s32[1,128]{1,0:T(1,128)S(1)} %pad.4.need), channel_id=1, source_target_pairs={{0,32},{16,48},{32,0},{48,16},{64,96},{80,112},{96,64},{112,80},{1... | collective-permute-start | bytes 1544 | tf_op jit(solution)/shard_map/ppermute | solution.py:252
  17.1 3.6 %collective-permute-start.2 = (s32[1,128]{1,0:T(1,128)S(1)}, s32[1,128]{1,0:T(1,128)S(1)}, u32[]{:S(2)}, u32[]{:S(2)}) collective-permute-start(s32[1,128]{1,0:T(1,128)S(1)} %pad.4.need), channel_id=1, source_target_pairs={{0,16},{16,32},{32,48},{48,0},{64,80},{80,96},{96,112},{112,64},{1... | collective-permute-start | bytes 1544 | tf_op jit(solution)/shard_map/ppermute | solution.py:252
  22.6 16.0 %all-to-all-done.refs_3_.column = bf16[8,512,128]{2,1,0:T(8,128)(2,1)S(1)} async-done(((bf16[8,512,128]{2,1,0:T(8,128)(2,1)}), bf16[8,512,128]{2,1,0:T(8,128)(2,1)S(1)}, u32[]{:S(2)}, u32[]{:S(2)}) %all-to-all-start) | async-done | bytes 1048608 | tf_op jit(solution)/shard_map/all_to_all | solution.py:254
  40.6 3.1 %collective-permute-start.3 = (bf16[8,256,128]{2,1,0:T(8,128)(2,1)}, bf16[8,256,128]{2,1,0:T(8,128)(2,1)S(1)}, u32[]{:S(2)}, u32[]{:S(2)}) collective-permute-start(bf16[8,256,128]{2,1,0:T(8,128)(2,1)} %get-tuple-element.9), channel_id=1, source_target_pairs={{0,16},{16,32},{32,48},{48,0},{64,80},{80,96},{96,112},{112,64},{1... | collective-permute-start | bytes 1572872 | tf_op jit(solution)/shard_map/ppermute | solution.py:252
  46.4 3.0 %collective-permute-start.5 = (bf16[8,256,128]{2,1,0:T(8,128)(2,1)S(1)}, bf16[8,256,128]{2,1,0:T(8,128)(2,1)S(1)}, u32[]{:S(2)}, u32[]{:S(2)}) collective-permute-start(bf16[8,256,128]{2,1,0:T(8,128)(2,1)S(1)} %get-tuple-element.11), channel_id=1, source_target_pairs={{0,48},{16,0},{32,16},{48,32},{64,112},{80,64},{96,80},{112,96},{1... | collective-permute-start | bytes 1572872 | tf_op jit(solution)/shard_map/ppermute | solution.py:252
  50.2 7.3 %collective-permute-done.3 = bf16[8,256,128]{2,1,0:T(8,128)(2,1)S(1)} collective-permute-done((bf16[8,256,128]{2,1,0:T(8,128)(2,1)}, bf16[8,256,128]{2,1,0:T(8,128)(2,1)S(1)}, u32[]{:S(2)}, u32[]{:S(2)}) %collective-permute-start.3) | collective-permute-done | bytes 524320 | tf_op jit(solution)/shard_map/ppermute | solution.py:252
  57.5 10.3 %collective-permute-done.4 = bf16[8,256,128]{2,1,0:T(8,128)(2,1)S(1)} collective-permute-done((bf16[8,256,128]{2,1,0:T(8,128)(2,1)}, bf16[8,256,128]{2,1,0:T(8,128)(2,1)S(1)}, u32[]{:S(2)}, u32[]{:S(2)}) %collective-permute-start.4) | collective-permute-done | bytes 524320 | tf_op jit(solution)/shard_map/ppermute | solution.py:252
  67.8 3.7 %collective-permute-done.5 = bf16[8,256,128]{2,1,0:T(8,128)(2,1)S(1)} collective-permute-done((bf16[8,256,128]{2,1,0:T(8,128)(2,1)S(1)}, bf16[8,256,128]{2,1,0:T(8,128)(2,1)S(1)}, u32[]{:S(2)}, u32[]{:S(2)}) %collective-permute-start.5) | collective-permute-done | bytes 524320 | tf_op jit(solution)/shard_map/ppermute | solution.py:252
  73.7 7.8 %shard_map.104 = bf16[16,272,128]{2,1,0:T(8,128)(2,1)S(1)} custom-call(s32[1,1]{1,0:T(1,128)} %bitcast.me, s32[1,128]{1,0:T(1,128)S(1)} %bitcast.20, s32[1,1]{1,0:T(1,128)S(6)} %copy.15.live, s32[16,2]{1,0:T(8,128)S(1)} %copy.14.row_need, s32[1,128]{1,0:T(1,128)S(1)} %pad.4.need, bf16[128,128,128]{2,1,0:T(8,128)(2,1)S(1)} %bitcast.14, ...), custom_call_target="tpu_custom_call" | custom-call | flops 536870912 | bytes 8388608 | tf_op jit(solution)/shard_map/pallas_call | solution.py:275
  81.5 40.5 %all_to_all.20.arrived = bf16[16,272,128]{2,1,0:T(8,128)(2,1)S(1)} all-to-all(bf16[16,272,128]{2,1,0:T(8,128)(2,1)S(1)} %shard_map.104), channel_id=1, replica_groups=mesh['gr'=32,'gc'=16] {'gc'}, dimensions={0} | all-to-all | bytes 2228224 | tf_op jit(solution)/shard_map/all_to_all | solution.py:238
  124.1 30.4 %all_to_all.21.arrived = bf16[16,256,128]{2,1,0:T(8,128)(2,1)} all-to-all(bf16[16,256,128]{2,1,0:T(8,128)(2,1)S(1)} %get-tuple-element.14), channel_id=1, replica_groups=mesh['gr'=32,'gc'=16] {'gc'}, dimensions={0} | all-to-all | bytes 2097152 | tf_op jit(solution)/shard_map/all_to_all | solution.py:238
  154.5 8.3 %shard_map.106 = bf16[32,256,128]{2,1,0:T(8,128)(2,1)} custom-call(s32[1,128]{1,0:T(1,128)} %bitcast.19, s32[1,1]{1,0:T(1,128)S(6)} %copy.15.live, bf16[128,128,128]{2,1,0:T(8,128)(2,1)} %bitcast.13, bf16[16,256,128]{2,1,0:T(8,128)(2,1)} %all_to_all.21.arrived), custom_call_target="tpu_custom_call" | custom-call | flops 536870912 | bytes 8388608 | tf_op jit(solution)/shard_map/pallas_call | solution.py:335
  162.8 5.0 %all-to-all-start.3 = ((bf16[32,256,128]{2,1,0:T(8,128)(2,1)}), bf16[32,256,128]{2,1,0:T(8,128)(2,1)S(1)}, u32[]{:S(2)}, u32[]{:S(2)}) async-start(bf16[32,256,128]{2,1,0:T(8,128)(2,1)} %shard_map.106), calls=%async_computation.3 | async-start | bytes 4194304 | tf_op jit(solution)/shard_map/all_to_all | solution.py:238
  167.8 3.1 %collective-permute-start.6 = (f32[64,128]{1,0:T(8,128)S(1)}, f32[64,128]{1,0:T(8,128)S(1)}, u32[]{:S(2)}, u32[]{:S(2)}) collective-permute-start(f32[64,128]{1,0:T(8,128)S(1)} %slice_select_fusion), channel_id=1, source_target_pairs={{0,16},{16,0},{32,48},{48,32},{64,80},{80,64},{96,112},{112,96},{1... | collective-permute-start | bytes 98312 | tf_op jit(solution)/shard_map/ppermute | solution.py:242
  170.9 3.2 %collective-permute-done.6 = f32[64,128]{1,0:T(8,128)S(1)} collective-permute-done((f32[64,128]{1,0:T(8,128)S(1)}, f32[64,128]{1,0:T(8,128)S(1)}, u32[]{:S(2)}, u32[]{:S(2)}) %collective-permute-start.6) | collective-permute-done | bytes 32800 | tf_op jit(solution)/shard_map/ppermute | solution.py:242
  176.2 5.2 %collective-permute-done.7 = f32[32,128]{1,0:T(8,128)S(1)} collective-permute-done((f32[32,128]{1,0:T(8,128)S(1)}, f32[32,128]{1,0:T(8,128)S(1)}, u32[]{:S(2)}, u32[]{:S(2)}) %collective-permute-start.7) | collective-permute-done | bytes 16416 | tf_op jit(solution)/shard_map/ppermute | solution.py:242
  181.4 5.0 %collective-permute-start.8 = (f32[32,128]{1,0:T(8,128)S(1)}, f32[32,128]{1,0:T(8,128)S(1)}, u32[]{:S(2)}, u32[]{:S(2)}) collective-permute-start(f32[32,128]{1,0:T(8,128)S(1)} %select_add_fusion.1), channel_id=1, source_target_pairs={{0,64},{16,80},{32,96},{48,112},{64,0},{80,16},{96,32},{112,48},{1... | collective-permute-start | bytes 49160 | tf_op jit(solution)/shard_map/ppermute | solution.py:242
  186.4 29.9 %collective-permute-done.8 = f32[32,128]{1,0:T(8,128)S(1)} collective-permute-done((f32[32,128]{1,0:T(8,128)S(1)}, f32[32,128]{1,0:T(8,128)S(1)}, u32[]{:S(2)}, u32[]{:S(2)}) %collective-permute-start.8) | collective-permute-done | bytes 16416 | tf_op jit(solution)/shard_map/ppermute | solution.py:242
  216.3 3.8 %collective-permute-start.9 = (f32[32,128]{1,0:T(8,128)S(1)}, f32[32,128]{1,0:T(8,128)S(1)}, u32[]{:S(2)}, u32[]{:S(2)}) collective-permute-start(f32[32,128]{1,0:T(8,128)S(1)} %add.31), channel_id=1, source_target_pairs={{0,128},{16,144},{32,160},{48,176},{64,192},{80,208},{96,224},{112... | collective-permute-start | bytes 49160 | tf_op jit(solution)/shard_map/ppermute | solution.py:242
  222.9 5.5 %collective-permute-start.10 = (f32[32,128]{1,0:T(8,128)S(1)}, f32[32,128]{1,0:T(8,128)S(1)}, u32[]{:S(2)}, u32[]{:S(2)}) collective-permute-start(f32[32,128]{1,0:T(8,128)S(1)} %add.32), channel_id=1, source_target_pairs={{0,256},{16,272},{32,288},{48,304},{64,320},{80,336},{96,352},{112... | collective-permute-start | bytes 49160 | tf_op jit(solution)/shard_map/ppermute | solution.py:242
  228.3 4.0 %collective-permute-done.10 = f32[32,128]{1,0:T(8,128)S(1)} collective-permute-done((f32[32,128]{1,0:T(8,128)S(1)}, f32[32,128]{1,0:T(8,128)S(1)}, u32[]{:S(2)}, u32[]{:S(2)}) %collective-permute-start.10) | collective-permute-done | bytes 16416 | tf_op jit(solution)/shard_map/ppermute | solution.py:242
  237.4 3.7 %collective-permute-done.12 = f32[32,128]{1,0:T(8,128)S(1)} collective-permute-done((f32[32,128]{1,0:T(8,128)S(1)}, f32[32,128]{1,0:T(8,128)S(1)}, u32[]{:S(2)}, u32[]{:S(2)}) %collective-permute-start.12) | collective-permute-done | bytes 16416 | tf_op jit(solution)/shard_map/ppermute | solution.py:242
  243.3 4.3 %collective-permute-done.13 = f32[32,128]{1,0:T(8,128)S(1)} collective-permute-done((f32[32,128]{1,0:T(8,128)S(1)}, f32[32,128]{1,0:T(8,128)S(1)}, u32[]{:S(2)}, u32[]{:S(2)}) %collective-permute-start.13) | collective-permute-done | bytes 16416 | tf_op jit(solution)/shard_map/ppermute | solution.py:242
  247.6 3.2 %collective-permute-start.14 = (f32[32,128]{1,0:T(8,128)S(1)}, f32[32,128]{1,0:T(8,128)S(1)}, u32[]{:S(2)}, u32[]{:S(2)}) collective-permute-start(f32[32,128]{1,0:T(8,128)S(1)} %add.36), channel_id=1, source_target_pairs={{0,8},{1,9},{2,10},{3,11},{4,12},{5,13},{6,14},{7,15},{8,0},{9,1},... | collective-permute-start | bytes 49160 | tf_op jit(solution)/shard_map/ppermute | solution.py:242
  250.8 6.5 %collective-permute-done.14 = f32[32,128]{1,0:T(8,128)S(1)} collective-permute-done((f32[32,128]{1,0:T(8,128)S(1)}, f32[32,128]{1,0:T(8,128)S(1)}, u32[]{:S(2)}, u32[]{:S(2)}) %collective-permute-start.14) | collective-permute-done | bytes 16416 | tf_op jit(solution)/shard_map/ppermute | solution.py:242
  259.8 4.7 %collective-permute-done.15 = f32[32,128]{1,0:T(8,128)S(1)} collective-permute-done((f32[32,128]{1,0:T(8,128)S(1)}, f32[32,128]{1,0:T(8,128)S(1)}, u32[]{:S(2)}, u32[]{:S(2)}) %collective-permute-start.15) | collective-permute-done | bytes 16416 | tf_op jit(solution)/shard_map/ppermute | solution.py:242
  264.4 4.3 %collective-permute-start.16 = (f32[64,128]{1,0:T(8,128)S(1)}, f32[64,128]{1,0:T(8,128)S(1)}, u32[]{:S(2)}, u32[]{:S(2)}) collective-permute-start(f32[64,128]{1,0:T(8,128)S(1)} %pad_maximum_fusion), channel_id=1, source_target_pairs={{0,16},{16,0},{32,48},{48,32},{64,80},{80,64},{96,112},{112,96},{1... | collective-permute-start | bytes 98312 | tf_op jit(solution)/shard_map/ppermute | solution.py:242
  270.7 3.6 %collective-permute-done.17 = s32[4,128]{1,0:T(4,128)S(1)} collective-permute-done((s32[4,128]{1,0:T(4,128)S(1)}, s32[4,128]{1,0:T(4,128)S(1)}, u32[]{:S(2)}, u32[]{:S(2)}) %collective-permute-start.17) | collective-permute-done | bytes 2080 | tf_op jit(solution)/shard_map/ppermute | solution.py:242
  276.3 4.4 %collective-permute-done.18 = s32[8,128]{1,0:T(8,128)S(1)} collective-permute-done((s32[8,128]{1,0:T(8,128)S(1)}, s32[8,128]{1,0:T(8,128)S(1)}, u32[]{:S(2)}, u32[]{:S(2)}) %collective-permute-start.18) | collective-permute-done | bytes 4128 | tf_op jit(solution)/shard_map/ppermute | solution.py:242
  280.7 5.2 %collective-permute-start.19 = (s32[16,128]{1,0:T(8,128)S(1)}, s32[16,128]{1,0:T(8,128)S(1)}, u32[]{:S(2)}, u32[]{:S(2)}) collective-permute-start(s32[16,128]{1,0:T(8,128)S(1)} %concatenate.25), channel_id=1, source_target_pairs={{0,256},{16,272},{32,288},{48,304},{64,320},{80,336},{96,352},{112... | collective-permute-start | bytes 24584 | tf_op jit(solution)/shard_map/ppermute | solution.py:242
  286.0 4.2 %collective-permute-done.19 = s32[16,128]{1,0:T(8,128)S(1)} collective-permute-done((s32[16,128]{1,0:T(8,128)S(1)}, s32[16,128]{1,0:T(8,128)S(1)}, u32[]{:S(2)}, u32[]{:S(2)}) %collective-permute-start.19) | collective-permute-done | bytes 8224 | tf_op jit(solution)/shard_map/ppermute | solution.py:242
  (55 shorter events, 37.0 us)
Async XLA Ops:
  0.6 9.2 %copy-start.4 = (s32[1,1,32,2]{2,3,1,0:T(2,128)S(1)}, s32[1,1,32,2]{2,3,1,0:T(2,128)}, u32[]{:S(2)}) copy-start(s32[1,1,32,2]{2,3,1,0:T(2,128)} %param.15) | copy-start | bytes 772
  0.6 49.5 %copy-start.5 = (s32[1,1,16,2]{2,3,1,0:T(2,128)S(1)}, s32[1,1,16,2]{2,3,1,0:T(2,128)}, u32[]{:S(2)}) copy-start(s32[1,1,16,2]{2,3,1,0:T(2,128)} %param.14) | copy-start | bytes 388
  0.7 70.9 %copy-start.3 = (s32[1,1,128]{2,1,0:T(1,128)S(1)}, s32[1,1,128]{2,1,0:T(1,128)}, u32[]{:S(2)}) copy-start(s32[1,1,128]{2,1,0:T(1,128)} %param.12) | copy-start | bytes 1540
  2.7 35.8 %all-to-all-start = ((bf16[8,512,128]{2,1,0:T(8,128)(2,1)}), bf16[8,512,128]{2,1,0:T(8,128)(2,1)S(1)}, u32[]{:S(2)}, u32[]{:S(2)}) async-start(bf16[8,512,128]{2,1,0:T(8,128)(2,1)} %broadcast_in_dim.8), calls=%async_computation | async-start | bytes 2097152 | tf_op jit(solution)/shard_map/all_to_all | solution.py:254
  10.0 10.7 %collective-permute-start = (s32[1,128]{1,0:T(1,128)S(1)}, s32[1,128]{1,0:T(1,128)S(1)}, u32[]{:S(2)}, u32[]{:S(2)}) collective-permute-start(s32[1,128]{1,0:T(1,128)S(1)} %pad.4.need), channel_id=1, source_target_pairs={{0,48},{16,0},{32,16},{48,32},{64,112},{80,64},{96,80},{112,96},{1... | collective-permute-start | bytes 1544 | tf_op jit(solution)/shard_map/ppermute | solution.py:252
  12.5 8.3 %collective-permute-start.1 = (s32[1,128]{1,0:T(1,128)S(1)}, s32[1,128]{1,0:T(1,128)S(1)}, u32[]{:S(2)}, u32[]{:S(2)}) collective-permute-start(s32[1,128]{1,0:T(1,128)S(1)} %pad.4.need), channel_id=1, source_target_pairs={{0,32},{16,48},{32,0},{48,16},{64,96},{80,112},{96,64},{112,80},{1... | collective-permute-start | bytes 1544 | tf_op jit(solution)/shard_map/ppermute | solution.py:252
  17.1 5.5 %collective-permute-start.2 = (s32[1,128]{1,0:T(1,128)S(1)}, s32[1,128]{1,0:T(1,128)S(1)}, u32[]{:S(2)}, u32[]{:S(2)}) collective-permute-start(s32[1,128]{1,0:T(1,128)S(1)} %pad.4.need), channel_id=1, source_target_pairs={{0,16},{16,32},{32,48},{48,0},{64,80},{80,96},{96,112},{112,64},{1... | collective-permute-start | bytes 1544 | tf_op jit(solution)/shard_map/ppermute | solution.py:252
  40.6 16.9 %collective-permute-start.3 = (bf16[8,256,128]{2,1,0:T(8,128)(2,1)}, bf16[8,256,128]{2,1,0:T(8,128)(2,1)S(1)}, u32[]{:S(2)}, u32[]{:S(2)}) collective-permute-start(bf16[8,256,128]{2,1,0:T(8,128)(2,1)} %get-tuple-element.9), channel_id=1, source_target_pairs={{0,16},{16,32},{32,48},{48,0},{64,80},{80,96},{96,112},{112,64},{1... | collective-permute-start | bytes 1572872 | tf_op jit(solution)/shard_map/ppermute | solution.py:252
  43.7 24.1 %collective-permute-start.4 = (bf16[8,256,128]{2,1,0:T(8,128)(2,1)}, bf16[8,256,128]{2,1,0:T(8,128)(2,1)S(1)}, u32[]{:S(2)}, u32[]{:S(2)}) collective-permute-start(bf16[8,256,128]{2,1,0:T(8,128)(2,1)} %get-tuple-element.10), channel_id=1, source_target_pairs={{0,32},{16,48},{32,0},{48,16},{64,96},{80,112},{96,64},{112,80},{1... | collective-permute-start | bytes 1572872 | tf_op jit(solution)/shard_map/ppermute | solution.py:252
  46.4 25.1 %collective-permute-start.5 = (bf16[8,256,128]{2,1,0:T(8,128)(2,1)S(1)}, bf16[8,256,128]{2,1,0:T(8,128)(2,1)S(1)}, u32[]{:S(2)}, u32[]{:S(2)}) collective-permute-start(bf16[8,256,128]{2,1,0:T(8,128)(2,1)S(1)} %get-tuple-element.11), channel_id=1, source_target_pairs={{0,48},{16,0},{32,16},{48,32},{64,112},{80,64},{96,80},{112,96},{1... | collective-permute-start | bytes 1572872 | tf_op jit(solution)/shard_map/ppermute | solution.py:252
  71.5 2.2 copy-start
  81.5 40.5 %copy-start.1 = (bf16[1,1,512,128]{3,2,1,0:T(8,128)(2,1)S(1)}, bf16[1,1,512,128]{3,2,1,0:T(8,128)(2,1)}, u32[]{:S(2)}) copy-start(bf16[1,1,512,128]{3,2,1,0:T(8,128)(2,1)} %param.9) | copy-start | bytes 393220
  81.5 40.5 %copy-start.2 = (bf16[128,128]{1,0:T(8,128)(2,1)S(1)}, bf16[128,128]{1,0:T(8,128)(2,1)}, u32[]{:S(2)}) copy-start(bf16[128,128]{1,0:T(8,128)(2,1)} %weight.1) | copy-start | bytes 98308
  162.8 128.0 %all-to-all-start.3 = ((bf16[32,256,128]{2,1,0:T(8,128)(2,1)}), bf16[32,256,128]{2,1,0:T(8,128)(2,1)S(1)}, u32[]{:S(2)}, u32[]{:S(2)}) async-start(bf16[32,256,128]{2,1,0:T(8,128)(2,1)} %shard_map.106), calls=%async_computation.3 | async-start | bytes 4194304 | tf_op jit(solution)/shard_map/all_to_all | solution.py:238
  167.8 6.3 %collective-permute-start.6 = (f32[64,128]{1,0:T(8,128)S(1)}, f32[64,128]{1,0:T(8,128)S(1)}, u32[]{:S(2)}, u32[]{:S(2)}) collective-permute-start(f32[64,128]{1,0:T(8,128)S(1)} %slice_select_fusion), channel_id=1, source_target_pairs={{0,16},{16,0},{32,48},{48,32},{64,80},{80,64},{96,112},{112,96},{1... | collective-permute-start | bytes 98312 | tf_op jit(solution)/shard_map/ppermute | solution.py:242
  174.2 7.2 %collective-permute-start.7 = (f32[32,128]{1,0:T(8,128)S(1)}, f32[32,128]{1,0:T(8,128)S(1)}, u32[]{:S(2)}, u32[]{:S(2)}) collective-permute-start(f32[32,128]{1,0:T(8,128)S(1)} %slice_select_fusion.1), channel_id=1, source_target_pairs={{0,32},{16,48},{32,0},{48,16},{64,96},{80,112},{96,64},{112,80},{1... | collective-permute-start | bytes 49160 | tf_op jit(solution)/shard_map/ppermute | solution.py:242
  181.4 34.9 %collective-permute-start.8 = (f32[32,128]{1,0:T(8,128)S(1)}, f32[32,128]{1,0:T(8,128)S(1)}, u32[]{:S(2)}, u32[]{:S(2)}) collective-permute-start(f32[32,128]{1,0:T(8,128)S(1)} %select_add_fusion.1), channel_id=1, source_target_pairs={{0,64},{16,80},{32,96},{48,112},{64,0},{80,16},{96,32},{112,48},{1... | collective-permute-start | bytes 49160 | tf_op jit(solution)/shard_map/ppermute | solution.py:242
  216.3 6.5 %collective-permute-start.9 = (f32[32,128]{1,0:T(8,128)S(1)}, f32[32,128]{1,0:T(8,128)S(1)}, u32[]{:S(2)}, u32[]{:S(2)}) collective-permute-start(f32[32,128]{1,0:T(8,128)S(1)} %add.31), channel_id=1, source_target_pairs={{0,128},{16,144},{32,160},{48,176},{64,192},{80,208},{96,224},{112... | collective-permute-start | bytes 49160 | tf_op jit(solution)/shard_map/ppermute | solution.py:242
  222.9 9.5 %collective-permute-start.10 = (f32[32,128]{1,0:T(8,128)S(1)}, f32[32,128]{1,0:T(8,128)S(1)}, u32[]{:S(2)}, u32[]{:S(2)}) collective-permute-start(f32[32,128]{1,0:T(8,128)S(1)} %add.32), channel_id=1, source_target_pairs={{0,256},{16,272},{32,288},{48,304},{64,320},{80,336},{96,352},{112... | collective-permute-start | bytes 49160 | tf_op jit(solution)/shard_map/ppermute | solution.py:242
  232.4 3.1 %collective-permute-start.11 = (f32[32,128]{1,0:T(8,128)S(1)}, f32[32,128]{1,0:T(8,128)S(1)}, u32[]{:S(2)}, u32[]{:S(2)}) collective-permute-start(f32[32,128]{1,0:T(8,128)S(1)} %add.33), channel_id=1, source_target_pairs={{0,1},{1,0},{2,3},{3,2},{4,5},{5,4},{6,7},{7,6},{8,9},{9,8},{10,11... | collective-permute-start | bytes 49160 | tf_op jit(solution)/shard_map/ppermute | solution.py:242
  235.5 5.6 %collective-permute-start.12 = (f32[32,128]{1,0:T(8,128)S(1)}, f32[32,128]{1,0:T(8,128)S(1)}, u32[]{:S(2)}, u32[]{:S(2)}) collective-permute-start(f32[32,128]{1,0:T(8,128)S(1)} %add.34), channel_id=1, source_target_pairs={{0,2},{1,3},{2,0},{3,1},{4,6},{5,7},{6,4},{7,5},{8,10},{9,11},{10,... | collective-permute-start | bytes 49160 | tf_op jit(solution)/shard_map/ppermute | solution.py:242
  241.1 6.5 %collective-permute-start.13 = (f32[32,128]{1,0:T(8,128)S(1)}, f32[32,128]{1,0:T(8,128)S(1)}, u32[]{:S(2)}, u32[]{:S(2)}) collective-permute-start(f32[32,128]{1,0:T(8,128)S(1)} %add.35), channel_id=1, source_target_pairs={{0,4},{1,5},{2,6},{3,7},{4,0},{5,1},{6,2},{7,3},{8,12},{9,13},{10,... | collective-permute-start | bytes 49160 | tf_op jit(solution)/shard_map/ppermute | solution.py:242
  247.6 9.7 %collective-permute-start.14 = (f32[32,128]{1,0:T(8,128)S(1)}, f32[32,128]{1,0:T(8,128)S(1)}, u32[]{:S(2)}, u32[]{:S(2)}) collective-permute-start(f32[32,128]{1,0:T(8,128)S(1)} %add.36), channel_id=1, source_target_pairs={{0,8},{1,9},{2,10},{3,11},{4,12},{5,13},{6,14},{7,15},{8,0},{9,1},... | collective-permute-start | bytes 49160 | tf_op jit(solution)/shard_map/ppermute | solution.py:242
  257.3 7.1 %collective-permute-start.15 = (f32[32,128]{1,0:T(8,128)S(1)}, f32[32,128]{1,0:T(8,128)S(1)}, u32[]{:S(2)}, u32[]{:S(2)}) collective-permute-start(f32[32,128]{1,0:T(8,128)S(1)} %add.37), channel_id=1, source_target_pairs={{0,32},{16,48},{32,0},{48,16},{64,96},{80,112},{96,64},{112,80},{1... | collective-permute-start | bytes 49160 | tf_op jit(solution)/shard_map/ppermute | solution.py:242
  264.4 25.8 %collective-permute-start.16 = (f32[64,128]{1,0:T(8,128)S(1)}, f32[64,128]{1,0:T(8,128)S(1)}, u32[]{:S(2)}, u32[]{:S(2)}) collective-permute-start(f32[64,128]{1,0:T(8,128)S(1)} %pad_maximum_fusion), channel_id=1, source_target_pairs={{0,16},{16,0},{32,48},{48,32},{64,80},{80,64},{96,112},{112,96},{1... | collective-permute-start | bytes 98312 | tf_op jit(solution)/shard_map/ppermute | solution.py:242
  268.8 5.5 %collective-permute-start.17 = (s32[4,128]{1,0:T(4,128)S(1)}, s32[4,128]{1,0:T(4,128)S(1)}, u32[]{:S(2)}, u32[]{:S(2)}) collective-permute-start(s32[4,128]{1,0:T(4,128)S(1)} %pad_add_fusion), channel_id=1, source_target_pairs={{0,64},{16,80},{32,96},{48,112},{64,0},{80,16},{96,32},{112,48},{1... | collective-permute-start | bytes 6152 | tf_op jit(solution)/shard_map/ppermute | solution.py:242
  274.3 6.4 %collective-permute-start.18 = (s32[8,128]{1,0:T(8,128)S(1)}, s32[8,128]{1,0:T(8,128)S(1)}, u32[]{:S(2)}, u32[]{:S(2)}) collective-permute-start(s32[8,128]{1,0:T(8,128)S(1)} %concatenate.24), channel_id=1, source_target_pairs={{0,128},{16,144},{32,160},{48,176},{64,192},{80,208},{96,224},{112... | collective-permute-start | bytes 12296 | tf_op jit(solution)/shard_map/ppermute | solution.py:242
  280.7 9.4 %collective-permute-start.19 = (s32[16,128]{1,0:T(8,128)S(1)}, s32[16,128]{1,0:T(8,128)S(1)}, u32[]{:S(2)}, u32[]{:S(2)}) collective-permute-start(s32[16,128]{1,0:T(8,128)S(1)} %concatenate.25), channel_id=1, source_target_pairs={{0,256},{16,272},{32,288},{48,304},{64,320},{80,336},{96,352},{112... | collective-permute-start | bytes 24584 | tf_op jit(solution)/shard_map/ppermute | solution.py:242

commit v4 on v3

--- a/solution.py
+++ b/solution.py
@@ -14,10 +14,9 @@
 GROUP = 8
 BATCH = 2
 PICK_GRANT = 40
-BACKWARD_GRANT = 58
+BACKWARD_GRANT = 40
 FORWARD_GRANT = 40
 
-ANY = pl.BlockSpec(memory_space=pl.ANY)
 VMEM = pl.BlockSpec(memory_space=pltpu.VMEM)
 SMEM = pl.BlockSpec(memory_space=pltpu.SMEM)
 HBM = pl.BlockSpec(memory_space=pltpu.HBM)
@@ -25,41 +24,62 @@
 
 def call(kernel, out_shape, in_specs, scratch=(), flops=0, moved=0, out_spec=VMEM, grant=48):
     many = isinstance(out_shape, (tuple, list))
+    chosen = isinstance(out_spec, tuple)
     return pl.pallas_call(
         kernel,
         out_shape=out_shape,
         in_specs=in_specs,
-        out_specs=tuple(out_spec for _ in out_shape) if many else out_spec,
+        out_specs=(out_spec,) * len(out_shape) if many and not chosen else out_spec,
         scratch_shapes=list(scratch),
         cost_estimate=pl.CostEstimate(flops=flops, bytes_accessed=moved, transcendentals=0),
         compiler_params=pltpu.CompilerParams(vmem_limit_bytes=grant << 20),
     )
 
 
+def repeat_kernel(feats, out, sems):
+    n = out.shape[0]
+    copies = [pltpu.make_async_copy(feats, out.at[y], sems.at[y]) for y in range(n)]
+    for copy in copies:
+        copy.start()
+    for copy in copies:
+        copy.wait()
+
+
 def pick_kernel(me, *refs):
     peers = NX - 1
-    tables, column, outs, sems = refs[:peers], refs[peers], refs[peers + 1 : -1], refs[-1]
-    n = column.shape[0]
+    tables, column, outs = refs[:peers], refs[peers], refs[peers + 1 :]
     blk = outs[0].shape[1] // 2
-    mine = me[0, 0] % NX
-
-    def copy(d, y, k):
-        start = pl.multiple_of(tables[d][0, 2 * (NX * y + mine) + k] * blk, blk)
-        return pltpu.make_async_copy(
-            column.at[y, pl.ds(start, blk), :],
-            outs[d].at[y, pl.ds(k * blk, blk), :],
-            sems.at[d, y, k],
-        )
-
-    every = [(d, y, k) for d in range(peers) for y in range(n) for k in range(2)]
-    for place in every:
-        copy(*place).start()
-    for place in every:
-        copy(*place).wait()
+    mine = me[0, 0] & (NX - 1)
+
+    def step(y, carry):
+        for d in range(peers):
+            for k in range(2):
+                start = pl.multiple_of(tables[d][0, 2 * (NX * y + mine) + k] * blk, blk)
+                outs[d][y, k * blk : (k + 1) * blk, :] = column[y, pl.ds(start, blk), :]
+        return carry
+
+    lax.fori_loop(0, column.shape[0], step, 0)
+
+
+def shipper(held, out, sems):
+    n = out.shape[0]
+
+    def copy(c):
+        return pltpu.make_async_copy(held.at[c], out.at[c], sems.at[c])
+
+    def ship(c):
+        if c:
+            copy(c - 1).start()
+        if c == n - 1:
+            copy(c).start()
+            for done in range(n):
+                copy(done).wait()
+
+    return ship
 
 
 def load_groups(live, source, values, sems):
-    groups = live[0, 0] // GROUP
+    groups = live[0, 0] >> 3
 
     def load(g):
         part = pl.ds(pl.multiple_of(g * GROUP, GROUP), GROUP)
@@ -74,32 +94,23 @@
 
 
 def forward_kernel(col_slots, me, slots, live, row_need, need, source, column, *refs):
-    peers, (out, values, arrived, acc, sems, own_sems, peer_sems) = refs[: NX - 1], refs[NX - 1 :]
+    peers, (out, values, arrived, acc, held, sems, out_sems) = refs[: NX - 1], refs[NX - 1 :]
     n, _, width = out.shape
     blk = values.shape[1]
-    rows = column.shape[0]
-    mine = me[0, 0] % NX
-
-    def own(y, k):
-        start = pl.multiple_of(need[0, 2 * (NX * y + mine) + k] * blk, blk)
-        return pltpu.make_async_copy(
-            column.at[y, pl.ds(start, blk), :], arrived.at[0, 2 * y + k], own_sems.at[y, k]
-        )
-
-    def received(d):
-        return pltpu.make_async_copy(peers[d], arrived.at[d + 1], peer_sems.at[d])
-
-    every = [(y, k) for y in range(rows) for k in range(2)]
-    for d in range(NX - 1):
-        received(d).start()
-    for place in every:
-        own(*place).start()
+    mine = me[0, 0] & (NX - 1)
+    shift = col_slots.bit_length() - 1
     groups, load = load_groups(live, source, values, sems)
     acc[...] = jnp.zeros_like(acc)
-    for d in range(NX - 1):
-        received(d).wait()
-    for place in every:
-        own(*place).wait()
+
+    def place(y, carry):
+        for k in range(2):
+            start = pl.multiple_of(need[0, 2 * (NX * y + mine) + k] * blk, blk)
+            arrived[0, 2 * y + k] = column[y, pl.ds(start, blk), :]
+            for d in range(NX - 1):
+                arrived[d + 1, 2 * y + k] = peers[d][2 * y + k]
+        return carry
+
+    lax.fori_loop(0, column.shape[0], place, 0)
 
     def group(g, carry):
         load(g).wait()
@@ -108,26 +119,29 @@
             for u in range(first, first + BATCH):
                 b = g * GROUP + u
                 slot = slots[0, b]
-                col = slot % col_slots
-                owner = col // 2
-                piece = (mine + NX - owner % NX) % NX
-                feats = arrived[piece, 2 * (owner // NX) + col % 2]
+                col = slot & (col_slots - 1)
+                piece = (mine - (col >> 1)) & (NX - 1)
+                feats = arrived[piece, ((col >> 3) << 1) + (col & 1)]
                 term = jnp.dot(values[b], feats, preferred_element_type=F32)
-                terms.append((slot // col_slots, term))
+                terms.append((slot >> shift, term))
             for row, term in terms:
                 acc[row] += term
         return carry
 
     lax.fori_loop(0, groups, group, 0)
     sub = lax.broadcasted_iota(jnp.int32, (EXTRA, width), 0)
+    ship = shipper(held, out, out_sems)
     for c in range(n):
         for k in range(2):
-            out[c, k * blk : (k + 1) * blk, :] = acc[2 * c + k].astype(BF16)
+            held[c, k * blk : (k + 1) * blk, :] = acc[2 * c + k].astype(BF16)
         ids = jnp.where(sub < EXTRA // 2, row_need[c, 0], row_need[c, 1])
-        out[c, 2 * blk :, :] = ids.astype(F32).astype(BF16)
-
-
-def middle_kernel(arrived, weight, upstream, act, out, local_term, back):
+        held[c, 2 * blk :, :] = ids.astype(F32).astype(BF16)
+        ship(c)
+
+
+def middle_kernel(
+    arrived, weight, upstream, act, out, local_term, back, held, sems
+):
     n, rows, width = arrived.shape
     blk = (rows - EXTRA) // 2
     per_dev = upstream.shape[0] // blk
@@ -154,18 +168,21 @@
             grad, w, (((1,), (1,)), ((), ())), preferred_element_type=F32
         ).astype(BF16)
     local_term[...] = total
+    ship = shipper(held, out, sems)
     for c in range(n):
         for k in range(2):
             chosen = back[0]
             for q in range(1, per_dev):
                 chosen = jnp.where(ids[c][k].astype(BF16) == float(q), back[q], chosen)
-            out[c, k * blk : (k + 1) * blk, :] = chosen
+            held[c, k * blk : (k + 1) * blk, :] = chosen
+        ship(c)
 
 
 def backward_kernel(
     col_slots, slots, live, source, arrived, out, values, acc, held, load_sems, sems
 ):
     blk = values.shape[1]
+    shift = col_slots.bit_length() - 1
     groups, load = load_groups(live, source, values, load_sems)
     acc[...] = jnp.zeros_like(acc)
 
@@ -176,30 +193,21 @@
             for u in range(first, first + BATCH):
                 b = g * GROUP + u
                 slot = slots[0, b]
-                row = slot // col_slots
-                grads = arrived[row // 2, pl.ds(pl.multiple_of((row % 2) * blk, blk), blk), :]
+                grads = arrived[slot >> shift]
                 term = lax.dot_general(
                     values[b], grads, (((0,), (0,)), ((), ())), preferred_element_type=F32
                 )
-                terms.append((slot % col_slots, term))
+                terms.append((slot & (col_slots - 1), term))
             for col, term in terms:
                 acc[col] += term
         return carry
 
     lax.fori_loop(0, groups, group, 0)
-    n = out.shape[0]
-
-    def copy(r):
-        return pltpu.make_async_copy(held.at[r], out.at[r], sems.at[r])
-
-    for r in range(n):
+    ship = shipper(held, out, sems)
+    for r in range(out.shape[0]):
         for k in range(2):
             held[r, k * blk : (k + 1) * blk, :] = acc[2 * r + k].astype(BF16)
-        if r:
-            copy(r - 1).start()
-    copy(n - 1).start()
-    for r in range(n):
-        copy(r).wait()
+        ship(r)
 
 
 def final_kernel(me, asked, arrived, out, acc):
@@ -209,8 +217,8 @@
     acc[...] = jnp.zeros_like(acc)
 
     def step(r, carry):
-        ring = (r % NX + NX - mine % NX) % NX
-        place = ((r // NX) ^ (mine // NX)) * NX + ring
+        ring = (r - mine) & (NX - 1)
+        place = ((r ^ mine) & ~(NX - 1)) | ring
         for k in range(2):
             term = arrived[r, k * blk : (k + 1) * blk, :].astype(F32)
             acc[asked[place, 2 * mine + k]] += term
@@ -224,7 +232,7 @@
 def on_device(features, out_grad, weight, block_values, block_slot, live_count, row_need, col_need):
     n_rows = lax.axis_size("gr")
     n_cols = lax.axis_size("gc")
-    values = block_values[0, 0]
+    values = pltpu.with_memory_space_constraint(block_values[0, 0], pltpu.HBM)
     slot_total, blk, _ = values.shape
     local, width = features.shape[2:]
     cap = row_need.shape[3]
@@ -251,8 +259,17 @@
         pairs = [(i, i - i % NX + (i + shift) % NX) for i in range(n_rows)]
         return lax.ppermute(array, "gr", pairs)
 
+    copies = call(
+        repeat_kernel,
+        jax.ShapeDtypeStruct((n_y, local, width), BF16),
+        [VMEM],
+        [pltpu.SemaphoreType.DMA((n_y,))],
+        moved=2 << 20,
+        out_spec=HBM,
+        grant=60,
+    )(features[0, 0])
     column = lax.all_to_all(
-        jnp.broadcast_to(features[0, 0][None], (n_y, local, width)),
+        copies,
         "gr",
         split_axis=0,
         concat_axis=0,
@@ -265,27 +282,26 @@
         pick_kernel,
         [jax.ShapeDtypeStruct((n_y, cap * blk, width), BF16) for _ in tables],
         [SMEM, *[SMEM for _ in tables], VMEM],
-        [pltpu.SemaphoreType.DMA((NX - 1, n_y, cap))],
         moved=4 << 20,
-        out_spec=ANY,
         grant=PICK_GRANT,
     )(me, *tables, column)
     pieces = [along_x(chosen[d], d + 1) for d in range(NX - 1)]
     pieces = [p.reshape(cap * n_y, blk, width) for p in pieces]
     partial = call(
         functools.partial(forward_kernel, col_slots),
-        jax.ShapeDtypeStruct((n_cols, cap * blk + EXTRA, width), BF16),
-        [SMEM, SMEM, SMEM, SMEM, SMEM, HBM, ANY, *[ANY for _ in pieces]],
+        pltpu.HBM((n_cols, cap * blk + EXTRA, width), BF16),
+        [SMEM, SMEM, SMEM, SMEM, SMEM, HBM, VMEM, *[VMEM for _ in pieces]],
         [
             pltpu.VMEM(values.shape, BF16),
             pltpu.VMEM((NX, cap * n_y, blk, width), BF16),
             pltpu.VMEM((row_slots, blk, width), F32),
+            pltpu.VMEM((n_cols, cap * blk + EXTRA, width), BF16),
             pltpu.SemaphoreType.DMA((slot_total // GROUP,)),
-            pltpu.SemaphoreType.DMA((n_y, cap)),
-            pltpu.SemaphoreType.DMA((NX - 1,)),
+            pltpu.SemaphoreType.DMA((n_cols,)),
         ],
         flops=work,
         moved=8 << 20,
+        out_spec=HBM,
         grant=FORWARD_GRANT,
     )(me, slots, live_count, row_need[0, 0], need, values, column, *pieces)
     asked = jnp.concatenate([need, *tables], axis=0)
@@ -299,11 +315,16 @@
         middle_kernel,
         (
             jax.ShapeDtypeStruct((local, width), BF16),
-            jax.ShapeDtypeStruct((n_cols, cap * blk, width), BF16),
+            pltpu.HBM((n_cols, cap * blk, width), BF16),
             jax.ShapeDtypeStruct((width, width), F32),
         ),
         [VMEM, VMEM, VMEM],
-        [pltpu.VMEM((per_dev, blk, width), BF16)],
+        [
+            pltpu.VMEM((per_dev, blk, width), BF16),
+            pltpu.VMEM((n_cols, cap * blk, width), BF16),
+            pltpu.SemaphoreType.DMA((n_cols,)),
+        ],
+        out_spec=(VMEM, HBM, VMEM),
         flops=work // 8,
         moved=4 << 20,
     )(partial, weight, out_grad[0, 0])
@@ -334,7 +355,7 @@
 
     returned = call(
         functools.partial(backward_kernel, col_slots),
-        jax.ShapeDtypeStruct((n_rows, cap * blk, width), BF16),
+        pltpu.HBM((n_rows, cap * blk, width), BF16),
         [SMEM, SMEM, HBM, VMEM],
         [
             pltpu.VMEM(values.shape, BF16),
@@ -347,7 +368,7 @@
         moved=8 << 20,
         out_spec=HBM,
         grant=BACKWARD_GRANT,
-    )(slots, live_count, values, back)
+    )(slots, live_count, values, back.reshape(row_slots, blk, width))
     returned = swap(returned, "gr")
     input_grad = call(
         final_kernel,

time: 294 us -> 291 us (0.990)
  starting transfers between devices: 76 us -> 81.1 us
  waiting for transfers between devices: 117 us -> 112 us
  local copies, waits for them, and re-layouts: 4.59 us -> 0.37 us
    ppermute x14, waiting for transfers between devices: 77.7 us -> 72.6 us  [trade(): return lax.ppermute(array, axis, pairs)]
    ppermute x14, starting transfers between devices: 44.4 us -> 49.4 us  [trade(): return lax.ppermute(array, axis, pairs)]
    pallas_call x3 -> x4, Pallas kernels: 18.1 us -> 19.8 us  [the longest x1 7.74 us: on_device(): call(functools.partial(backward_kernel, col_slots), pltpu.HBM((n_rows, ca...]
where the time goes in v4:
time: 291 us; the launch traced here: 290 us
  waiting for transfers between devices  112 us (38%)
  starting transfers between devices  81.1 us (28%)
  blocking collectives  71.5 us (25%)
  Pallas kernels  23.5 us (8%)
    ppermute x14, waiting for transfers between devices, trade(): return lax.ppermute(array, axis, pairs)  72.6 us
    all_to_all x2, blocking collectives, swap(): return lax.all_to_all(array, axis, split_axis=0, concat_axis=0, tiled=True)  71.5 us
    ppermute x14, starting transfers between devices, trade(): return lax.ppermute(array, axis, pairs)  49.4 us
    ppermute x6, waiting for transfers between devices, along_x(): return lax.ppermute(array, 'gr', pairs)  23.1 us
    ppermute x6, starting transfers between devices, along_x(): return lax.ppermute(array, 'gr', pairs)  19.5 us
    all_to_all x1, waiting for transfers between devices, on_device(): lax.all_to_all(copies, 'gr', split_axis=0, concat_axis=0, tiled=True, axi...  16 us
    pallas_call x1, Pallas kernels, on_device(): call(functools.partial(backward_kernel, col_slots), pltpu.HBM((n_rows, ca...  7.74 us
    all_to_all x1, starting transfers between devices, on_device(): lax.all_to_all(copies, 'gr', split_axis=0, concat_axis=0, tiled=True, axi...  7.11 us
  transfers between devices with their start and end apart: 22, of which 18 were waited for; matrix products, arithmetic and copies ran while one was open for 0% of the time, Pallas kernels for 0%

profile of v4, /device:TPU:4, one launch (start us, length us, event | category | flops | bytes accessed | tf_op | source)
XLA Modules:
  0.0 290.5 jit_solution(8728968721898338556)
XLA Ops:
  2.6 7.1 %all-to-all-start = ((bf16[8,512,128]{2,1,0:T(8,128)(2,1)}), bf16[8,512,128]{2,1,0:T(8,128)(2,1)S(1)}, u32[]{:S(2)}, u32[]{:S(2)}) async-start(bf16[8,512,128]{2,1,0:T(8,128)(2,1)} %shard_map.103), calls=%async_computation | async-start | bytes 2097152 | tf_op jit(solution)/shard_map/all_to_all | solution.py:271
  12.4 4.6 %collective-permute-start.1 = (s32[1,128]{1,0:T(1,128)S(1)}, s32[1,128]{1,0:T(1,128)S(1)}, u32[]{:S(2)}, u32[]{:S(2)}) collective-permute-start(s32[1,128]{1,0:T(1,128)S(1)} %pad.4.need), channel_id=1, source_target_pairs={{0,32},{16,48},{32,0},{48,16},{64,96},{80,112},{96,64},{112,80},{1... | collective-permute-start | bytes 1544 | tf_op jit(solution)/shard_map/ppermute | solution.py:260
  17.1 3.6 %collective-permute-start.2 = (s32[1,128]{1,0:T(1,128)S(1)}, s32[1,128]{1,0:T(1,128)S(1)}, u32[]{:S(2)}, u32[]{:S(2)}) collective-permute-start(s32[1,128]{1,0:T(1,128)S(1)} %pad.4.need), channel_id=1, source_target_pairs={{0,16},{16,32},{32,48},{48,0},{64,80},{80,96},{96,112},{112,64},{1... | collective-permute-start | bytes 1544 | tf_op jit(solution)/shard_map/ppermute | solution.py:260
  22.5 16.0 %all-to-all-done.refs_3_.column = bf16[8,512,128]{2,1,0:T(8,128)(2,1)S(1)} async-done(((bf16[8,512,128]{2,1,0:T(8,128)(2,1)}), bf16[8,512,128]{2,1,0:T(8,128)(2,1)S(1)}, u32[]{:S(2)}, u32[]{:S(2)}) %all-to-all-start) | async-done | bytes 1048608 | tf_op jit(solution)/shard_map/all_to_all | solution.py:271
  40.2 3.1 %collective-permute-start.3 = (bf16[8,256,128]{2,1,0:T(8,128)(2,1)}, bf16[8,256,128]{2,1,0:T(8,128)(2,1)S(1)}, u32[]{:S(2)}, u32[]{:S(2)}) collective-permute-start(bf16[8,256,128]{2,1,0:T(8,128)(2,1)} %get-tuple-element.9), channel_id=1, source_target_pairs={{0,16},{16,32},{32,48},{48,0},{64,80},{80,96},{96,112},{112,64},{1... | collective-permute-start | bytes 1572872 | tf_op jit(solution)/shard_map/ppermute | solution.py:260
  49.8 7.3 %collective-permute-done.3 = bf16[8,256,128]{2,1,0:T(8,128)(2,1)S(1)} collective-permute-done((bf16[8,256,128]{2,1,0:T(8,128)(2,1)}, bf16[8,256,128]{2,1,0:T(8,128)(2,1)S(1)}, u32[]{:S(2)}, u32[]{:S(2)}) %collective-permute-start.3) | collective-permute-done | bytes 524320 | tf_op jit(solution)/shard_map/ppermute | solution.py:260
  57.1 10.3 %collective-permute-done.4 = bf16[8,256,128]{2,1,0:T(8,128)(2,1)S(1)} collective-permute-done((bf16[8,256,128]{2,1,0:T(8,128)(2,1)}, bf16[8,256,128]{2,1,0:T(8,128)(2,1)S(1)}, u32[]{:S(2)}, u32[]{:S(2)}) %collective-permute-start.4) | collective-permute-done | bytes 524320 | tf_op jit(solution)/shard_map/ppermute | solution.py:260
  67.3 3.7 %collective-permute-done.5 = bf16[8,256,128]{2,1,0:T(8,128)(2,1)S(1)} collective-permute-done((bf16[8,256,128]{2,1,0:T(8,128)(2,1)S(1)}, bf16[8,256,128]{2,1,0:T(8,128)(2,1)S(1)}, u32[]{:S(2)}, u32[]{:S(2)}) %collective-permute-start.5) | collective-permute-done | bytes 524320 | tf_op jit(solution)/shard_map/ppermute | solution.py:260
  71.1 6.7 %shard_map.105 = bf16[16,272,128]{2,1,0:T(8,128)(2,1)} custom-call(s32[1,1]{1,0:T(1,128)} %bitcast.me, s32[1,128]{1,0:T(1,128)S(1)} %bitcast.19, s32[1,1]{1,0:T(1,128)S(6)} %copy.15.live, s32[16,2]{1,0:T(8,128)S(1)} %copy.14.row_need, s32[1,128]{1,0:T(1,128)S(1)} %pad.4.need, bf16[128,128,128]{2,1,0:T(8,128)(2,1)} %bitcast.21, ...), custom_call_target="tpu_custom_call" | custom-call | flops 536870912 | bytes 8388608 | tf_op jit(solution)/shard_map/pallas_call | solution.py:290
  77.8 40.7 %all_to_all.20.arrived = bf16[16,272,128]{2,1,0:T(8,128)(2,1)S(1)} all-to-all(bf16[16,272,128]{2,1,0:T(8,128)(2,1)} %shard_map.105), channel_id=1, replica_groups=mesh['gr'=32,'gc'=16] {'gc'}, dimensions={0} | all-to-all | bytes 2228224 | tf_op jit(solution)/shard_map/all_to_all | solution.py:246
  118.5 3.4 %shard_map.106 = (bf16[512,128]{1,0:T(8,128)(2,1)}, bf16[16,256,128]{2,1,0:T(8,128)(2,1)}, f32[128,128]{1,0:T(8,128)S(1)}) custom-call(bf16[16,272,128]{2,1,0:T(8,128)(2,1)S(1)} %all_to_all.20.arrived, bf16[128,128]{1,0:T(8,128)(2,1)S(1)} %copy-done.1, bf16[512,128]{1,0:T(8,128)(2,1)S(1)} %bitcast.18), custom_call_target="tpu_custom_call" | custom-call | flops 67108864 | bytes 4194304 | tf_op jit(solution)/shard_map/pallas_call | solution.py:314
  121.9 30.8 %all_to_all.21 = bf16[16,256,128]{2,1,0:T(8,128)(2,1)S(1)} all-to-all(bf16[16,256,128]{2,1,0:T(8,128)(2,1)} %get-tuple-element.14), channel_id=1, replica_groups=mesh['gr'=32,'gc'=16] {'gc'}, dimensions={0} | all-to-all | bytes 2097152 | tf_op jit(solution)/shard_map/all_to_all | solution.py:246
  152.7 7.7 %shard_map.107 = bf16[32,256,128]{2,1,0:T(8,128)(2,1)} custom-call(s32[1,128]{1,0:T(1,128)S(1)} %bitcast.20, s32[1,1]{1,0:T(1,128)S(6)} %copy.15.live, bf16[128,128,128]{2,1,0:T(8,128)(2,1)} %bitcast.22, bf16[32,128,128]{2,1,0:T(8,128)(2,1)S(1)} %bitcast.14), custom_call_target="tpu_custom_call" | custom-call | flops 536870912 | bytes 8388608 | tf_op jit(solution)/shard_map/pallas_call | solution.py:356
  160.4 5.0 %all-to-all-start.3 = ((bf16[32,256,128]{2,1,0:T(8,128)(2,1)}), bf16[32,256,128]{2,1,0:T(8,128)(2,1)S(1)}, u32[]{:S(2)}, u32[]{:S(2)}) async-start(bf16[32,256,128]{2,1,0:T(8,128)(2,1)} %shard_map.107), calls=%async_computation.3 | async-start | bytes 4194304 | tf_op jit(solution)/shard_map/all_to_all | solution.py:246
  168.5 3.2 %collective-permute-done.6 = f32[64,128]{1,0:T(8,128)S(1)} collective-permute-done((f32[64,128]{1,0:T(8,128)S(1)}, f32[64,128]{1,0:T(8,128)S(1)}, u32[]{:S(2)}, u32[]{:S(2)}) %collective-permute-start.6) | collective-permute-done | bytes 32800 | tf_op jit(solution)/shard_map/ppermute | solution.py:250
  173.8 5.2 %collective-permute-done.7 = f32[32,128]{1,0:T(8,128)S(1)} collective-permute-done((f32[32,128]{1,0:T(8,128)S(1)}, f32[32,128]{1,0:T(8,128)S(1)}, u32[]{:S(2)}, u32[]{:S(2)}) %collective-permute-start.7) | collective-permute-done | bytes 16416 | tf_op jit(solution)/shard_map/ppermute | solution.py:250
  179.0 5.0 %collective-permute-start.8 = (f32[32,128]{1,0:T(8,128)S(1)}, f32[32,128]{1,0:T(8,128)S(1)}, u32[]{:S(2)}, u32[]{:S(2)}) collective-permute-start(f32[32,128]{1,0:T(8,128)S(1)} %select_add_fusion.1), channel_id=1, source_target_pairs={{0,64},{16,80},{32,96},{48,112},{64,0},{80,16},{96,32},{112,48},{1... | collective-permute-start | bytes 49160 | tf_op jit(solution)/shard_map/ppermute | solution.py:250
  184.0 29.1 %collective-permute-done.8 = f32[32,128]{1,0:T(8,128)S(1)} collective-permute-done((f32[32,128]{1,0:T(8,128)S(1)}, f32[32,128]{1,0:T(8,128)S(1)}, u32[]{:S(2)}, u32[]{:S(2)}) %collective-permute-start.8) | collective-permute-done | bytes 16416 | tf_op jit(solution)/shard_map/ppermute | solution.py:250
  213.1 4.9 %collective-permute-start.9 = (f32[32,128]{1,0:T(8,128)S(1)}, f32[32,128]{1,0:T(8,128)S(1)}, u32[]{:S(2)}, u32[]{:S(2)}) collective-permute-start(f32[32,128]{1,0:T(8,128)S(1)} %add.31), channel_id=1, source_target_pairs={{0,128},{16,144},{32,160},{48,176},{64,192},{80,208},{96,224},{112... | collective-permute-start | bytes 49160 | tf_op jit(solution)/shard_map/ppermute | solution.py:250
  219.7 6.1 %collective-permute-start.10 = (f32[32,128]{1,0:T(8,128)S(1)}, f32[32,128]{1,0:T(8,128)S(1)}, u32[]{:S(2)}, u32[]{:S(2)}) collective-permute-start(f32[32,128]{1,0:T(8,128)S(1)} %add.32), channel_id=1, source_target_pairs={{0,256},{16,272},{32,288},{48,304},{64,320},{80,336},{96,352},{112... | collective-permute-start | bytes 49160 | tf_op jit(solution)/shard_map/ppermute | solution.py:250
  225.8 3.4 %collective-permute-done.10 = f32[32,128]{1,0:T(8,128)S(1)} collective-permute-done((f32[32,128]{1,0:T(8,128)S(1)}, f32[32,128]{1,0:T(8,128)S(1)}, u32[]{:S(2)}, u32[]{:S(2)}) %collective-permute-start.10) | collective-permute-done | bytes 16416 | tf_op jit(solution)/shard_map/ppermute | solution.py:250
  234.2 3.7 %collective-permute-done.12 = f32[32,128]{1,0:T(8,128)S(1)} collective-permute-done((f32[32,128]{1,0:T(8,128)S(1)}, f32[32,128]{1,0:T(8,128)S(1)}, u32[]{:S(2)}, u32[]{:S(2)}) %collective-permute-start.12) | collective-permute-done | bytes 16416 | tf_op jit(solution)/shard_map/ppermute | solution.py:250
  240.9 3.6 %collective-permute-done.13 = f32[32,128]{1,0:T(8,128)S(1)} collective-permute-done((f32[32,128]{1,0:T(8,128)S(1)}, f32[32,128]{1,0:T(8,128)S(1)}, u32[]{:S(2)}, u32[]{:S(2)}) %collective-permute-start.13) | collective-permute-done | bytes 16416 | tf_op jit(solution)/shard_map/ppermute | solution.py:250
  244.5 4.0 %collective-permute-start.14 = (f32[32,128]{1,0:T(8,128)S(1)}, f32[32,128]{1,0:T(8,128)S(1)}, u32[]{:S(2)}, u32[]{:S(2)}) collective-permute-start(f32[32,128]{1,0:T(8,128)S(1)} %add.36), channel_id=1, source_target_pairs={{0,8},{1,9},{2,10},{3,11},{4,12},{5,13},{6,14},{7,15},{8,0},{9,1},... | collective-permute-start | bytes 49160 | tf_op jit(solution)/shard_map/ppermute | solution.py:250
  248.4 5.6 %collective-permute-done.14 = f32[32,128]{1,0:T(8,128)S(1)} collective-permute-done((f32[32,128]{1,0:T(8,128)S(1)}, f32[32,128]{1,0:T(8,128)S(1)}, u32[]{:S(2)}, u32[]{:S(2)}) %collective-permute-start.14) | collective-permute-done | bytes 16416 | tf_op jit(solution)/shard_map/ppermute | solution.py:250
  254.0 3.4 %collective-permute-start.15 = (f32[32,128]{1,0:T(8,128)S(1)}, f32[32,128]{1,0:T(8,128)S(1)}, u32[]{:S(2)}, u32[]{:S(2)}) collective-permute-start(f32[32,128]{1,0:T(8,128)S(1)} %add.37), channel_id=1, source_target_pairs={{0,32},{16,48},{32,0},{48,16},{64,96},{80,112},{96,64},{112,80},{1... | collective-permute-start | bytes 49160 | tf_op jit(solution)/shard_map/ppermute | solution.py:250
  257.4 3.7 %collective-permute-done.15 = f32[32,128]{1,0:T(8,128)S(1)} collective-permute-done((f32[32,128]{1,0:T(8,128)S(1)}, f32[32,128]{1,0:T(8,128)S(1)}, u32[]{:S(2)}, u32[]{:S(2)}) %collective-permute-start.15) | collective-permute-done | bytes 16416 | tf_op jit(solution)/shard_map/ppermute | solution.py:250
  261.1 5.3 %collective-permute-start.16 = (f32[64,128]{1,0:T(8,128)S(1)}, f32[64,128]{1,0:T(8,128)S(1)}, u32[]{:S(2)}, u32[]{:S(2)}) collective-permute-start(f32[64,128]{1,0:T(8,128)S(1)} %pad_maximum_fusion), channel_id=1, source_target_pairs={{0,16},{16,0},{32,48},{48,32},{64,80},{80,64},{96,112},{112,96},{1... | collective-permute-start | bytes 98312 | tf_op jit(solution)/shard_map/ppermute | solution.py:250
  268.3 3.6 %collective-permute-done.17 = s32[4,128]{1,0:T(4,128)S(1)} collective-permute-done((s32[4,128]{1,0:T(4,128)S(1)}, s32[4,128]{1,0:T(4,128)S(1)}, u32[]{:S(2)}, u32[]{:S(2)}) %collective-permute-start.17) | collective-permute-done | bytes 2080 | tf_op jit(solution)/shard_map/ppermute | solution.py:250
  273.8 4.5 %collective-permute-done.18 = s32[8,128]{1,0:T(8,128)S(1)} collective-permute-done((s32[8,128]{1,0:T(8,128)S(1)}, s32[8,128]{1,0:T(8,128)S(1)}, u32[]{:S(2)}, u32[]{:S(2)}) %collective-permute-start.18) | collective-permute-done | bytes 4128 | tf_op jit(solution)/shard_map/ppermute | solution.py:250
  278.3 5.2 %collective-permute-start.19 = (s32[16,128]{1,0:T(8,128)S(1)}, s32[16,128]{1,0:T(8,128)S(1)}, u32[]{:S(2)}, u32[]{:S(2)}) collective-permute-start(s32[16,128]{1,0:T(8,128)S(1)} %concatenate.25), channel_id=1, source_target_pairs={{0,256},{16,272},{32,288},{48,304},{64,320},{80,336},{96,352},{112... | collective-permute-start | bytes 24584 | tf_op jit(solution)/shard_map/ppermute | solution.py:250
  283.6 4.2 %collective-permute-done.19 = s32[16,128]{1,0:T(8,128)S(1)} collective-permute-done((s32[16,128]{1,0:T(8,128)S(1)}, s32[16,128]{1,0:T(8,128)S(1)}, u32[]{:S(2)}, u32[]{:S(2)}) %collective-permute-start.19) | collective-permute-done | bytes 8224 | tf_op jit(solution)/shard_map/ppermute | solution.py:250
  (53 shorter events, 35.3 us)
Async XLA Ops:
  0.6 9.1 %copy-start.3 = (s32[1,1,32,2]{2,3,1,0:T(2,128)S(1)}, s32[1,1,32,2]{2,3,1,0:T(2,128)}, u32[]{:S(2)}) copy-start(s32[1,1,32,2]{2,3,1,0:T(2,128)} %param.15) | copy-start | bytes 772
  0.6 49.1 %copy-start.4 = (s32[1,1,16,2]{2,3,1,0:T(2,128)S(1)}, s32[1,1,16,2]{2,3,1,0:T(2,128)}, u32[]{:S(2)}) copy-start(s32[1,1,16,2]{2,3,1,0:T(2,128)} %param.14) | copy-start | bytes 388
  0.7 70.4 %copy-start.2 = (s32[1,1,128]{2,1,0:T(1,128)S(1)}, s32[1,1,128]{2,1,0:T(1,128)}, u32[]{:S(2)}) copy-start(s32[1,1,128]{2,1,0:T(1,128)} %param.12) | copy-start | bytes 1540
  2.6 35.8 %all-to-all-start = ((bf16[8,512,128]{2,1,0:T(8,128)(2,1)}), bf16[8,512,128]{2,1,0:T(8,128)(2,1)S(1)}, u32[]{:S(2)}, u32[]{:S(2)}) async-start(bf16[8,512,128]{2,1,0:T(8,128)(2,1)} %shard_map.103), calls=%async_computation | async-start | bytes 2097152 | tf_op jit(solution)/shard_map/all_to_all | solution.py:271
  10.0 10.7 %collective-permute-start = (s32[1,128]{1,0:T(1,128)S(1)}, s32[1,128]{1,0:T(1,128)S(1)}, u32[]{:S(2)}, u32[]{:S(2)}) collective-permute-start(s32[1,128]{1,0:T(1,128)S(1)} %pad.4.need), channel_id=1, source_target_pairs={{0,48},{16,0},{32,16},{48,32},{64,112},{80,64},{96,80},{112,96},{1... | collective-permute-start | bytes 1544 | tf_op jit(solution)/shard_map/ppermute | solution.py:260
  12.4 8.3 %collective-permute-start.1 = (s32[1,128]{1,0:T(1,128)S(1)}, s32[1,128]{1,0:T(1,128)S(1)}, u32[]{:S(2)}, u32[]{:S(2)}) collective-permute-start(s32[1,128]{1,0:T(1,128)S(1)} %pad.4.need), channel_id=1, source_target_pairs={{0,32},{16,48},{32,0},{48,16},{64,96},{80,112},{96,64},{112,80},{1... | collective-permute-start | bytes 1544 | tf_op jit(solution)/shard_map/ppermute | solution.py:260
  17.1 5.5 %collective-permute-start.2 = (s32[1,128]{1,0:T(1,128)S(1)}, s32[1,128]{1,0:T(1,128)S(1)}, u32[]{:S(2)}, u32[]{:S(2)}) collective-permute-start(s32[1,128]{1,0:T(1,128)S(1)} %pad.4.need), channel_id=1, source_target_pairs={{0,16},{16,32},{32,48},{48,0},{64,80},{80,96},{96,112},{112,64},{1... | collective-permute-start | bytes 1544 | tf_op jit(solution)/shard_map/ppermute | solution.py:260
  40.2 16.9 %collective-permute-start.3 = (bf16[8,256,128]{2,1,0:T(8,128)(2,1)}, bf16[8,256,128]{2,1,0:T(8,128)(2,1)S(1)}, u32[]{:S(2)}, u32[]{:S(2)}) collective-permute-start(bf16[8,256,128]{2,1,0:T(8,128)(2,1)} %get-tuple-element.9), channel_id=1, source_target_pairs={{0,16},{16,32},{32,48},{48,0},{64,80},{80,96},{96,112},{112,64},{1... | collective-permute-start | bytes 1572872 | tf_op jit(solution)/shard_map/ppermute | solution.py:260
  43.3 24.1 %collective-permute-start.4 = (bf16[8,256,128]{2,1,0:T(8,128)(2,1)}, bf16[8,256,128]{2,1,0:T(8,128)(2,1)S(1)}, u32[]{:S(2)}, u32[]{:S(2)}) collective-permute-start(bf16[8,256,128]{2,1,0:T(8,128)(2,1)} %get-tuple-element.10), channel_id=1, source_target_pairs={{0,32},{16,48},{32,0},{48,16},{64,96},{80,112},{96,64},{112,80},{1... | collective-permute-start | bytes 1572872 | tf_op jit(solution)/shard_map/ppermute | solution.py:260
  46.0 25.1 %collective-permute-start.5 = (bf16[8,256,128]{2,1,0:T(8,128)(2,1)S(1)}, bf16[8,256,128]{2,1,0:T(8,128)(2,1)S(1)}, u32[]{:S(2)}, u32[]{:S(2)}) collective-permute-start(bf16[8,256,128]{2,1,0:T(8,128)(2,1)S(1)} %get-tuple-element.11), channel_id=1, source_target_pairs={{0,48},{16,0},{32,16},{48,32},{64,112},{80,64},{96,80},{112,96},{1... | collective-permute-start | bytes 1572872 | tf_op jit(solution)/shard_map/ppermute | solution.py:260
  77.8 40.7 %copy-start = (bf16[1,1,512,128]{3,2,1,0:T(8,128)(2,1)S(1)}, bf16[1,1,512,128]{3,2,1,0:T(8,128)(2,1)}, u32[]{:S(2)}) copy-start(bf16[1,1,512,128]{3,2,1,0:T(8,128)(2,1)} %param.9) | copy-start | bytes 393220
  77.8 40.7 %copy-start.1 = (bf16[128,128]{1,0:T(8,128)(2,1)S(1)}, bf16[128,128]{1,0:T(8,128)(2,1)}, u32[]{:S(2)}) copy-start(bf16[128,128]{1,0:T(8,128)(2,1)} %weight.1) | copy-start | bytes 98308
  160.4 128.0 %all-to-all-start.3 = ((bf16[32,256,128]{2,1,0:T(8,128)(2,1)}), bf16[32,256,128]{2,1,0:T(8,128)(2,1)S(1)}, u32[]{:S(2)}, u32[]{:S(2)}) async-start(bf16[32,256,128]{2,1,0:T(8,128)(2,1)} %shard_map.107), calls=%async_computation.3 | async-start | bytes 4194304 | tf_op jit(solution)/shard_map/all_to_all | solution.py:246
  165.4 6.3 %collective-permute-start.6 = (f32[64,128]{1,0:T(8,128)S(1)}, f32[64,128]{1,0:T(8,128)S(1)}, u32[]{:S(2)}, u32[]{:S(2)}) collective-permute-start(f32[64,128]{1,0:T(8,128)S(1)} %slice_select_fusion), channel_id=1, source_target_pairs={{0,16},{16,0},{32,48},{48,32},{64,80},{80,64},{96,112},{112,96},{1... | collective-permute-start | bytes 98312 | tf_op jit(solution)/shard_map/ppermute | solution.py:250
  171.8 7.2 %collective-permute-start.7 = (f32[32,128]{1,0:T(8,128)S(1)}, f32[32,128]{1,0:T(8,128)S(1)}, u32[]{:S(2)}, u32[]{:S(2)}) collective-permute-start(f32[32,128]{1,0:T(8,128)S(1)} %slice_select_fusion.1), channel_id=1, source_target_pairs={{0,32},{16,48},{32,0},{48,16},{64,96},{80,112},{96,64},{112,80},{1... | collective-permute-start | bytes 49160 | tf_op jit(solution)/shard_map/ppermute | solution.py:250
  179.0 34.1 %collective-permute-start.8 = (f32[32,128]{1,0:T(8,128)S(1)}, f32[32,128]{1,0:T(8,128)S(1)}, u32[]{:S(2)}, u32[]{:S(2)}) collective-permute-start(f32[32,128]{1,0:T(8,128)S(1)} %select_add_fusion.1), channel_id=1, source_target_pairs={{0,64},{16,80},{32,96},{48,112},{64,0},{80,16},{96,32},{112,48},{1... | collective-permute-start | bytes 49160 | tf_op jit(solution)/shard_map/ppermute | solution.py:250
  213.1 6.6 %collective-permute-start.9 = (f32[32,128]{1,0:T(8,128)S(1)}, f32[32,128]{1,0:T(8,128)S(1)}, u32[]{:S(2)}, u32[]{:S(2)}) collective-permute-start(f32[32,128]{1,0:T(8,128)S(1)} %add.31), channel_id=1, source_target_pairs={{0,128},{16,144},{32,160},{48,176},{64,192},{80,208},{96,224},{112... | collective-permute-start | bytes 49160 | tf_op jit(solution)/shard_map/ppermute | solution.py:250
  219.7 9.5 %collective-permute-start.10 = (f32[32,128]{1,0:T(8,128)S(1)}, f32[32,128]{1,0:T(8,128)S(1)}, u32[]{:S(2)}, u32[]{:S(2)}) collective-permute-start(f32[32,128]{1,0:T(8,128)S(1)} %add.32), channel_id=1, source_target_pairs={{0,256},{16,272},{32,288},{48,304},{64,320},{80,336},{96,352},{112... | collective-permute-start | bytes 49160 | tf_op jit(solution)/shard_map/ppermute | solution.py:250
  229.2 3.1 %collective-permute-start.11 = (f32[32,128]{1,0:T(8,128)S(1)}, f32[32,128]{1,0:T(8,128)S(1)}, u32[]{:S(2)}, u32[]{:S(2)}) collective-permute-start(f32[32,128]{1,0:T(8,128)S(1)} %add.33), channel_id=1, source_target_pairs={{0,1},{1,0},{2,3},{3,2},{4,5},{5,4},{6,7},{7,6},{8,9},{9,8},{10,11... | collective-permute-start | bytes 49160 | tf_op jit(solution)/shard_map/ppermute | solution.py:250
  232.3 5.6 %collective-permute-start.12 = (f32[32,128]{1,0:T(8,128)S(1)}, f32[32,128]{1,0:T(8,128)S(1)}, u32[]{:S(2)}, u32[]{:S(2)}) collective-permute-start(f32[32,128]{1,0:T(8,128)S(1)} %add.34), channel_id=1, source_target_pairs={{0,2},{1,3},{2,0},{3,1},{4,6},{5,7},{6,4},{7,5},{8,10},{9,11},{10,... | collective-permute-start | bytes 49160 | tf_op jit(solution)/shard_map/ppermute | solution.py:250
  237.9 6.5 %collective-permute-start.13 = (f32[32,128]{1,0:T(8,128)S(1)}, f32[32,128]{1,0:T(8,128)S(1)}, u32[]{:S(2)}, u32[]{:S(2)}) collective-permute-start(f32[32,128]{1,0:T(8,128)S(1)} %add.35), channel_id=1, source_target_pairs={{0,4},{1,5},{2,6},{3,7},{4,0},{5,1},{6,2},{7,3},{8,12},{9,13},{10,... | collective-permute-start | bytes 49160 | tf_op jit(solution)/shard_map/ppermute | solution.py:250
  244.5 9.5 %collective-permute-start.14 = (f32[32,128]{1,0:T(8,128)S(1)}, f32[32,128]{1,0:T(8,128)S(1)}, u32[]{:S(2)}, u32[]{:S(2)}) collective-permute-start(f32[32,128]{1,0:T(8,128)S(1)} %add.36), channel_id=1, source_target_pairs={{0,8},{1,9},{2,10},{3,11},{4,12},{5,13},{6,14},{7,15},{8,0},{9,1},... | collective-permute-start | bytes 49160 | tf_op jit(solution)/shard_map/ppermute | solution.py:250
  254.0 7.1 %collective-permute-start.15 = (f32[32,128]{1,0:T(8,128)S(1)}, f32[32,128]{1,0:T(8,128)S(1)}, u32[]{:S(2)}, u32[]{:S(2)}) collective-permute-start(f32[32,128]{1,0:T(8,128)S(1)} %add.37), channel_id=1, source_target_pairs={{0,32},{16,48},{32,0},{48,16},{64,96},{80,112},{96,64},{112,80},{1... | collective-permute-start | bytes 49160 | tf_op jit(solution)/shard_map/ppermute | solution.py:250
  261.1 26.7 %collective-permute-start.16 = (f32[64,128]{1,0:T(8,128)S(1)}, f32[64,128]{1,0:T(8,128)S(1)}, u32[]{:S(2)}, u32[]{:S(2)}) collective-permute-start(f32[64,128]{1,0:T(8,128)S(1)} %pad_maximum_fusion), channel_id=1, source_target_pairs={{0,16},{16,0},{32,48},{48,32},{64,80},{80,64},{96,112},{112,96},{1... | collective-permute-start | bytes 98312 | tf_op jit(solution)/shard_map/ppermute | solution.py:250
  266.4 5.5 %collective-permute-start.17 = (s32[4,128]{1,0:T(4,128)S(1)}, s32[4,128]{1,0:T(4,128)S(1)}, u32[]{:S(2)}, u32[]{:S(2)}) collective-permute-start(s32[4,128]{1,0:T(4,128)S(1)} %pad_add_fusion), channel_id=1, source_target_pairs={{0,64},{16,80},{32,96},{48,112},{64,0},{80,16},{96,32},{112,48},{1... | collective-permute-start | bytes 6152 | tf_op jit(solution)/shard_map/ppermute | solution.py:250
  271.9 6.4 %collective-permute-start.18 = (s32[8,128]{1,0:T(8,128)S(1)}, s32[8,128]{1,0:T(8,128)S(1)}, u32[]{:S(2)}, u32[]{:S(2)}) collective-permute-start(s32[8,128]{1,0:T(8,128)S(1)} %concatenate.24), channel_id=1, source_target_pairs={{0,128},{16,144},{32,160},{48,176},{64,192},{80,208},{96,224},{112... | collective-permute-start | bytes 12296 | tf_op jit(solution)/shard_map/ppermute | solution.py:250
  278.3 9.4 %collective-permute-start.19 = (s32[16,128]{1,0:T(8,128)S(1)}, s32[16,128]{1,0:T(8,128)S(1)}, u32[]{:S(2)}, u32[]{:S(2)}) collective-permute-start(s32[16,128]{1,0:T(8,128)S(1)} %concatenate.25), channel_id=1, source_target_pairs={{0,256},{16,272},{32,288},{48,304},{64,320},{80,336},{96,352},{112... | collective-permute-start | bytes 24584 | tf_op jit(solution)/shard_map/ppermute | solution.py:250

commit v5 on v4

--- a/solution.py
+++ b/solution.py
@@ -13,6 +13,8 @@
 NX = 4
 GROUP = 8
 BATCH = 2
+PARTS = 4
+ROWS = 32
 PICK_GRANT = 40
 BACKWARD_GRANT = 40
 FORWARD_GRANT = 40
@@ -24,12 +26,11 @@
 
 def call(kernel, out_shape, in_specs, scratch=(), flops=0, moved=0, out_spec=VMEM, grant=48):
     many = isinstance(out_shape, (tuple, list))
-    chosen = isinstance(out_spec, tuple)
     return pl.pallas_call(
         kernel,
         out_shape=out_shape,
         in_specs=in_specs,
-        out_specs=(out_spec,) * len(out_shape) if many and not chosen else out_spec,
+        out_specs=(out_spec,) * len(out_shape) if many else out_spec,
         scratch_shapes=list(scratch),
         cost_estimate=pl.CostEstimate(flops=flops, bytes_accessed=moved, transcendentals=0),
         compiler_params=pltpu.CompilerParams(vmem_limit_bytes=grant << 20),
@@ -63,85 +64,150 @@
 
 def shipper(held, out, sems):
     n = out.shape[0]
-
-    def copy(c):
-        return pltpu.make_async_copy(held.at[c], out.at[c], sems.at[c])
+    size = n // PARTS
+
+    def copy(p):
+        part = pl.ds(p * size, size)
+        return pltpu.make_async_copy(held.at[part], out.at[part], sems.at[p])
 
     def ship(c):
-        if c:
-            copy(c - 1).start()
+        if c and c % size == 0:
+            copy(c // size - 1).start()
         if c == n - 1:
-            copy(c).start()
-            for done in range(n):
-                copy(done).wait()
+            copy(PARTS - 1).start()
+            for p in range(PARTS):
+                copy(p).wait()
 
     return ship
 
 
-def load_groups(live, source, values, sems):
-    groups = live[0, 0] >> 3
-
-    def load(g):
-        part = pl.ds(pl.multiple_of(g * GROUP, GROUP), GROUP)
-        return pltpu.make_async_copy(source.at[part], values.at[part], sems.at[g])
-
-    def start(g, carry):
-        load(g).start()
-        return carry
-
-    lax.fori_loop(0, groups, start, 0)
-    return groups, load
-
-
-def forward_kernel(col_slots, me, slots, live, row_need, need, source, column, *refs):
-    peers, (out, values, arrived, acc, held, sems, out_sems) = refs[: NX - 1], refs[NX - 1 :]
-    n, _, width = out.shape
+def plan_kernel(col_slots, me, slots, live, plan):
+    mine = me[0, 0] & (NX - 1)
+    shift = col_slots.bit_length() - 1
+    spare = plan.shape[1] - 1
+
+    def scan(b, counts):
+        slot = slots[0, b]
+        col = slot & (col_slots - 1)
+        piece = (mine - (col >> 1)) & (NX - 1)
+        late = (piece == NX // 2).astype(jnp.int32)
+        count = jnp.where(late == 1, counts[1], counts[0])
+        place = ((piece - (piece >> 1)) * (1 - late)) * (col_slots // NX)
+        feat = place + ((col >> 3) << 1) + (col & 1)
+        plan[3 * late, count] = b
+        plan[3 * late + 1, count] = feat
+        plan[3 * late + 2, count] = slot >> shift
+        return counts[0] + 1 - late, counts[1] + late
+
+    zero = jnp.int32(0)
+    counts = lax.fori_loop(0, live[0, 0], scan, (zero, zero))
+    for part in range(2):
+        for u in range(GROUP):
+            plan[3 * part, counts[part] + u] = 0
+            plan[3 * part + 1, counts[part] + u] = 0
+            plan[3 * part + 2, counts[part] + u] = ROWS
+        plan[3 * part, spare] = (counts[part] + GROUP - 1) >> 3
+
+
+def accumulate(plan, first, groups, ready, values, feats, acc):
+    def group(g, carry):
+        ready(g)
+        for start in range(0, GROUP, BATCH):
+            terms = []
+            for u in range(start, start + BATCH):
+                b = g * GROUP + u
+                term = jnp.dot(
+                    values[b], feats[plan[first + 1, b]], preferred_element_type=F32
+                )
+                terms.append((plan[first + 2, b], term))
+            for row, term in terms:
+                acc[row] += term
+        return carry
+
+    lax.fori_loop(0, groups, group, 0)
+
+
+def early_kernel(
+    me, plan, need, source, column, near, far, acc, late, values, arrived, sems, late_sems
+):
     blk = values.shape[1]
     mine = me[0, 0] & (NX - 1)
-    shift = col_slots.bit_length() - 1
-    groups, load = load_groups(live, source, values, sems)
+    spare = plan.shape[1] - 1
+    groups, late_groups = plan[0, spare], plan[3, spare]
+
+    def starter(first, target, sem):
+        def start(g, carry):
+            for u in range(GROUP):
+                b = g * GROUP + u
+                pltpu.make_async_copy(source.at[plan[first, b]], target.at[b], sem.at[g]).start()
+            return carry
+
+        return start
+
+    def waiter(target, sem):
+        def wait(g):
+            part = pl.ds(pl.multiple_of(g * GROUP, GROUP), GROUP)
+            pltpu.make_async_copy(source.at[pl.ds(0, GROUP)], target.at[part], sem.at[g]).wait()
+
+        return wait
+
+    lax.fori_loop(0, groups, starter(0, values, sems), 0)
+    lax.fori_loop(0, late_groups, starter(3, late, late_sems), 0)
     acc[...] = jnp.zeros_like(acc)
+    count = near.shape[0]
 
     def place(y, carry):
         for k in range(2):
             start = pl.multiple_of(need[0, 2 * (NX * y + mine) + k] * blk, blk)
-            arrived[0, 2 * y + k] = column[y, pl.ds(start, blk), :]
-            for d in range(NX - 1):
-                arrived[d + 1, 2 * y + k] = peers[d][2 * y + k]
+            arrived[2 * y + k] = column[y, pl.ds(start, blk), :]
+            arrived[count + 2 * y + k] = near[2 * y + k]
+            arrived[2 * count + 2 * y + k] = far[2 * y + k]
         return carry
 
     lax.fori_loop(0, column.shape[0], place, 0)
-
-    def group(g, carry):
-        load(g).wait()
-        for first in range(0, GROUP, BATCH):
-            terms = []
-            for u in range(first, first + BATCH):
-                b = g * GROUP + u
-                slot = slots[0, b]
-                col = slot & (col_slots - 1)
-                piece = (mine - (col >> 1)) & (NX - 1)
-                feats = arrived[piece, ((col >> 3) << 1) + (col & 1)]
-                term = jnp.dot(values[b], feats, preferred_element_type=F32)
-                terms.append((slot >> shift, term))
-            for row, term in terms:
-                acc[row] += term
-        return carry
-
-    lax.fori_loop(0, groups, group, 0)
+    accumulate(plan, 0, groups, waiter(values, sems), values, arrived, acc)
+    done = waiter(late, late_sems)
+
+    def finish(g, carry):
+        done(g)
+        return carry
+
+    lax.fori_loop(0, late_groups, finish, 0)
+
+
+def late_kernel(plan, row_need, early, values, arrived, out, acc, held, out_sems):
+    n, _, width = out.shape
+    blk = values.shape[1]
+    spare = plan.shape[1] - 1
+    acc[...] = jnp.zeros_like(acc)
+    accumulate(plan, 3, plan[3, spare], lambda g: None, values, arrived, acc)
     sub = lax.broadcasted_iota(jnp.int32, (EXTRA, width), 0)
     ship = shipper(held, out, out_sems)
     for c in range(n):
         for k in range(2):
-            held[c, k * blk : (k + 1) * blk, :] = acc[2 * c + k].astype(BF16)
+            total = early[2 * c + k] + acc[2 * c + k]
+            held[c, k * blk : (k + 1) * blk, :] = total.astype(BF16)
         ids = jnp.where(sub < EXTRA // 2, row_need[c, 0], row_need[c, 1])
         held[c, 2 * blk :, :] = ids.astype(F32).astype(BF16)
         ship(c)
 
 
-def middle_kernel(
-    arrived, weight, upstream, act, out, local_term, back, held, sems
-):
+def load_groups(live, source, values, sems):
+    groups = live[0, 0] >> 3
+
+    def load(g):
+        part = pl.ds(pl.multiple_of(g * GROUP, GROUP), GROUP)
+        return pltpu.make_async_copy(source.at[part], values.at[part], sems.at[g])
+
+    def start(g, carry):
+        load(g).start()
+        return carry
+
+    lax.fori_loop(0, groups, start, 0)
+    return groups, load
+
+
+def middle_kernel(arrived, weight, upstream, act, out, local_term, back):
     n, rows, width = arrived.shape
     blk = (rows - EXTRA) // 2
     per_dev = upstream.shape[0] // blk
@@ -168,14 +234,12 @@
             grad, w, (((1,), (1,)), ((), ())), preferred_element_type=F32
         ).astype(BF16)
     local_term[...] = total
-    ship = shipper(held, out, sems)
     for c in range(n):
         for k in range(2):
             chosen = back[0]
             for q in range(1, per_dev):
                 chosen = jnp.where(ids[c][k].astype(BF16) == float(q), back[q], chosen)
-            held[c, k * blk : (k + 1) * blk, :] = chosen
-        ship(c)
+            out[c, k * blk : (k + 1) * blk, :] = chosen
 
 
 def backward_kernel(
@@ -285,25 +349,47 @@
         moved=4 << 20,
         grant=PICK_GRANT,
     )(me, *tables, column)
-    pieces = [along_x(chosen[d], d + 1) for d in range(NX - 1)]
-    pieces = [p.reshape(cap * n_y, blk, width) for p in pieces]
-    partial = call(
-        functools.partial(forward_kernel, col_slots),
-        pltpu.HBM((n_cols, cap * blk + EXTRA, width), BF16),
-        [SMEM, SMEM, SMEM, SMEM, SMEM, HBM, VMEM, *[VMEM for _ in pieces]],
+    plan = call(
+        functools.partial(plan_kernel, col_slots),
+        jax.ShapeDtypeStruct((6, slot_total + 2 * GROUP), jnp.int32),
+        [SMEM, SMEM, SMEM],
+        out_spec=SMEM,
+    )(me, slots, live_count)
+    pieces = {}
+    for d in (1, NX - 1, NX // 2):
+        piece = along_x(chosen[d - 1], d)
+        pieces[d] = piece.reshape(cap * n_y, blk, width)
+    early, late = call(
+        early_kernel,
+        (
+            jax.ShapeDtypeStruct((row_slots + 1, blk, width), F32),
+            jax.ShapeDtypeStruct(values.shape, BF16),
+        ),
+        [SMEM, SMEM, SMEM, HBM, VMEM, VMEM, VMEM],
         [
             pltpu.VMEM(values.shape, BF16),
-            pltpu.VMEM((NX, cap * n_y, blk, width), BF16),
-            pltpu.VMEM((row_slots, blk, width), F32),
-            pltpu.VMEM((n_cols, cap * blk + EXTRA, width), BF16),
+            pltpu.VMEM(((NX - 1) * cap * n_y, blk, width), BF16),
             pltpu.SemaphoreType.DMA((slot_total // GROUP,)),
-            pltpu.SemaphoreType.DMA((n_cols,)),
+            pltpu.SemaphoreType.DMA((slot_total // GROUP,)),
         ],
         flops=work,
         moved=8 << 20,
+        grant=FORWARD_GRANT,
+    )(me, plan, need, values, column, pieces[1], pieces[NX - 1])
+    partial = call(
+        late_kernel,
+        pltpu.HBM((n_cols, cap * blk + EXTRA, width), BF16),
+        [SMEM, SMEM, VMEM, VMEM, VMEM],
+        [
+            pltpu.VMEM((row_slots + 1, blk, width), F32),
+            pltpu.VMEM((n_cols, cap * blk + EXTRA, width), BF16),
+            pltpu.SemaphoreType.DMA((PARTS,)),
+        ],
+        flops=work // 4,
+        moved=8 << 20,
         out_spec=HBM,
         grant=FORWARD_GRANT,
-    )(me, slots, live_count, row_need[0, 0], need, values, column, *pieces)
+    )(plan, row_need[0, 0], early, late, pieces[NX // 2])
     asked = jnp.concatenate([need, *tables], axis=0)
     bit = 1
     while bit < n_y:
@@ -319,12 +405,7 @@
             jax.ShapeDtypeStruct((width, width), F32),
         ),
         [VMEM, VMEM, VMEM],
-        [
-            pltpu.VMEM((per_dev, blk, width), BF16),
-            pltpu.VMEM((n_cols, cap * blk, width), BF16),
-            pltpu.SemaphoreType.DMA((n_cols,)),
-        ],
-        out_spec=(VMEM, HBM, VMEM),
+        [pltpu.VMEM((per_dev, blk, width), BF16)],
         flops=work // 8,
         moved=4 << 20,
     )(partial, weight, out_grad[0, 0])
@@ -362,7 +443,7 @@
             pltpu.VMEM((col_slots, blk, width), F32),
             pltpu.VMEM((n_rows, cap * blk, width), BF16),
             pltpu.SemaphoreType.DMA((slot_total // GROUP,)),
-            pltpu.SemaphoreType.DMA((n_rows,)),
+            pltpu.SemaphoreType.DMA((PARTS,)),
         ],
         flops=work,
         moved=8 << 20,

time: 291 us -> 290 us (level)
  waiting for transfers between devices: 112 us -> 99.4 us
  starting transfers between devices: 81.1 us -> 87.4 us
  Pallas kernels: 23.5 us -> 28.1 us
    ppermute x6, waiting for transfers between devices: 23.1 us -> 9.6 us  [along_x(): return lax.ppermute(array, 'gr', pairs)]
    all_to_all x1, starting transfers between devices: 4.97 us -> 12.6 us  [swap(): return lax.all_to_all(array, axis, split_axis=0, concat_axis=0, tiled=True)]
    pallas_call x1 -> x3, Pallas kernels: 6.7 us -> 12.1 us  [the longest x1 4.83 us: on_device(): call(early_kernel, (jax.ShapeDtypeStruct((row_slots + 1, blk, width), F32...]
  transfers between devices with their start and end apart: 22 -> 22, of which waited for: 18 -> 18; matrix products, arithmetic and copies ran while one was open for 0% -> 0% of each run, Pallas kernels for 0% -> 3%
where the time goes in v5:
time: 290 us; the launch traced here: 289 us
  waiting for transfers between devices  99.4 us (34%)
  starting transfers between devices  87.4 us (30%)
  blocking collectives  71.5 us (25%)
  Pallas kernels  28.1 us (10%)
    ppermute x14, waiting for transfers between devices, trade(): return lax.ppermute(array, axis, pairs)  73.9 us
    all_to_all x2, blocking collectives, swap(): return lax.all_to_all(array, axis, split_axis=0, concat_axis=0, tiled=True)  71.5 us
    ppermute x14, starting transfers between devices, trade(): return lax.ppermute(array, axis, pairs)  47.5 us
    ppermute x6, starting transfers between devices, along_x(): return lax.ppermute(array, 'gr', pairs)  20.1 us
    all_to_all x1, waiting for transfers between devices, on_device(): lax.all_to_all(copies, 'gr', split_axis=0, concat_axis=0, tiled=True, axi...  16 us
    all_to_all x1, starting transfers between devices, swap(): return lax.all_to_all(array, axis, split_axis=0, concat_axis=0, tiled=True)  12.6 us
    ppermute x6, waiting for transfers between devices, along_x(): return lax.ppermute(array, 'gr', pairs)  9.6 us
    pallas_call x1, Pallas kernels, on_device(): call(functools.partial(backward_kernel, col_slots), pltpu.HBM((n_rows, ca...  7.53 us
  transfers between devices with their start and end apart: 22, of which 18 were waited for; matrix products, arithmetic and copies ran while one was open for 0% of the time, Pallas kernels for 3%

profile of v5, /device:TPU:4, one launch (start us, length us, event | category | flops | bytes accessed | tf_op | source)
XLA Modules:
  0.0 289.1 jit_solution(8191037819114950713)
XLA Ops:
  2.6 7.1 %all-to-all-start = ((bf16[8,512,128]{2,1,0:T(8,128)(2,1)}), bf16[8,512,128]{2,1,0:T(8,128)(2,1)S(1)}, u32[]{:S(2)}, u32[]{:S(2)}) async-start(bf16[8,512,128]{2,1,0:T(8,128)(2,1)} %shard_map.104), calls=%async_computation | async-start | bytes 2097152 | tf_op jit(solution)/shard_map/all_to_all | solution.py:335
  12.4 4.6 %collective-permute-start.1 = (s32[1,128]{1,0:T(1,128)S(1)}, s32[1,128]{1,0:T(1,128)S(1)}, u32[]{:S(2)}, u32[]{:S(2)}) collective-permute-start(s32[1,128]{1,0:T(1,128)S(1)} %pad.4.need), channel_id=1, source_target_pairs={{0,32},{16,48},{32,0},{48,16},{64,96},{80,112},{96,64},{112,80},{1... | collective-permute-start | bytes 1544 | tf_op jit(solution)/shard_map/ppermute | solution.py:324
  17.1 3.6 %collective-permute-start.2 = (s32[1,128]{1,0:T(1,128)S(1)}, s32[1,128]{1,0:T(1,128)S(1)}, u32[]{:S(2)}, u32[]{:S(2)}) collective-permute-start(s32[1,128]{1,0:T(1,128)S(1)} %pad.4.need), channel_id=1, source_target_pairs={{0,16},{16,32},{32,48},{48,0},{64,80},{80,96},{96,112},{112,64},{1... | collective-permute-start | bytes 1544 | tf_op jit(solution)/shard_map/ppermute | solution.py:324
  22.5 16.0 %all-to-all-done.refs_3_.column = bf16[8,512,128]{2,1,0:T(8,128)(2,1)S(1)} async-done(((bf16[8,512,128]{2,1,0:T(8,128)(2,1)}), bf16[8,512,128]{2,1,0:T(8,128)(2,1)S(1)}, u32[]{:S(2)}, u32[]{:S(2)}) %all-to-all-start) | async-done | bytes 1048608 | tf_op jit(solution)/shard_map/all_to_all | solution.py:335
  40.2 3.1 %collective-permute-start.3 = (bf16[8,256,128]{2,1,0:T(8,128)(2,1)}, bf16[8,256,128]{2,1,0:T(8,128)(2,1)S(1)}, u32[]{:S(2)}, u32[]{:S(2)}) collective-permute-start(bf16[8,256,128]{2,1,0:T(8,128)(2,1)} %get-tuple-element.11), channel_id=1, source_target_pairs={{0,16},{16,32},{32,48},{48,0},{64,80},{80,96},{96,112},{112,64},{1... | collective-permute-start | bytes 1572872 | tf_op jit(solution)/shard_map/ppermute | solution.py:324
  46.0 3.6 %collective-permute-start.5 = (bf16[8,256,128]{2,1,0:T(8,128)(2,1)S(1)}, bf16[8,256,128]{2,1,0:T(8,128)(2,1)S(1)}, u32[]{:S(2)}, u32[]{:S(2)}) collective-permute-start(bf16[8,256,128]{2,1,0:T(8,128)(2,1)S(1)} %get-tuple-element.15), channel_id=1, source_target_pairs={{0,32},{16,48},{32,0},{48,16},{64,96},{80,112},{96,64},{112,80},{1... | collective-permute-start | bytes 1572872 | tf_op jit(solution)/shard_map/ppermute | solution.py:324
  50.4 4.3 %shard_map.103.plan = s32[6,144]{1,0:T(8,128)S(1)} custom-call(s32[1,1]{1,0:T(1,128)} %bitcast.me, s32[1,128]{1,0:T(1,128)S(1)} %bitcast.19, s32[1,1]{1,0:T(1,128)S(6)} %copy.15.live), custom_call_target="tpu_custom_call" | custom-call | tf_op jit(solution)/shard_map/pallas_call | solution.py:352
  57.1 3.1 %collective-permute-done.4 = bf16[8,256,128]{2,1,0:T(8,128)(2,1)S(1)} collective-permute-done((bf16[8,256,128]{2,1,0:T(8,128)(2,1)}, bf16[8,256,128]{2,1,0:T(8,128)(2,1)S(1)}, u32[]{:S(2)}, u32[]{:S(2)}) %collective-permute-start.4) | collective-permute-done | bytes 524320 | tf_op jit(solution)/shard_map/ppermute | solution.py:324
  60.2 4.8 %shard_map.106 = (f32[33,128,128]{2,1,0:T(8,128)S(1)}, bf16[128,128,128]{2,1,0:T(8,128)(2,1)S(1)}) custom-call(s32[1,1]{1,0:T(1,128)} %bitcast.me, s32[6,144]{1,0:T(8,128)S(1)} %shard_map.103.plan, s32[1,128]{1,0:T(1,128)S(1)} %pad.4.need, bf16[128,128,128]{2,1,0:T(8,128)(2,1)} %bitcast.21, bf16[8,512,128]{2,1,0:T(8,128)(2,1)S(1)} %all-to-all-done.refs_3_.column, ...), custom_call_target="tpu_custom_call" | custom-call | flops 536870912 | bytes 8388608 | tf_op jit(solution)/shard_map/pallas_call | solution.py:362
  67.3 3.0 %shard_map.107 = bf16[16,272,128]{2,1,0:T(8,128)(2,1)} custom-call(s32[6,144]{1,0:T(8,128)S(1)} %shard_map.103.plan, s32[16,2]{1,0:T(8,128)S(1)} %copy.14.row_need, f32[33,128,128]{2,1,0:T(8,128)S(1)} %get-tuple-element.13.early, bf16[128,128,128]{2,1,0:T(8,128)(2,1)S(1)} %get-tuple-element.14.values, bf16[16,128,128]{2,1,0:T(8,128)(2,1)S(1)} %bitcast.17), custom_call_target="tpu_custom_call" | custom-call | flops 134217728 | bytes 8388608 | tf_op jit(solution)/shard_map/pallas_call | solution.py:379
  70.3 40.7 %all_to_all.20.arrived = bf16[16,272,128]{2,1,0:T(8,128)(2,1)S(1)} all-to-all(bf16[16,272,128]{2,1,0:T(8,128)(2,1)} %shard_map.107), channel_id=1, replica_groups=mesh['gr'=32,'gc'=16] {'gc'}, dimensions={0} | all-to-all | bytes 2228224 | tf_op jit(solution)/shard_map/all_to_all | solution.py:310
  113.8 30.8 %all_to_all.21 = bf16[16,256,128]{2,1,0:T(8,128)(2,1)S(1)} all-to-all(bf16[16,256,128]{2,1,0:T(8,128)(2,1)} %get-tuple-element.18), channel_id=1, replica_groups=mesh['gr'=32,'gc'=16] {'gc'}, dimensions={0} | all-to-all | bytes 2097152 | tf_op jit(solution)/shard_map/all_to_all | solution.py:310
  144.5 7.5 %shard_map.109 = bf16[32,256,128]{2,1,0:T(8,128)(2,1)} custom-call(s32[1,128]{1,0:T(1,128)S(1)} %bitcast.20, s32[1,1]{1,0:T(1,128)S(6)} %copy.15.live, bf16[128,128,128]{2,1,0:T(8,128)(2,1)} %bitcast.22, bf16[32,128,128]{2,1,0:T(8,128)(2,1)S(1)} %bitcast.14), custom_call_target="tpu_custom_call" | custom-call | flops 536870912 | bytes 8388608 | tf_op jit(solution)/shard_map/pallas_call | solution.py:437
  152.1 12.6 %all-to-all-start.3 = ((bf16[32,256,128]{2,1,0:T(8,128)(2,1)}), bf16[32,256,128]{2,1,0:T(8,128)(2,1)S(1)}, u32[]{:S(2)}, u32[]{:S(2)}) async-start(bf16[32,256,128]{2,1,0:T(8,128)(2,1)} %shard_map.109), calls=%async_computation.3 | async-start | bytes 4194304 | tf_op jit(solution)/shard_map/all_to_all | solution.py:310
  164.7 3.1 %collective-permute-start.6 = (f32[64,128]{1,0:T(8,128)S(1)}, f32[64,128]{1,0:T(8,128)S(1)}, u32[]{:S(2)}, u32[]{:S(2)}) collective-permute-start(f32[64,128]{1,0:T(8,128)S(1)} %slice_select_fusion), channel_id=1, source_target_pairs={{0,16},{16,0},{32,48},{48,32},{64,80},{80,64},{96,112},{112,96},{1... | collective-permute-start | bytes 98312 | tf_op jit(solution)/shard_map/ppermute | solution.py:314
  173.6 4.4 %collective-permute-done.7 = f32[32,128]{1,0:T(8,128)S(1)} collective-permute-done((f32[32,128]{1,0:T(8,128)S(1)}, f32[32,128]{1,0:T(8,128)S(1)}, u32[]{:S(2)}, u32[]{:S(2)}) %collective-permute-start.7) | collective-permute-done | bytes 16416 | tf_op jit(solution)/shard_map/ppermute | solution.py:314
  178.0 4.8 %collective-permute-start.8 = (f32[32,128]{1,0:T(8,128)S(1)}, f32[32,128]{1,0:T(8,128)S(1)}, u32[]{:S(2)}, u32[]{:S(2)}) collective-permute-start(f32[32,128]{1,0:T(8,128)S(1)} %select_add_fusion.1), channel_id=1, source_target_pairs={{0,64},{16,80},{32,96},{48,112},{64,0},{80,16},{96,32},{112,48},{1... | collective-permute-start | bytes 49160 | tf_op jit(solution)/shard_map/ppermute | solution.py:314
  182.8 29.7 %collective-permute-done.8 = f32[32,128]{1,0:T(8,128)S(1)} collective-permute-done((f32[32,128]{1,0:T(8,128)S(1)}, f32[32,128]{1,0:T(8,128)S(1)}, u32[]{:S(2)}, u32[]{:S(2)}) %collective-permute-start.8) | collective-permute-done | bytes 16416 | tf_op jit(solution)/shard_map/ppermute | solution.py:314
  212.6 4.2 %collective-permute-start.9 = (f32[32,128]{1,0:T(8,128)S(1)}, f32[32,128]{1,0:T(8,128)S(1)}, u32[]{:S(2)}, u32[]{:S(2)}) collective-permute-start(f32[32,128]{1,0:T(8,128)S(1)} %add.31), channel_id=1, source_target_pairs={{0,128},{16,144},{32,160},{48,176},{64,192},{80,208},{96,224},{112... | collective-permute-start | bytes 49160 | tf_op jit(solution)/shard_map/ppermute | solution.py:314
  219.2 6.0 %collective-permute-start.10 = (f32[32,128]{1,0:T(8,128)S(1)}, f32[32,128]{1,0:T(8,128)S(1)}, u32[]{:S(2)}, u32[]{:S(2)}) collective-permute-start(f32[32,128]{1,0:T(8,128)S(1)} %add.32), channel_id=1, source_target_pairs={{0,256},{16,272},{32,288},{48,304},{64,320},{80,336},{96,352},{112... | collective-permute-start | bytes 49160 | tf_op jit(solution)/shard_map/ppermute | solution.py:314
  225.2 3.5 %collective-permute-done.10 = f32[32,128]{1,0:T(8,128)S(1)} collective-permute-done((f32[32,128]{1,0:T(8,128)S(1)}, f32[32,128]{1,0:T(8,128)S(1)}, u32[]{:S(2)}, u32[]{:S(2)}) %collective-permute-start.10) | collective-permute-done | bytes 16416 | tf_op jit(solution)/shard_map/ppermute | solution.py:314
  233.7 3.7 %collective-permute-done.12 = f32[32,128]{1,0:T(8,128)S(1)} collective-permute-done((f32[32,128]{1,0:T(8,128)S(1)}, f32[32,128]{1,0:T(8,128)S(1)}, u32[]{:S(2)}, u32[]{:S(2)}) %collective-permute-start.12) | collective-permute-done | bytes 16416 | tf_op jit(solution)/shard_map/ppermute | solution.py:314
  237.5 3.2 %collective-permute-start.13 = (f32[32,128]{1,0:T(8,128)S(1)}, f32[32,128]{1,0:T(8,128)S(1)}, u32[]{:S(2)}, u32[]{:S(2)}) collective-permute-start(f32[32,128]{1,0:T(8,128)S(1)} %add.35), channel_id=1, source_target_pairs={{0,4},{1,5},{2,6},{3,7},{4,0},{5,1},{6,2},{7,3},{8,12},{9,13},{10,... | collective-permute-start | bytes 49160 | tf_op jit(solution)/shard_map/ppermute | solution.py:314
  240.7 3.3 %collective-permute-done.13 = f32[32,128]{1,0:T(8,128)S(1)} collective-permute-done((f32[32,128]{1,0:T(8,128)S(1)}, f32[32,128]{1,0:T(8,128)S(1)}, u32[]{:S(2)}, u32[]{:S(2)}) %collective-permute-start.13) | collective-permute-done | bytes 16416 | tf_op jit(solution)/shard_map/ppermute | solution.py:314
  244.0 3.1 %collective-permute-start.14 = (f32[32,128]{1,0:T(8,128)S(1)}, f32[32,128]{1,0:T(8,128)S(1)}, u32[]{:S(2)}, u32[]{:S(2)}) collective-permute-start(f32[32,128]{1,0:T(8,128)S(1)} %add.36), channel_id=1, source_target_pairs={{0,8},{1,9},{2,10},{3,11},{4,12},{5,13},{6,14},{7,15},{8,0},{9,1},... | collective-permute-start | bytes 49160 | tf_op jit(solution)/shard_map/ppermute | solution.py:314
  247.1 6.4 %collective-permute-done.14 = f32[32,128]{1,0:T(8,128)S(1)} collective-permute-done((f32[32,128]{1,0:T(8,128)S(1)}, f32[32,128]{1,0:T(8,128)S(1)}, u32[]{:S(2)}, u32[]{:S(2)}) %collective-permute-start.14) | collective-permute-done | bytes 16416 | tf_op jit(solution)/shard_map/ppermute | solution.py:314
  256.4 4.3 %collective-permute-done.15 = f32[32,128]{1,0:T(8,128)S(1)} collective-permute-done((f32[32,128]{1,0:T(8,128)S(1)}, f32[32,128]{1,0:T(8,128)S(1)}, u32[]{:S(2)}, u32[]{:S(2)}) %collective-permute-start.15) | collective-permute-done | bytes 16416 | tf_op jit(solution)/shard_map/ppermute | solution.py:314
  260.7 4.4 %collective-permute-start.16 = (f32[64,128]{1,0:T(8,128)S(1)}, f32[64,128]{1,0:T(8,128)S(1)}, u32[]{:S(2)}, u32[]{:S(2)}) collective-permute-start(f32[64,128]{1,0:T(8,128)S(1)} %pad_maximum_fusion), channel_id=1, source_target_pairs={{0,16},{16,0},{32,48},{48,32},{64,80},{80,64},{96,112},{112,96},{1... | collective-permute-start | bytes 98312 | tf_op jit(solution)/shard_map/ppermute | solution.py:314
  267.0 3.6 %collective-permute-done.17 = s32[4,128]{1,0:T(4,128)S(1)} collective-permute-done((s32[4,128]{1,0:T(4,128)S(1)}, s32[4,128]{1,0:T(4,128)S(1)}, u32[]{:S(2)}, u32[]{:S(2)}) %collective-permute-start.17) | collective-permute-done | bytes 2080 | tf_op jit(solution)/shard_map/ppermute | solution.py:314
  272.6 4.3 %collective-permute-done.18 = s32[8,128]{1,0:T(8,128)S(1)} collective-permute-done((s32[8,128]{1,0:T(8,128)S(1)}, s32[8,128]{1,0:T(8,128)S(1)}, u32[]{:S(2)}, u32[]{:S(2)}) %collective-permute-start.18) | collective-permute-done | bytes 4128 | tf_op jit(solution)/shard_map/ppermute | solution.py:314
  277.0 5.4 %collective-permute-start.19 = (s32[16,128]{1,0:T(8,128)S(1)}, s32[16,128]{1,0:T(8,128)S(1)}, u32[]{:S(2)}, u32[]{:S(2)}) collective-permute-start(s32[16,128]{1,0:T(8,128)S(1)} %concatenate.25), channel_id=1, source_target_pairs={{0,256},{16,272},{32,288},{48,304},{64,320},{80,336},{96,352},{112... | collective-permute-start | bytes 24584 | tf_op jit(solution)/shard_map/ppermute | solution.py:314
  282.3 4.1 %collective-permute-done.19 = s32[16,128]{1,0:T(8,128)S(1)} collective-permute-done((s32[16,128]{1,0:T(8,128)S(1)}, s32[16,128]{1,0:T(8,128)S(1)}, u32[]{:S(2)}, u32[]{:S(2)}) %collective-permute-start.19) | collective-permute-done | bytes 8224 | tf_op jit(solution)/shard_map/ppermute | solution.py:314
  (55 shorter events, 41.2 us)
Async XLA Ops:
  0.6 9.1 %copy-start.3 = (s32[1,1,32,2]{2,3,1,0:T(2,128)S(1)}, s32[1,1,32,2]{2,3,1,0:T(2,128)}, u32[]{:S(2)}) copy-start(s32[1,1,32,2]{2,3,1,0:T(2,128)} %param.15) | copy-start | bytes 772
  0.6 49.7 %copy-start.4 = (s32[1,1,16,2]{2,3,1,0:T(2,128)S(1)}, s32[1,1,16,2]{2,3,1,0:T(2,128)}, u32[]{:S(2)}) copy-start(s32[1,1,16,2]{2,3,1,0:T(2,128)} %param.14) | copy-start | bytes 388
  0.7 49.7 %copy-start.2 = (s32[1,1,128]{2,1,0:T(1,128)S(1)}, s32[1,1,128]{2,1,0:T(1,128)}, u32[]{:S(2)}) copy-start(s32[1,1,128]{2,1,0:T(1,128)} %param.12) | copy-start | bytes 1540
  2.6 35.8 %all-to-all-start = ((bf16[8,512,128]{2,1,0:T(8,128)(2,1)}), bf16[8,512,128]{2,1,0:T(8,128)(2,1)S(1)}, u32[]{:S(2)}, u32[]{:S(2)}) async-start(bf16[8,512,128]{2,1,0:T(8,128)(2,1)} %shard_map.104), calls=%async_computation | async-start | bytes 2097152 | tf_op jit(solution)/shard_map/all_to_all | solution.py:335
  10.0 10.7 %collective-permute-start = (s32[1,128]{1,0:T(1,128)S(1)}, s32[1,128]{1,0:T(1,128)S(1)}, u32[]{:S(2)}, u32[]{:S(2)}) collective-permute-start(s32[1,128]{1,0:T(1,128)S(1)} %pad.4.need), channel_id=1, source_target_pairs={{0,48},{16,0},{32,16},{48,32},{64,112},{80,64},{96,80},{112,96},{1... | collective-permute-start | bytes 1544 | tf_op jit(solution)/shard_map/ppermute | solution.py:324
  12.4 8.3 %collective-permute-start.1 = (s32[1,128]{1,0:T(1,128)S(1)}, s32[1,128]{1,0:T(1,128)S(1)}, u32[]{:S(2)}, u32[]{:S(2)}) collective-permute-start(s32[1,128]{1,0:T(1,128)S(1)} %pad.4.need), channel_id=1, source_target_pairs={{0,32},{16,48},{32,0},{48,16},{64,96},{80,112},{96,64},{112,80},{1... | collective-permute-start | bytes 1544 | tf_op jit(solution)/shard_map/ppermute | solution.py:324
  17.1 5.5 %collective-permute-start.2 = (s32[1,128]{1,0:T(1,128)S(1)}, s32[1,128]{1,0:T(1,128)S(1)}, u32[]{:S(2)}, u32[]{:S(2)}) collective-permute-start(s32[1,128]{1,0:T(1,128)S(1)} %pad.4.need), channel_id=1, source_target_pairs={{0,16},{16,32},{32,48},{48,0},{64,80},{80,96},{96,112},{112,64},{1... | collective-permute-start | bytes 1544 | tf_op jit(solution)/shard_map/ppermute | solution.py:324
  40.2 16.9 %collective-permute-start.3 = (bf16[8,256,128]{2,1,0:T(8,128)(2,1)}, bf16[8,256,128]{2,1,0:T(8,128)(2,1)S(1)}, u32[]{:S(2)}, u32[]{:S(2)}) collective-permute-start(bf16[8,256,128]{2,1,0:T(8,128)(2,1)} %get-tuple-element.11), channel_id=1, source_target_pairs={{0,16},{16,32},{32,48},{48,0},{64,80},{80,96},{96,112},{112,64},{1... | collective-permute-start | bytes 1572872 | tf_op jit(solution)/shard_map/ppermute | solution.py:324
  43.3 16.9 %collective-permute-start.4 = (bf16[8,256,128]{2,1,0:T(8,128)(2,1)}, bf16[8,256,128]{2,1,0:T(8,128)(2,1)S(1)}, u32[]{:S(2)}, u32[]{:S(2)}) collective-permute-start(bf16[8,256,128]{2,1,0:T(8,128)(2,1)} %get-tuple-element.12), channel_id=1, source_target_pairs={{0,48},{16,0},{32,16},{48,32},{64,112},{80,64},{96,80},{112,96},{1... | collective-permute-start | bytes 1572872 | tf_op jit(solution)/shard_map/ppermute | solution.py:324
  46.0 21.3 %collective-permute-start.5 = (bf16[8,256,128]{2,1,0:T(8,128)(2,1)S(1)}, bf16[8,256,128]{2,1,0:T(8,128)(2,1)S(1)}, u32[]{:S(2)}, u32[]{:S(2)}) collective-permute-start(bf16[8,256,128]{2,1,0:T(8,128)(2,1)S(1)} %get-tuple-element.15), channel_id=1, source_target_pairs={{0,32},{16,48},{32,0},{48,16},{64,96},{80,112},{96,64},{112,80},{1... | collective-permute-start | bytes 1572872 | tf_op jit(solution)/shard_map/ppermute | solution.py:324
  70.3 40.7 %copy-start = (bf16[1,1,512,128]{3,2,1,0:T(8,128)(2,1)S(1)}, bf16[1,1,512,128]{3,2,1,0:T(8,128)(2,1)}, u32[]{:S(2)}) copy-start(bf16[1,1,512,128]{3,2,1,0:T(8,128)(2,1)} %param.9) | copy-start | bytes 393220
  70.3 40.7 %copy-start.1 = (bf16[128,128]{1,0:T(8,128)(2,1)S(1)}, bf16[128,128]{1,0:T(8,128)(2,1)}, u32[]{:S(2)}) copy-start(bf16[128,128]{1,0:T(8,128)(2,1)} %weight.1) | copy-start | bytes 98308
  152.1 135.0 %all-to-all-start.3 = ((bf16[32,256,128]{2,1,0:T(8,128)(2,1)}), bf16[32,256,128]{2,1,0:T(8,128)(2,1)S(1)}, u32[]{:S(2)}, u32[]{:S(2)}) async-start(bf16[32,256,128]{2,1,0:T(8,128)(2,1)} %shard_map.109), calls=%async_computation.3 | async-start | bytes 4194304 | tf_op jit(solution)/shard_map/all_to_all | solution.py:310
  164.7 6.1 %collective-permute-start.6 = (f32[64,128]{1,0:T(8,128)S(1)}, f32[64,128]{1,0:T(8,128)S(1)}, u32[]{:S(2)}, u32[]{:S(2)}) collective-permute-start(f32[64,128]{1,0:T(8,128)S(1)} %slice_select_fusion), channel_id=1, source_target_pairs={{0,16},{16,0},{32,48},{48,32},{64,80},{80,64},{96,112},{112,96},{1... | collective-permute-start | bytes 98312 | tf_op jit(solution)/shard_map/ppermute | solution.py:314
  170.8 7.2 %collective-permute-start.7 = (f32[32,128]{1,0:T(8,128)S(1)}, f32[32,128]{1,0:T(8,128)S(1)}, u32[]{:S(2)}, u32[]{:S(2)}) collective-permute-start(f32[32,128]{1,0:T(8,128)S(1)} %slice_select_fusion.1), channel_id=1, source_target_pairs={{0,32},{16,48},{32,0},{48,16},{64,96},{80,112},{96,64},{112,80},{1... | collective-permute-start | bytes 49160 | tf_op jit(solution)/shard_map/ppermute | solution.py:314
  178.0 34.5 %collective-permute-start.8 = (f32[32,128]{1,0:T(8,128)S(1)}, f32[32,128]{1,0:T(8,128)S(1)}, u32[]{:S(2)}, u32[]{:S(2)}) collective-permute-start(f32[32,128]{1,0:T(8,128)S(1)} %select_add_fusion.1), channel_id=1, source_target_pairs={{0,64},{16,80},{32,96},{48,112},{64,0},{80,16},{96,32},{112,48},{1... | collective-permute-start | bytes 49160 | tf_op jit(solution)/shard_map/ppermute | solution.py:314
  212.6 6.7 %collective-permute-start.9 = (f32[32,128]{1,0:T(8,128)S(1)}, f32[32,128]{1,0:T(8,128)S(1)}, u32[]{:S(2)}, u32[]{:S(2)}) collective-permute-start(f32[32,128]{1,0:T(8,128)S(1)} %add.31), channel_id=1, source_target_pairs={{0,128},{16,144},{32,160},{48,176},{64,192},{80,208},{96,224},{112... | collective-permute-start | bytes 49160 | tf_op jit(solution)/shard_map/ppermute | solution.py:314
  219.2 9.5 %collective-permute-start.10 = (f32[32,128]{1,0:T(8,128)S(1)}, f32[32,128]{1,0:T(8,128)S(1)}, u32[]{:S(2)}, u32[]{:S(2)}) collective-permute-start(f32[32,128]{1,0:T(8,128)S(1)} %add.32), channel_id=1, source_target_pairs={{0,256},{16,272},{32,288},{48,304},{64,320},{80,336},{96,352},{112... | collective-permute-start | bytes 49160 | tf_op jit(solution)/shard_map/ppermute | solution.py:314
  228.8 3.1 %collective-permute-start.11 = (f32[32,128]{1,0:T(8,128)S(1)}, f32[32,128]{1,0:T(8,128)S(1)}, u32[]{:S(2)}, u32[]{:S(2)}) collective-permute-start(f32[32,128]{1,0:T(8,128)S(1)} %add.33), channel_id=1, source_target_pairs={{0,1},{1,0},{2,3},{3,2},{4,5},{5,4},{6,7},{7,6},{8,9},{9,8},{10,11... | collective-permute-start | bytes 49160 | tf_op jit(solution)/shard_map/ppermute | solution.py:314
  231.8 5.6 %collective-permute-start.12 = (f32[32,128]{1,0:T(8,128)S(1)}, f32[32,128]{1,0:T(8,128)S(1)}, u32[]{:S(2)}, u32[]{:S(2)}) collective-permute-start(f32[32,128]{1,0:T(8,128)S(1)} %add.34), channel_id=1, source_target_pairs={{0,2},{1,3},{2,0},{3,1},{4,6},{5,7},{6,4},{7,5},{8,10},{9,11},{10,... | collective-permute-start | bytes 49160 | tf_op jit(solution)/shard_map/ppermute | solution.py:314
  237.5 6.5 %collective-permute-start.13 = (f32[32,128]{1,0:T(8,128)S(1)}, f32[32,128]{1,0:T(8,128)S(1)}, u32[]{:S(2)}, u32[]{:S(2)}) collective-permute-start(f32[32,128]{1,0:T(8,128)S(1)} %add.35), channel_id=1, source_target_pairs={{0,4},{1,5},{2,6},{3,7},{4,0},{5,1},{6,2},{7,3},{8,12},{9,13},{10,... | collective-permute-start | bytes 49160 | tf_op jit(solution)/shard_map/ppermute | solution.py:314
  244.0 9.5 %collective-permute-start.14 = (f32[32,128]{1,0:T(8,128)S(1)}, f32[32,128]{1,0:T(8,128)S(1)}, u32[]{:S(2)}, u32[]{:S(2)}) collective-permute-start(f32[32,128]{1,0:T(8,128)S(1)} %add.36), channel_id=1, source_target_pairs={{0,8},{1,9},{2,10},{3,11},{4,12},{5,13},{6,14},{7,15},{8,0},{9,1},... | collective-permute-start | bytes 49160 | tf_op jit(solution)/shard_map/ppermute | solution.py:314
  253.5 7.1 %collective-permute-start.15 = (f32[32,128]{1,0:T(8,128)S(1)}, f32[32,128]{1,0:T(8,128)S(1)}, u32[]{:S(2)}, u32[]{:S(2)}) collective-permute-start(f32[32,128]{1,0:T(8,128)S(1)} %add.37), channel_id=1, source_target_pairs={{0,32},{16,48},{32,0},{48,16},{64,96},{80,112},{96,64},{112,80},{1... | collective-permute-start | bytes 49160 | tf_op jit(solution)/shard_map/ppermute | solution.py:314
  260.7 25.8 %collective-permute-start.16 = (f32[64,128]{1,0:T(8,128)S(1)}, f32[64,128]{1,0:T(8,128)S(1)}, u32[]{:S(2)}, u32[]{:S(2)}) collective-permute-start(f32[64,128]{1,0:T(8,128)S(1)} %pad_maximum_fusion), channel_id=1, source_target_pairs={{0,16},{16,0},{32,48},{48,32},{64,80},{80,64},{96,112},{112,96},{1... | collective-permute-start | bytes 98312 | tf_op jit(solution)/shard_map/ppermute | solution.py:314
  265.1 5.5 %collective-permute-start.17 = (s32[4,128]{1,0:T(4,128)S(1)}, s32[4,128]{1,0:T(4,128)S(1)}, u32[]{:S(2)}, u32[]{:S(2)}) collective-permute-start(s32[4,128]{1,0:T(4,128)S(1)} %pad_add_fusion), channel_id=1, source_target_pairs={{0,64},{16,80},{32,96},{48,112},{64,0},{80,16},{96,32},{112,48},{1... | collective-permute-start | bytes 6152 | tf_op jit(solution)/shard_map/ppermute | solution.py:314
  270.6 6.4 %collective-permute-start.18 = (s32[8,128]{1,0:T(8,128)S(1)}, s32[8,128]{1,0:T(8,128)S(1)}, u32[]{:S(2)}, u32[]{:S(2)}) collective-permute-start(s32[8,128]{1,0:T(8,128)S(1)} %concatenate.24), channel_id=1, source_target_pairs={{0,128},{16,144},{32,160},{48,176},{64,192},{80,208},{96,224},{112... | collective-permute-start | bytes 12296 | tf_op jit(solution)/shard_map/ppermute | solution.py:314
  277.0 9.4 %collective-permute-start.19 = (s32[16,128]{1,0:T(8,128)S(1)}, s32[16,128]{1,0:T(8,128)S(1)}, u32[]{:S(2)}, u32[]{:S(2)}) collective-permute-start(s32[16,128]{1,0:T(8,128)S(1)} %concatenate.25), channel_id=1, source_target_pairs={{0,256},{16,272},{32,288},{48,304},{64,320},{80,336},{96,352},{112... | collective-permute-start | bytes 24584 | tf_op jit(solution)/shard_map/ppermute | solution.py:314

commit v6 on v5

--- a/solution.py
+++ b/solution.py
@@ -90,10 +90,9 @@
         slot = slots[0, b]
         col = slot & (col_slots - 1)
         piece = (mine - (col >> 1)) & (NX - 1)
-        late = (piece == NX // 2).astype(jnp.int32)
+        late = piece & 1
         count = jnp.where(late == 1, counts[1], counts[0])
-        place = ((piece - (piece >> 1)) * (1 - late)) * (col_slots // NX)
-        feat = place + ((col >> 3) << 1) + (col & 1)
+        feat = (piece >> 1) * (col_slots // NX) + ((col >> 3) << 1) + (col & 1)
         plan[3 * late, count] = b
         plan[3 * late + 1, count] = feat
         plan[3 * late + 2, count] = slot >> shift
@@ -128,7 +127,7 @@
 
 
 def early_kernel(
-    me, plan, need, source, column, near, far, acc, late, values, arrived, sems, late_sems
+    me, plan, need, source, column, far, acc, late, values, arrived, sems, late_sems
 ):
     blk = values.shape[1]
     mine = me[0, 0] & (NX - 1)
@@ -154,14 +153,13 @@
     lax.fori_loop(0, groups, starter(0, values, sems), 0)
     lax.fori_loop(0, late_groups, starter(3, late, late_sems), 0)
     acc[...] = jnp.zeros_like(acc)
-    count = near.shape[0]
+    count = far.shape[0]
 
     def place(y, carry):
         for k in range(2):
             start = pl.multiple_of(need[0, 2 * (NX * y + mine) + k] * blk, blk)
             arrived[2 * y + k] = column[y, pl.ds(start, blk), :]
-            arrived[count + 2 * y + k] = near[2 * y + k]
-            arrived[2 * count + 2 * y + k] = far[2 * y + k]
+            arrived[count + 2 * y + k] = far[2 * y + k]
         return carry
 
     lax.fori_loop(0, column.shape[0], place, 0)
@@ -175,11 +173,14 @@
     lax.fori_loop(0, late_groups, finish, 0)
 
 
-def late_kernel(plan, row_need, early, values, arrived, out, acc, held, out_sems):
+def late_kernel(plan, row_need, early, values, left, right, out, acc, arrived, held, out_sems):
     n, _, width = out.shape
     blk = values.shape[1]
     spare = plan.shape[1] - 1
     acc[...] = jnp.zeros_like(acc)
+    count = left.shape[0]
+    arrived[:count] = left[...]
+    arrived[count:] = right[...]
     accumulate(plan, 3, plan[3, spare], lambda g: None, values, arrived, acc)
     sub = lax.broadcasted_iota(jnp.int32, (EXTRA, width), 0)
     ship = shipper(held, out, out_sems)
@@ -356,7 +357,7 @@
         out_spec=SMEM,
     )(me, slots, live_count)
     pieces = {}
-    for d in (1, NX - 1, NX // 2):
+    for d in (2, 1, 3):
         piece = along_x(chosen[d - 1], d)
         pieces[d] = piece.reshape(cap * n_y, blk, width)
     early, late = call(
@@ -365,31 +366,32 @@
             jax.ShapeDtypeStruct((row_slots + 1, blk, width), F32),
             jax.ShapeDtypeStruct(values.shape, BF16),
         ),
-        [SMEM, SMEM, SMEM, HBM, VMEM, VMEM, VMEM],
+        [SMEM, SMEM, SMEM, HBM, VMEM, VMEM],
         [
             pltpu.VMEM(values.shape, BF16),
-            pltpu.VMEM(((NX - 1) * cap * n_y, blk, width), BF16),
+            pltpu.VMEM((2 * cap * n_y, blk, width), BF16),
             pltpu.SemaphoreType.DMA((slot_total // GROUP,)),
             pltpu.SemaphoreType.DMA((slot_total // GROUP,)),
         ],
         flops=work,
         moved=8 << 20,
         grant=FORWARD_GRANT,
-    )(me, plan, need, values, column, pieces[1], pieces[NX - 1])
+    )(me, plan, need, values, column, pieces[2])
     partial = call(
         late_kernel,
         pltpu.HBM((n_cols, cap * blk + EXTRA, width), BF16),
-        [SMEM, SMEM, VMEM, VMEM, VMEM],
+        [SMEM, SMEM, VMEM, VMEM, VMEM, VMEM],
         [
             pltpu.VMEM((row_slots + 1, blk, width), F32),
+            pltpu.VMEM((2 * cap * n_y, blk, width), BF16),
             pltpu.VMEM((n_cols, cap * blk + EXTRA, width), BF16),
             pltpu.SemaphoreType.DMA((PARTS,)),
         ],
-        flops=work // 4,
+        flops=work // 2,
         moved=8 << 20,
         out_spec=HBM,
         grant=FORWARD_GRANT,
-    )(plan, row_need[0, 0], early, late, pieces[NX // 2])
+    )(plan, row_need[0, 0], early, late, pieces[1], pieces[3])
     asked = jnp.concatenate([need, *tables], axis=0)
     bit = 1
     while bit < n_y:
@@ -411,18 +413,15 @@
     )(partial, weight, out_grad[0, 0])
     back = swap(back, "gc")
 
-    halved = []
-    bit = 1
-    while bit < n_rows:
-        if len(halved) < 2:
-            low, high = jnp.split(term, 2, axis=0)
-            top = upper("gr", bit)
-            term = jnp.where(top, high, low) + trade(jnp.where(top, low, high), "gr", bit)
-            halved.append(bit)
-        else:
-            other = trade(term, "gr", bit)
-            term = term + other
-        bit *= 2
+    halved = [1, 2]
+    for bit in halved:
+        low, high = jnp.split(term, 2, axis=0)
+        top = upper("gr", bit)
+        term = jnp.where(top, high, low) + trade(jnp.where(top, low, high), "gr", bit)
+    other = trade(term, "gr", 4)
+    term = term + other
+    others = [trade(term, "gr", bits) for bits in (8, 16, 24)]
+    term = (term + others[0]) + (others[1] + others[2])
     bit = 1
     while bit < n_cols:
         term = term + trade(term, "gc", bit)

time: 290 us -> 285 us (0.983)
  the two profiles are of different devices: /device:TPU:4 before, /device:TPU:56 now
where the time goes in v6:
time: 285 us; the launch traced here: 284 us
  waiting for transfers between devices  92.2 us (32%)
  starting transfers between devices  90.2 us (32%)
  blocking collectives  70.6 us (25%)
  Pallas kernels  28 us (10%)
    ppermute x15, waiting for transfers between devices, trade(): return lax.ppermute(array, axis, pairs)  72.8 us
    all_to_all x2, blocking collectives, swap(): return lax.all_to_all(array, axis, split_axis=0, concat_axis=0, tiled=True)  70.6 us
    ppermute x15, starting transfers between devices, trade(): return lax.ppermute(array, axis, pairs)  48.8 us
    ppermute x6, starting transfers between devices, along_x(): return lax.ppermute(array, 'gr', pairs)  19.7 us
    all_to_all x1, starting transfers between devices, swap(): return lax.all_to_all(array, axis, split_axis=0, concat_axis=0, tiled=True)  13.2 us
    all_to_all x1, waiting for transfers between devices, on_device(): lax.all_to_all(copies, 'gr', split_axis=0, concat_axis=0, tiled=True, axi...  10.4 us
    ppermute x6, waiting for transfers between devices, along_x(): return lax.ppermute(array, 'gr', pairs)  9.05 us
    all_to_all x1, starting transfers between devices, on_device(): lax.all_to_all(copies, 'gr', split_axis=0, concat_axis=0, tiled=True, axi...  8.62 us
  transfers between devices with their start and end apart: 23, of which 19 were waited for; matrix products, arithmetic and copies ran while one was open for 0% of the time, Pallas kernels for 3%

profile of v6, /device:TPU:56, one launch (start us, length us, event | category | flops | bytes accessed | tf_op | source)
XLA Modules:
  0.0 283.7 jit_solution(8186093511467856799)
XLA Ops:
  2.6 8.6 %all-to-all-start = ((bf16[8,512,128]{2,1,0:T(8,128)(2,1)}), bf16[8,512,128]{2,1,0:T(8,128)(2,1)S(1)}, u32[]{:S(2)}, u32[]{:S(2)}) async-start(bf16[8,512,128]{2,1,0:T(8,128)(2,1)} %shard_map.104), calls=%async_computation | async-start | bytes 2097152 | tf_op jit(solution)/shard_map/all_to_all | solution.py:336
  11.5 2.9 %collective-permute-start = (s32[1,128]{1,0:T(1,128)S(1)}, s32[1,128]{1,0:T(1,128)S(1)}, u32[]{:S(2)}, u32[]{:S(2)}) collective-permute-start(s32[1,128]{1,0:T(1,128)S(1)} %pad.4.need), channel_id=1, source_target_pairs={{0,48},{16,0},{32,16},{48,32},{64,112},{80,64},{96,80},{112,96},{1... | collective-permute-start | bytes 1544 | tf_op jit(solution)/shard_map/ppermute | solution.py:325
  17.1 2.8 collective-permute-start.2
  23.8 10.4 %all-to-all-done.refs_3_.column = bf16[8,512,128]{2,1,0:T(8,128)(2,1)S(1)} async-done(((bf16[8,512,128]{2,1,0:T(8,128)(2,1)}), bf16[8,512,128]{2,1,0:T(8,128)(2,1)S(1)}, u32[]{:S(2)}, u32[]{:S(2)}) %all-to-all-start) | async-done | bytes 1048608 | tf_op jit(solution)/shard_map/all_to_all | solution.py:336
  35.9 4.2 %collective-permute-start.3 = (bf16[8,256,128]{2,1,0:T(8,128)(2,1)}, bf16[8,256,128]{2,1,0:T(8,128)(2,1)S(1)}, u32[]{:S(2)}, u32[]{:S(2)}) collective-permute-start(bf16[8,256,128]{2,1,0:T(8,128)(2,1)} %get-tuple-element.11), channel_id=1, source_target_pairs={{0,32},{16,48},{32,0},{48,16},{64,96},{80,112},{96,64},{112,80},{1... | collective-permute-start | bytes 1572872 | tf_op jit(solution)/shard_map/ppermute | solution.py:325
  42.5 4.6 %collective-permute-start.5 = (bf16[8,256,128]{2,1,0:T(8,128)(2,1)S(1)}, bf16[8,256,128]{2,1,0:T(8,128)(2,1)S(1)}, u32[]{:S(2)}, u32[]{:S(2)}) collective-permute-start(bf16[8,256,128]{2,1,0:T(8,128)(2,1)S(1)} %get-tuple-element.15), channel_id=1, source_target_pairs={{0,48},{16,0},{32,16},{48,32},{64,112},{80,64},{96,80},{112,96},{1... | collective-permute-start | bytes 1572872 | tf_op jit(solution)/shard_map/ppermute | solution.py:325
  47.9 4.1 %shard_map.103.plan = s32[6,144]{1,0:T(8,128)S(1)} custom-call(s32[1,1]{1,0:T(1,128)} %bitcast.me, s32[1,128]{1,0:T(1,128)S(1)} %bitcast.19, s32[1,1]{1,0:T(1,128)S(6)} %copy.15.live), custom_call_target="tpu_custom_call" | custom-call | tf_op jit(solution)/shard_map/pallas_call | solution.py:353
  54.3 3.7 %shard_map.106 = (f32[33,128,128]{2,1,0:T(8,128)S(1)}, bf16[128,128,128]{2,1,0:T(8,128)(2,1)S(1)}) custom-call(s32[1,1]{1,0:T(1,128)} %bitcast.me, s32[6,144]{1,0:T(8,128)S(1)} %shard_map.103.plan, s32[1,128]{1,0:T(1,128)S(1)} %pad.4.need, bf16[128,128,128]{2,1,0:T(8,128)(2,1)} %bitcast.21, bf16[8,512,128]{2,1,0:T(8,128)(2,1)S(1)} %all-to-all-done.refs_3_.column, ...), custom_call_target="tpu_custom_call" | custom-call | flops 536870912 | bytes 8388608 | tf_op jit(solution)/shard_map/pallas_call | solution.py:363
  60.9 4.2 %shard_map.107 = bf16[16,272,128]{2,1,0:T(8,128)(2,1)} custom-call(s32[6,144]{1,0:T(8,128)S(1)} %shard_map.103.plan, s32[16,2]{1,0:T(8,128)S(1)} %copy.14.row_need, f32[33,128,128]{2,1,0:T(8,128)S(1)} %get-tuple-element.12.early, bf16[128,128,128]{2,1,0:T(8,128)(2,1)S(1)} %get-tuple-element.13.values, bf16[16,128,128]{2,1,0:T(8,128)(2,1)S(1)} %bitcast.15, ...), custom_call_target="tpu_custom_call" | custom-call | flops 268435456 | bytes 8388608 | tf_op jit(solution)/shard_map/pallas_call | solution.py:380
  65.1 39.8 %all_to_all.20.arrived = bf16[16,272,128]{2,1,0:T(8,128)(2,1)S(1)} all-to-all(bf16[16,272,128]{2,1,0:T(8,128)(2,1)} %shard_map.107), channel_id=1, replica_groups=mesh['gr'=32,'gc'=16] {'gc'}, dimensions={0} | all-to-all | bytes 2228224 | tf_op jit(solution)/shard_map/all_to_all | solution.py:311
  104.9 2.7 shard_map.108
  107.7 30.8 %all_to_all.21 = bf16[16,256,128]{2,1,0:T(8,128)(2,1)S(1)} all-to-all(bf16[16,256,128]{2,1,0:T(8,128)(2,1)} %get-tuple-element.18), channel_id=1, replica_groups=mesh['gr'=32,'gc'=16] {'gc'}, dimensions={0} | all-to-all | bytes 2097152 | tf_op jit(solution)/shard_map/all_to_all | solution.py:311
  138.4 7.5 %shard_map.109 = bf16[32,256,128]{2,1,0:T(8,128)(2,1)} custom-call(s32[1,128]{1,0:T(1,128)S(1)} %bitcast.20, s32[1,1]{1,0:T(1,128)S(6)} %copy.15.live, bf16[128,128,128]{2,1,0:T(8,128)(2,1)} %bitcast.22, bf16[32,128,128]{2,1,0:T(8,128)(2,1)S(1)} %bitcast.14), custom_call_target="tpu_custom_call" | custom-call | flops 536870912 | bytes 8388608 | tf_op jit(solution)/shard_map/pallas_call | solution.py:436
  146.0 13.2 %all-to-all-start.3 = ((bf16[32,256,128]{2,1,0:T(8,128)(2,1)}), bf16[32,256,128]{2,1,0:T(8,128)(2,1)S(1)}, u32[]{:S(2)}, u32[]{:S(2)}) async-start(bf16[32,256,128]{2,1,0:T(8,128)(2,1)} %shard_map.109), calls=%async_computation.3 | async-start | bytes 4194304 | tf_op jit(solution)/shard_map/all_to_all | solution.py:311
  159.2 3.4 %collective-permute-start.6 = (f32[64,128]{1,0:T(8,128)S(1)}, f32[64,128]{1,0:T(8,128)S(1)}, u32[]{:S(2)}, u32[]{:S(2)}) collective-permute-start(f32[64,128]{1,0:T(8,128)S(1)} %slice_select_fusion), channel_id=1, source_target_pairs={{0,16},{16,0},{32,48},{48,32},{64,80},{80,64},{96,112},{112,96},{1... | collective-permute-start | bytes 98312 | tf_op jit(solution)/shard_map/ppermute | solution.py:315
  162.6 5.1 %collective-permute-done.6 = f32[64,128]{1,0:T(8,128)S(1)} collective-permute-done((f32[64,128]{1,0:T(8,128)S(1)}, f32[64,128]{1,0:T(8,128)S(1)}, u32[]{:S(2)}, u32[]{:S(2)}) %collective-permute-start.6) | collective-permute-done | bytes 32800 | tf_op jit(solution)/shard_map/ppermute | solution.py:315
  167.7 2.8 collective-permute-start.7
  170.5 5.8 %collective-permute-done.7 = f32[32,128]{1,0:T(8,128)S(1)} collective-permute-done((f32[32,128]{1,0:T(8,128)S(1)}, f32[32,128]{1,0:T(8,128)S(1)}, u32[]{:S(2)}, u32[]{:S(2)}) %collective-permute-start.7) | collective-permute-done | bytes 16416 | tf_op jit(solution)/shard_map/ppermute | solution.py:315
  176.3 6.6 %collective-permute-start.8 = (f32[32,128]{1,0:T(8,128)S(1)}, f32[32,128]{1,0:T(8,128)S(1)}, u32[]{:S(2)}, u32[]{:S(2)}) collective-permute-start(f32[32,128]{1,0:T(8,128)S(1)} %select_add_fusion.1), channel_id=1, source_target_pairs={{0,64},{16,80},{32,96},{48,112},{64,0},{80,16},{96,32},{112,48},{1... | collective-permute-start | bytes 49160 | tf_op jit(solution)/shard_map/ppermute | solution.py:315
  182.9 23.7 %collective-permute-done.8 = f32[32,128]{1,0:T(8,128)S(1)} collective-permute-done((f32[32,128]{1,0:T(8,128)S(1)}, f32[32,128]{1,0:T(8,128)S(1)}, u32[]{:S(2)}, u32[]{:S(2)}) %collective-permute-start.8) | collective-permute-done | bytes 16416 | tf_op jit(solution)/shard_map/ppermute | solution.py:315
  206.6 5.6 %collective-permute-start.10 = (f32[32,128]{1,0:T(8,128)S(1)}, f32[32,128]{1,0:T(8,128)S(1)}, u32[]{:S(2)}, u32[]{:S(2)}) collective-permute-start(f32[32,128]{1,0:T(8,128)S(1)} %add.34), channel_id=1, source_target_pairs={{0,256},{16,272},{32,288},{48,304},{64,320},{80,336},{96,352},{112... | collective-permute-start | bytes 49160 | tf_op jit(solution)/shard_map/ppermute | solution.py:315
  212.2 5.3 %collective-permute-start.11 = (f32[32,128]{1,0:T(8,128)S(1)}, f32[32,128]{1,0:T(8,128)S(1)}, u32[]{:S(2)}, u32[]{:S(2)}) collective-permute-start(f32[32,128]{1,0:T(8,128)S(1)} %add.34), channel_id=1, source_target_pairs={{0,384},{16,400},{32,416},{48,432},{64,448},{80,464},{96,480},{112... | collective-permute-start | bytes 49160 | tf_op jit(solution)/shard_map/ppermute | solution.py:315
  220.0 4.1 %collective-permute-done.9 = f32[32,128]{1,0:T(8,128)S(1)} collective-permute-done((f32[32,128]{1,0:T(8,128)S(1)}, f32[32,128]{1,0:T(8,128)S(1)}, u32[]{:S(2)}, u32[]{:S(2)}) %collective-permute-start.9) | collective-permute-done | bytes 16416 | tf_op jit(solution)/shard_map/ppermute | solution.py:315
  229.0 3.7 %collective-permute-done.13 = f32[32,128]{1,0:T(8,128)S(1)} collective-permute-done((f32[32,128]{1,0:T(8,128)S(1)}, f32[32,128]{1,0:T(8,128)S(1)}, u32[]{:S(2)}, u32[]{:S(2)}) %collective-permute-start.13) | collective-permute-done | bytes 16416 | tf_op jit(solution)/shard_map/ppermute | solution.py:315
  234.9 4.3 %collective-permute-done.14 = f32[32,128]{1,0:T(8,128)S(1)} collective-permute-done((f32[32,128]{1,0:T(8,128)S(1)}, f32[32,128]{1,0:T(8,128)S(1)}, u32[]{:S(2)}, u32[]{:S(2)}) %collective-permute-start.14) | collective-permute-done | bytes 16416 | tf_op jit(solution)/shard_map/ppermute | solution.py:315
  239.3 3.0 %collective-permute-start.15 = (f32[32,128]{1,0:T(8,128)S(1)}, f32[32,128]{1,0:T(8,128)S(1)}, u32[]{:S(2)}, u32[]{:S(2)}) collective-permute-start(f32[32,128]{1,0:T(8,128)S(1)} %add.40), channel_id=1, source_target_pairs={{0,8},{1,9},{2,10},{3,11},{4,12},{5,13},{6,14},{7,15},{8,0},{9,1},... | collective-permute-start | bytes 49160 | tf_op jit(solution)/shard_map/ppermute | solution.py:315
  242.3 6.5 %collective-permute-done.15 = f32[32,128]{1,0:T(8,128)S(1)} collective-permute-done((f32[32,128]{1,0:T(8,128)S(1)}, f32[32,128]{1,0:T(8,128)S(1)}, u32[]{:S(2)}, u32[]{:S(2)}) %collective-permute-start.15) | collective-permute-done | bytes 16416 | tf_op jit(solution)/shard_map/ppermute | solution.py:315
  248.8 4.8 %collective-permute-start.16 = (f32[32,128]{1,0:T(8,128)S(1)}, f32[32,128]{1,0:T(8,128)S(1)}, u32[]{:S(2)}, u32[]{:S(2)}) collective-permute-start(f32[32,128]{1,0:T(8,128)S(1)} %add.41), channel_id=1, source_target_pairs={{0,32},{16,48},{32,0},{48,16},{64,96},{80,112},{96,64},{112,80},{1... | collective-permute-start | bytes 49160 | tf_op jit(solution)/shard_map/ppermute | solution.py:315
  256.0 3.7 %collective-permute-start.17 = (f32[64,128]{1,0:T(8,128)S(1)}, f32[64,128]{1,0:T(8,128)S(1)}, u32[]{:S(2)}, u32[]{:S(2)}) collective-permute-start(f32[64,128]{1,0:T(8,128)S(1)} %pad_maximum_fusion), channel_id=1, source_target_pairs={{0,16},{16,0},{32,48},{48,32},{64,80},{80,64},{96,112},{112,96},{1... | collective-permute-start | bytes 98312 | tf_op jit(solution)/shard_map/ppermute | solution.py:315
  261.6 3.6 %collective-permute-done.18 = s32[4,128]{1,0:T(4,128)S(1)} collective-permute-done((s32[4,128]{1,0:T(4,128)S(1)}, s32[4,128]{1,0:T(4,128)S(1)}, u32[]{:S(2)}, u32[]{:S(2)}) %collective-permute-start.18) | collective-permute-done | bytes 2080 | tf_op jit(solution)/shard_map/ppermute | solution.py:315
  267.1 4.5 %collective-permute-done.19 = s32[8,128]{1,0:T(8,128)S(1)} collective-permute-done((s32[8,128]{1,0:T(8,128)S(1)}, s32[8,128]{1,0:T(8,128)S(1)}, u32[]{:S(2)}, u32[]{:S(2)}) %collective-permute-start.19) | collective-permute-done | bytes 4128 | tf_op jit(solution)/shard_map/ppermute | solution.py:315
  273.5 7.5 %collective-permute-done.20 = s32[16,128]{1,0:T(8,128)S(1)} collective-permute-done((s32[16,128]{1,0:T(8,128)S(1)}, s32[16,128]{1,0:T(8,128)S(1)}, u32[]{:S(2)}, u32[]{:S(2)}) %collective-permute-start.20) | collective-permute-done | bytes 8224 | tf_op jit(solution)/shard_map/ppermute | solution.py:315
  (56 shorter events, 38.8 us)
Async XLA Ops:
  0.6 10.6 %copy-start.3 = (s32[1,1,32,2]{2,3,1,0:T(2,128)S(1)}, s32[1,1,32,2]{2,3,1,0:T(2,128)}, u32[]{:S(2)}) copy-start(s32[1,1,32,2]{2,3,1,0:T(2,128)} %param.15) | copy-start | bytes 772
  0.6 47.1 %copy-start.4 = (s32[1,1,16,2]{2,3,1,0:T(2,128)S(1)}, s32[1,1,16,2]{2,3,1,0:T(2,128)}, u32[]{:S(2)}) copy-start(s32[1,1,16,2]{2,3,1,0:T(2,128)} %param.14) | copy-start | bytes 388
  0.7 47.2 %copy-start.2 = (s32[1,1,128]{2,1,0:T(1,128)S(1)}, s32[1,1,128]{2,1,0:T(1,128)}, u32[]{:S(2)}) copy-start(s32[1,1,128]{2,1,0:T(1,128)} %param.12) | copy-start | bytes 1540
  2.6 31.5 %all-to-all-start = ((bf16[8,512,128]{2,1,0:T(8,128)(2,1)}), bf16[8,512,128]{2,1,0:T(8,128)(2,1)S(1)}, u32[]{:S(2)}, u32[]{:S(2)}) async-start(bf16[8,512,128]{2,1,0:T(8,128)(2,1)} %shard_map.104), calls=%async_computation | async-start | bytes 2097152 | tf_op jit(solution)/shard_map/all_to_all | solution.py:336
  11.5 8.5 %collective-permute-start = (s32[1,128]{1,0:T(1,128)S(1)}, s32[1,128]{1,0:T(1,128)S(1)}, u32[]{:S(2)}, u32[]{:S(2)}) collective-permute-start(s32[1,128]{1,0:T(1,128)S(1)} %pad.4.need), channel_id=1, source_target_pairs={{0,48},{16,0},{32,16},{48,32},{64,112},{80,64},{96,80},{112,96},{1... | collective-permute-start | bytes 1544 | tf_op jit(solution)/shard_map/ppermute | solution.py:325
  14.4 7.0 %collective-permute-start.1 = (s32[1,128]{1,0:T(1,128)S(1)}, s32[1,128]{1,0:T(1,128)S(1)}, u32[]{:S(2)}, u32[]{:S(2)}) collective-permute-start(s32[1,128]{1,0:T(1,128)S(1)} %pad.4.need), channel_id=1, source_target_pairs={{0,32},{16,48},{32,0},{48,16},{64,96},{80,112},{96,64},{112,80},{1... | collective-permute-start | bytes 1544 | tf_op jit(solution)/shard_map/ppermute | solution.py:325
  17.1 6.7 %collective-permute-start.2 = (s32[1,128]{1,0:T(1,128)S(1)}, s32[1,128]{1,0:T(1,128)S(1)}, u32[]{:S(2)}, u32[]{:S(2)}) collective-permute-start(s32[1,128]{1,0:T(1,128)S(1)} %pad.4.need), channel_id=1, source_target_pairs={{0,16},{16,32},{32,48},{48,0},{64,80},{80,96},{96,112},{112,64},{1... | collective-permute-start | bytes 1544 | tf_op jit(solution)/shard_map/ppermute | solution.py:325
  35.9 18.4 %collective-permute-start.3 = (bf16[8,256,128]{2,1,0:T(8,128)(2,1)}, bf16[8,256,128]{2,1,0:T(8,128)(2,1)S(1)}, u32[]{:S(2)}, u32[]{:S(2)}) collective-permute-start(bf16[8,256,128]{2,1,0:T(8,128)(2,1)} %get-tuple-element.11), channel_id=1, source_target_pairs={{0,32},{16,48},{32,0},{48,16},{64,96},{80,112},{96,64},{112,80},{1... | collective-permute-start | bytes 1572872 | tf_op jit(solution)/shard_map/ppermute | solution.py:325
  40.0 20.6 %collective-permute-start.4 = (bf16[8,256,128]{2,1,0:T(8,128)(2,1)}, bf16[8,256,128]{2,1,0:T(8,128)(2,1)S(1)}, u32[]{:S(2)}, u32[]{:S(2)}) collective-permute-start(bf16[8,256,128]{2,1,0:T(8,128)(2,1)} %get-tuple-element.14), channel_id=1, source_target_pairs={{0,16},{16,32},{32,48},{48,0},{64,80},{80,96},{96,112},{112,64},{1... | collective-permute-start | bytes 1572872 | tf_op jit(solution)/shard_map/ppermute | solution.py:325
  42.5 18.4 %collective-permute-start.5 = (bf16[8,256,128]{2,1,0:T(8,128)(2,1)S(1)}, bf16[8,256,128]{2,1,0:T(8,128)(2,1)S(1)}, u32[]{:S(2)}, u32[]{:S(2)}) collective-permute-start(bf16[8,256,128]{2,1,0:T(8,128)(2,1)S(1)} %get-tuple-element.15), channel_id=1, source_target_pairs={{0,48},{16,0},{32,16},{48,32},{64,112},{80,64},{96,80},{112,96},{1... | collective-permute-start | bytes 1572872 | tf_op jit(solution)/shard_map/ppermute | solution.py:325
  65.1 39.8 %copy-start = (bf16[1,1,512,128]{3,2,1,0:T(8,128)(2,1)S(1)}, bf16[1,1,512,128]{3,2,1,0:T(8,128)(2,1)}, u32[]{:S(2)}) copy-start(bf16[1,1,512,128]{3,2,1,0:T(8,128)(2,1)} %param.9) | copy-start | bytes 393220
  65.1 39.8 %copy-start.1 = (bf16[128,128]{1,0:T(8,128)(2,1)S(1)}, bf16[128,128]{1,0:T(8,128)(2,1)}, u32[]{:S(2)}) copy-start(bf16[128,128]{1,0:T(8,128)(2,1)} %weight.1) | copy-start | bytes 98308
  146.0 135.7 %all-to-all-start.3 = ((bf16[32,256,128]{2,1,0:T(8,128)(2,1)}), bf16[32,256,128]{2,1,0:T(8,128)(2,1)S(1)}, u32[]{:S(2)}, u32[]{:S(2)}) async-start(bf16[32,256,128]{2,1,0:T(8,128)(2,1)} %shard_map.109), calls=%async_computation.3 | async-start | bytes 4194304 | tf_op jit(solution)/shard_map/all_to_all | solution.py:311
  159.2 8.5 %collective-permute-start.6 = (f32[64,128]{1,0:T(8,128)S(1)}, f32[64,128]{1,0:T(8,128)S(1)}, u32[]{:S(2)}, u32[]{:S(2)}) collective-permute-start(f32[64,128]{1,0:T(8,128)S(1)} %slice_select_fusion), channel_id=1, source_target_pairs={{0,16},{16,0},{32,48},{48,32},{64,80},{80,64},{96,112},{112,96},{1... | collective-permute-start | bytes 98312 | tf_op jit(solution)/shard_map/ppermute | solution.py:315
  167.7 8.6 %collective-permute-start.7 = (f32[32,128]{1,0:T(8,128)S(1)}, f32[32,128]{1,0:T(8,128)S(1)}, u32[]{:S(2)}, u32[]{:S(2)}) collective-permute-start(f32[32,128]{1,0:T(8,128)S(1)} %slice_select_fusion.1), channel_id=1, source_target_pairs={{0,32},{16,48},{32,0},{48,16},{64,96},{80,112},{96,64},{112,80},{1... | collective-permute-start | bytes 49160 | tf_op jit(solution)/shard_map/ppermute | solution.py:315
  176.3 30.3 %collective-permute-start.8 = (f32[32,128]{1,0:T(8,128)S(1)}, f32[32,128]{1,0:T(8,128)S(1)}, u32[]{:S(2)}, u32[]{:S(2)}) collective-permute-start(f32[32,128]{1,0:T(8,128)S(1)} %select_add_fusion.1), channel_id=1, source_target_pairs={{0,64},{16,80},{32,96},{48,112},{64,0},{80,16},{96,32},{112,48},{1... | collective-permute-start | bytes 49160 | tf_op jit(solution)/shard_map/ppermute | solution.py:315
  206.6 12.8 %collective-permute-start.10 = (f32[32,128]{1,0:T(8,128)S(1)}, f32[32,128]{1,0:T(8,128)S(1)}, u32[]{:S(2)}, u32[]{:S(2)}) collective-permute-start(f32[32,128]{1,0:T(8,128)S(1)} %add.34), channel_id=1, source_target_pairs={{0,256},{16,272},{32,288},{48,304},{64,320},{80,336},{96,352},{112... | collective-permute-start | bytes 49160 | tf_op jit(solution)/shard_map/ppermute | solution.py:315
  212.2 7.7 %collective-permute-start.11 = (f32[32,128]{1,0:T(8,128)S(1)}, f32[32,128]{1,0:T(8,128)S(1)}, u32[]{:S(2)}, u32[]{:S(2)}) collective-permute-start(f32[32,128]{1,0:T(8,128)S(1)} %add.34), channel_id=1, source_target_pairs={{0,384},{16,400},{32,416},{48,432},{64,448},{80,464},{96,480},{112... | collective-permute-start | bytes 49160 | tf_op jit(solution)/shard_map/ppermute | solution.py:315
  217.5 6.5 %collective-permute-start.9 = (f32[32,128]{1,0:T(8,128)S(1)}, f32[32,128]{1,0:T(8,128)S(1)}, u32[]{:S(2)}, u32[]{:S(2)}) collective-permute-start(f32[32,128]{1,0:T(8,128)S(1)} %add.34), channel_id=1, source_target_pairs={{0,128},{16,144},{32,160},{48,176},{64,192},{80,208},{96,224},{112... | collective-permute-start | bytes 49160 | tf_op jit(solution)/shard_map/ppermute | solution.py:315
  224.1 3.1 %collective-permute-start.12 = (f32[32,128]{1,0:T(8,128)S(1)}, f32[32,128]{1,0:T(8,128)S(1)}, u32[]{:S(2)}, u32[]{:S(2)}) collective-permute-start(f32[32,128]{1,0:T(8,128)S(1)} %add_add_fusion), channel_id=1, source_target_pairs={{0,1},{1,0},{2,3},{3,2},{4,5},{5,4},{6,7},{7,6},{8,9},{9,8},{10,11... | collective-permute-start | bytes 49160 | tf_op jit(solution)/shard_map/ppermute | solution.py:315
  227.1 5.6 %collective-permute-start.13 = (f32[32,128]{1,0:T(8,128)S(1)}, f32[32,128]{1,0:T(8,128)S(1)}, u32[]{:S(2)}, u32[]{:S(2)}) collective-permute-start(f32[32,128]{1,0:T(8,128)S(1)} %add.38), channel_id=1, source_target_pairs={{0,2},{1,3},{2,0},{3,1},{4,6},{5,7},{6,4},{7,5},{8,10},{9,11},{10,... | collective-permute-start | bytes 49160 | tf_op jit(solution)/shard_map/ppermute | solution.py:315
  232.8 6.5 %collective-permute-start.14 = (f32[32,128]{1,0:T(8,128)S(1)}, f32[32,128]{1,0:T(8,128)S(1)}, u32[]{:S(2)}, u32[]{:S(2)}) collective-permute-start(f32[32,128]{1,0:T(8,128)S(1)} %add.39), channel_id=1, source_target_pairs={{0,4},{1,5},{2,6},{3,7},{4,0},{5,1},{6,2},{7,3},{8,12},{9,13},{10,... | collective-permute-start | bytes 49160 | tf_op jit(solution)/shard_map/ppermute | solution.py:315
  239.3 9.5 %collective-permute-start.15 = (f32[32,128]{1,0:T(8,128)S(1)}, f32[32,128]{1,0:T(8,128)S(1)}, u32[]{:S(2)}, u32[]{:S(2)}) collective-permute-start(f32[32,128]{1,0:T(8,128)S(1)} %add.40), channel_id=1, source_target_pairs={{0,8},{1,9},{2,10},{3,11},{4,12},{5,13},{6,14},{7,15},{8,0},{9,1},... | collective-permute-start | bytes 49160 | tf_op jit(solution)/shard_map/ppermute | solution.py:315
  248.8 7.1 %collective-permute-start.16 = (f32[32,128]{1,0:T(8,128)S(1)}, f32[32,128]{1,0:T(8,128)S(1)}, u32[]{:S(2)}, u32[]{:S(2)}) collective-permute-start(f32[32,128]{1,0:T(8,128)S(1)} %add.41), channel_id=1, source_target_pairs={{0,32},{16,48},{32,0},{48,16},{64,96},{80,112},{96,64},{112,80},{1... | collective-permute-start | bytes 49160 | tf_op jit(solution)/shard_map/ppermute | solution.py:315
  256.0 25.1 %collective-permute-start.17 = (f32[64,128]{1,0:T(8,128)S(1)}, f32[64,128]{1,0:T(8,128)S(1)}, u32[]{:S(2)}, u32[]{:S(2)}) collective-permute-start(f32[64,128]{1,0:T(8,128)S(1)} %pad_maximum_fusion), channel_id=1, source_target_pairs={{0,16},{16,0},{32,48},{48,32},{64,80},{80,64},{96,112},{112,96},{1... | collective-permute-start | bytes 98312 | tf_op jit(solution)/shard_map/ppermute | solution.py:315
  259.7 5.5 %collective-permute-start.18 = (s32[4,128]{1,0:T(4,128)S(1)}, s32[4,128]{1,0:T(4,128)S(1)}, u32[]{:S(2)}, u32[]{:S(2)}) collective-permute-start(s32[4,128]{1,0:T(4,128)S(1)} %pad_add_fusion), channel_id=1, source_target_pairs={{0,64},{16,80},{32,96},{48,112},{64,0},{80,16},{96,32},{112,48},{1... | collective-permute-start | bytes 6152 | tf_op jit(solution)/shard_map/ppermute | solution.py:315
  265.2 6.4 %collective-permute-start.19 = (s32[8,128]{1,0:T(8,128)S(1)}, s32[8,128]{1,0:T(8,128)S(1)}, u32[]{:S(2)}, u32[]{:S(2)}) collective-permute-start(s32[8,128]{1,0:T(8,128)S(1)} %concatenate.24), channel_id=1, source_target_pairs={{0,128},{16,144},{32,160},{48,176},{64,192},{80,208},{96,224},{112... | collective-permute-start | bytes 12296 | tf_op jit(solution)/shard_map/ppermute | solution.py:315
  271.6 9.4 %collective-permute-start.20 = (s32[16,128]{1,0:T(8,128)S(1)}, s32[16,128]{1,0:T(8,128)S(1)}, u32[]{:S(2)}, u32[]{:S(2)}) collective-permute-start(s32[16,128]{1,0:T(8,128)S(1)} %concatenate.25), channel_id=1, source_target_pairs={{0,256},{16,272},{32,288},{48,304},{64,320},{80,336},{96,352},{112... | collective-permute-start | bytes 24584 | tf_op jit(solution)/shard_map/ppermute | solution.py:315

commit v7 on v6

--- a/solution.py
+++ b/solution.py
@@ -12,6 +12,7 @@
 EXTRA = 16
 NX = 4
 GROUP = 8
+WIDE = 16
 BATCH = 2
 PARTS = 4
 ROWS = 32
@@ -252,11 +253,12 @@
     acc[...] = jnp.zeros_like(acc)
 
     def group(g, carry):
-        load(g).wait()
-        for first in range(0, GROUP, BATCH):
+        for part in range(WIDE // GROUP):
+            load(g * (WIDE // GROUP) + part).wait()
+        for first in range(0, WIDE, BATCH):
             terms = []
             for u in range(first, first + BATCH):
-                b = g * GROUP + u
+                b = g * WIDE + u
                 slot = slots[0, b]
                 grads = arrived[slot >> shift]
                 term = lax.dot_general(
@@ -267,7 +269,7 @@
                 acc[col] += term
         return carry
 
-    lax.fori_loop(0, groups, group, 0)
+    lax.fori_loop(0, groups // (WIDE // GROUP), group, 0)
     ship = shipper(held, out, sems)
     for r in range(out.shape[0]):
         for k in range(2):
@@ -418,10 +420,9 @@
         low, high = jnp.split(term, 2, axis=0)
         top = upper("gr", bit)
         term = jnp.where(top, high, low) + trade(jnp.where(top, low, high), "gr", bit)
-    other = trade(term, "gr", 4)
-    term = term + other
-    others = [trade(term, "gr", bits) for bits in (8, 16, 24)]
-    term = (term + others[0]) + (others[1] + others[2])
+    for bit in (4, 8, 16):
+        other = trade(term, "gr", bit)
+        term = term + other
     bit = 1
     while bit < n_cols:
         term = term + trade(term, "gc", bit)

time: 285 us -> 284 us (level)
  the two profiles are of different devices: /device:TPU:56 before, /device:TPU:4 now
where the time goes in v7:
time: 284 us; the launch traced here: 283 us
  waiting for transfers between devices  101 us (36%)
  starting transfers between devices  80.8 us (28%)
  blocking collectives  71.7 us (25%)
  Pallas kernels  26.4 us (9%)
    ppermute x14, waiting for transfers between devices, trade(): return lax.ppermute(array, axis, pairs)  72.1 us
    all_to_all x2, blocking collectives, swap(): return lax.all_to_all(array, axis, split_axis=0, concat_axis=0, tiled=True)  71.7 us
    ppermute x14, starting transfers between devices, trade(): return lax.ppermute(array, axis, pairs)  49.6 us
    ppermute x6, starting transfers between devices, along_x(): return lax.ppermute(array, 'gr', pairs)  19.1 us
    all_to_all x1, waiting for transfers between devices, on_device(): lax.all_to_all(copies, 'gr', split_axis=0, concat_axis=0, tiled=True, axi...  16 us
    ppermute x6, waiting for transfers between devices, along_x(): return lax.ppermute(array, 'gr', pairs)  13.3 us
    all_to_all x1, starting transfers between devices, on_device(): lax.all_to_all(copies, 'gr', split_axis=0, concat_axis=0, tiled=True, axi...  7.11 us
    pallas_call x1, Pallas kernels, on_device(): call(functools.partial(backward_kernel, col_slots), pltpu.HBM((n_rows, ca...  5.99 us
  transfers between devices with their start and end apart: 22, of which 17 were waited for; matrix products, arithmetic and copies ran while one was open for 0% of the time, Pallas kernels for 3%

profile of v7, /device:TPU:4, one launch (start us, length us, event | category | flops | bytes accessed | tf_op | source)
XLA Modules:
  0.0 283.0 jit_solution(14289255178680281594)
XLA Ops:
  2.6 7.1 %all-to-all-start = ((bf16[8,512,128]{2,1,0:T(8,128)(2,1)}), bf16[8,512,128]{2,1,0:T(8,128)(2,1)S(1)}, u32[]{:S(2)}, u32[]{:S(2)}) async-start(bf16[8,512,128]{2,1,0:T(8,128)(2,1)} %shard_map.104), calls=%async_computation | async-start | bytes 2097152 | tf_op jit(solution)/shard_map/all_to_all | solution.py:338
  12.4 4.6 %collective-permute-start.1 = (s32[1,128]{1,0:T(1,128)S(1)}, s32[1,128]{1,0:T(1,128)S(1)}, u32[]{:S(2)}, u32[]{:S(2)}) collective-permute-start(s32[1,128]{1,0:T(1,128)S(1)} %pad.4.need), channel_id=1, source_target_pairs={{0,32},{16,48},{32,0},{48,16},{64,96},{80,112},{96,64},{112,80},{1... | collective-permute-start | bytes 1544 | tf_op jit(solution)/shard_map/ppermute | solution.py:327
  17.1 3.6 %collective-permute-start.2 = (s32[1,128]{1,0:T(1,128)S(1)}, s32[1,128]{1,0:T(1,128)S(1)}, u32[]{:S(2)}, u32[]{:S(2)}) collective-permute-start(s32[1,128]{1,0:T(1,128)S(1)} %pad.4.need), channel_id=1, source_target_pairs={{0,16},{16,32},{32,48},{48,0},{64,80},{80,96},{96,112},{112,64},{1... | collective-permute-start | bytes 1544 | tf_op jit(solution)/shard_map/ppermute | solution.py:327
  22.5 16.0 %all-to-all-done.refs_3_.column = bf16[8,512,128]{2,1,0:T(8,128)(2,1)S(1)} async-done(((bf16[8,512,128]{2,1,0:T(8,128)(2,1)}), bf16[8,512,128]{2,1,0:T(8,128)(2,1)S(1)}, u32[]{:S(2)}, u32[]{:S(2)}) %all-to-all-start) | async-done | bytes 1048608 | tf_op jit(solution)/shard_map/all_to_all | solution.py:338
  42.6 4.0 %collective-permute-start.4 = (bf16[8,256,128]{2,1,0:T(8,128)(2,1)}, bf16[8,256,128]{2,1,0:T(8,128)(2,1)S(1)}, u32[]{:S(2)}, u32[]{:S(2)}) collective-permute-start(bf16[8,256,128]{2,1,0:T(8,128)(2,1)} %get-tuple-element.14), channel_id=1, source_target_pairs={{0,16},{16,32},{32,48},{48,0},{64,80},{80,96},{96,112},{112,64},{1... | collective-permute-start | bytes 1572872 | tf_op jit(solution)/shard_map/ppermute | solution.py:327
  49.3 4.1 %shard_map.103.plan = s32[6,144]{1,0:T(8,128)S(1)} custom-call(s32[1,1]{1,0:T(1,128)} %bitcast.me, s32[1,128]{1,0:T(1,128)S(1)} %bitcast.19, s32[1,1]{1,0:T(1,128)S(6)} %copy.15.live), custom_call_target="tpu_custom_call" | custom-call | tf_op jit(solution)/shard_map/pallas_call | solution.py:355
  53.5 5.1 %collective-permute-done.3 = bf16[8,256,128]{2,1,0:T(8,128)(2,1)S(1)} collective-permute-done((bf16[8,256,128]{2,1,0:T(8,128)(2,1)}, bf16[8,256,128]{2,1,0:T(8,128)(2,1)S(1)}, u32[]{:S(2)}, u32[]{:S(2)}) %collective-permute-start.3) | collective-permute-done | bytes 524320 | tf_op jit(solution)/shard_map/ppermute | solution.py:327
  58.6 3.9 %shard_map.106 = (f32[33,128,128]{2,1,0:T(8,128)S(1)}, bf16[128,128,128]{2,1,0:T(8,128)(2,1)S(1)}) custom-call(s32[1,1]{1,0:T(1,128)} %bitcast.me, s32[6,144]{1,0:T(8,128)S(1)} %shard_map.103.plan, s32[1,128]{1,0:T(1,128)S(1)} %pad.4.need, bf16[128,128,128]{2,1,0:T(8,128)(2,1)} %bitcast.21, bf16[8,512,128]{2,1,0:T(8,128)(2,1)S(1)} %all-to-all-done.refs_3_.column, ...), custom_call_target="tpu_custom_call" | custom-call | flops 536870912 | bytes 8388608 | tf_op jit(solution)/shard_map/pallas_call | solution.py:365
  62.6 6.3 %collective-permute-done.4 = bf16[8,256,128]{2,1,0:T(8,128)(2,1)S(1)} collective-permute-done((bf16[8,256,128]{2,1,0:T(8,128)(2,1)}, bf16[8,256,128]{2,1,0:T(8,128)(2,1)S(1)}, u32[]{:S(2)}, u32[]{:S(2)}) %collective-permute-start.4) | collective-permute-done | bytes 524320 | tf_op jit(solution)/shard_map/ppermute | solution.py:327
  68.8 3.9 %shard_map.107 = bf16[16,272,128]{2,1,0:T(8,128)(2,1)} custom-call(s32[6,144]{1,0:T(8,128)S(1)} %shard_map.103.plan, s32[16,2]{1,0:T(8,128)S(1)} %copy.14.row_need, f32[33,128,128]{2,1,0:T(8,128)S(1)} %get-tuple-element.12.early, bf16[128,128,128]{2,1,0:T(8,128)(2,1)S(1)} %get-tuple-element.13.values, bf16[16,128,128]{2,1,0:T(8,128)(2,1)S(1)} %bitcast.15, ...), custom_call_target="tpu_custom_call" | custom-call | flops 268435456 | bytes 8388608 | tf_op jit(solution)/shard_map/pallas_call | solution.py:382
  72.8 40.9 %all_to_all.20.arrived = bf16[16,272,128]{2,1,0:T(8,128)(2,1)S(1)} all-to-all(bf16[16,272,128]{2,1,0:T(8,128)(2,1)} %shard_map.107), channel_id=1, replica_groups=mesh['gr'=32,'gc'=16] {'gc'}, dimensions={0} | all-to-all | bytes 2228224 | tf_op jit(solution)/shard_map/all_to_all | solution.py:313
  116.5 30.8 %all_to_all.21 = bf16[16,256,128]{2,1,0:T(8,128)(2,1)S(1)} all-to-all(bf16[16,256,128]{2,1,0:T(8,128)(2,1)} %get-tuple-element.18), channel_id=1, replica_groups=mesh['gr'=32,'gc'=16] {'gc'}, dimensions={0} | all-to-all | bytes 2097152 | tf_op jit(solution)/shard_map/all_to_all | solution.py:313
  147.3 6.0 %shard_map.109 = bf16[32,256,128]{2,1,0:T(8,128)(2,1)} custom-call(s32[1,128]{1,0:T(1,128)S(1)} %bitcast.20, s32[1,1]{1,0:T(1,128)S(6)} %copy.15.live, bf16[128,128,128]{2,1,0:T(8,128)(2,1)} %bitcast.22, bf16[32,128,128]{2,1,0:T(8,128)(2,1)S(1)} %bitcast.14), custom_call_target="tpu_custom_call" | custom-call | flops 536870912 | bytes 8388608 | tf_op jit(solution)/shard_map/pallas_call | solution.py:437
  153.3 5.0 %all-to-all-start.3 = ((bf16[32,256,128]{2,1,0:T(8,128)(2,1)}), bf16[32,256,128]{2,1,0:T(8,128)(2,1)S(1)}, u32[]{:S(2)}, u32[]{:S(2)}) async-start(bf16[32,256,128]{2,1,0:T(8,128)(2,1)} %shard_map.109), calls=%async_computation.3 | async-start | bytes 4194304 | tf_op jit(solution)/shard_map/all_to_all | solution.py:313
  161.4 3.1 %collective-permute-done.6 = f32[64,128]{1,0:T(8,128)S(1)} collective-permute-done((f32[64,128]{1,0:T(8,128)S(1)}, f32[64,128]{1,0:T(8,128)S(1)}, u32[]{:S(2)}, u32[]{:S(2)}) %collective-permute-start.6) | collective-permute-done | bytes 32800 | tf_op jit(solution)/shard_map/ppermute | solution.py:317
  167.3 4.5 %collective-permute-done.7 = f32[32,128]{1,0:T(8,128)S(1)} collective-permute-done((f32[32,128]{1,0:T(8,128)S(1)}, f32[32,128]{1,0:T(8,128)S(1)}, u32[]{:S(2)}, u32[]{:S(2)}) %collective-permute-start.7) | collective-permute-done | bytes 16416 | tf_op jit(solution)/shard_map/ppermute | solution.py:317
  171.8 4.9 %collective-permute-start.8 = (f32[32,128]{1,0:T(8,128)S(1)}, f32[32,128]{1,0:T(8,128)S(1)}, u32[]{:S(2)}, u32[]{:S(2)}) collective-permute-start(f32[32,128]{1,0:T(8,128)S(1)} %select_add_fusion.1), channel_id=1, source_target_pairs={{0,64},{16,80},{32,96},{48,112},{64,0},{80,16},{96,32},{112,48},{1... | collective-permute-start | bytes 49160 | tf_op jit(solution)/shard_map/ppermute | solution.py:317
  176.7 28.9 %collective-permute-done.8 = f32[32,128]{1,0:T(8,128)S(1)} collective-permute-done((f32[32,128]{1,0:T(8,128)S(1)}, f32[32,128]{1,0:T(8,128)S(1)}, u32[]{:S(2)}, u32[]{:S(2)}) %collective-permute-start.8) | collective-permute-done | bytes 16416 | tf_op jit(solution)/shard_map/ppermute | solution.py:317
  205.7 5.3 %collective-permute-start.9 = (f32[32,128]{1,0:T(8,128)S(1)}, f32[32,128]{1,0:T(8,128)S(1)}, u32[]{:S(2)}, u32[]{:S(2)}) collective-permute-start(f32[32,128]{1,0:T(8,128)S(1)} %add.31), channel_id=1, source_target_pairs={{0,128},{16,144},{32,160},{48,176},{64,192},{80,208},{96,224},{112... | collective-permute-start | bytes 49160 | tf_op jit(solution)/shard_map/ppermute | solution.py:317
  212.7 5.8 %collective-permute-start.10 = (f32[32,128]{1,0:T(8,128)S(1)}, f32[32,128]{1,0:T(8,128)S(1)}, u32[]{:S(2)}, u32[]{:S(2)}) collective-permute-start(f32[32,128]{1,0:T(8,128)S(1)} %add.32), channel_id=1, source_target_pairs={{0,256},{16,272},{32,288},{48,304},{64,320},{80,336},{96,352},{112... | collective-permute-start | bytes 49160 | tf_op jit(solution)/shard_map/ppermute | solution.py:317
  218.5 3.7 %collective-permute-done.10 = f32[32,128]{1,0:T(8,128)S(1)} collective-permute-done((f32[32,128]{1,0:T(8,128)S(1)}, f32[32,128]{1,0:T(8,128)S(1)}, u32[]{:S(2)}, u32[]{:S(2)}) %collective-permute-start.10) | collective-permute-done | bytes 16416 | tf_op jit(solution)/shard_map/ppermute | solution.py:317
  227.2 3.7 %collective-permute-done.12 = f32[32,128]{1,0:T(8,128)S(1)} collective-permute-done((f32[32,128]{1,0:T(8,128)S(1)}, f32[32,128]{1,0:T(8,128)S(1)}, u32[]{:S(2)}, u32[]{:S(2)}) %collective-permute-start.12) | collective-permute-done | bytes 16416 | tf_op jit(solution)/shard_map/ppermute | solution.py:317
  233.7 3.7 %collective-permute-done.13 = f32[32,128]{1,0:T(8,128)S(1)} collective-permute-done((f32[32,128]{1,0:T(8,128)S(1)}, f32[32,128]{1,0:T(8,128)S(1)}, u32[]{:S(2)}, u32[]{:S(2)}) %collective-permute-start.13) | collective-permute-done | bytes 16416 | tf_op jit(solution)/shard_map/ppermute | solution.py:317
  237.4 3.6 %collective-permute-start.14 = (f32[32,128]{1,0:T(8,128)S(1)}, f32[32,128]{1,0:T(8,128)S(1)}, u32[]{:S(2)}, u32[]{:S(2)}) collective-permute-start(f32[32,128]{1,0:T(8,128)S(1)} %add.36), channel_id=1, source_target_pairs={{0,8},{1,9},{2,10},{3,11},{4,12},{5,13},{6,14},{7,15},{8,0},{9,1},... | collective-permute-start | bytes 49160 | tf_op jit(solution)/shard_map/ppermute | solution.py:317
  241.1 5.9 %collective-permute-done.14 = f32[32,128]{1,0:T(8,128)S(1)} collective-permute-done((f32[32,128]{1,0:T(8,128)S(1)}, f32[32,128]{1,0:T(8,128)S(1)}, u32[]{:S(2)}, u32[]{:S(2)}) %collective-permute-start.14) | collective-permute-done | bytes 16416 | tf_op jit(solution)/shard_map/ppermute | solution.py:317
  247.0 3.5 %collective-permute-start.15 = (f32[32,128]{1,0:T(8,128)S(1)}, f32[32,128]{1,0:T(8,128)S(1)}, u32[]{:S(2)}, u32[]{:S(2)}) collective-permute-start(f32[32,128]{1,0:T(8,128)S(1)} %add.37), channel_id=1, source_target_pairs={{0,32},{16,48},{32,0},{48,16},{64,96},{80,112},{96,64},{112,80},{1... | collective-permute-start | bytes 49160 | tf_op jit(solution)/shard_map/ppermute | solution.py:317
  250.5 3.6 %collective-permute-done.15 = f32[32,128]{1,0:T(8,128)S(1)} collective-permute-done((f32[32,128]{1,0:T(8,128)S(1)}, f32[32,128]{1,0:T(8,128)S(1)}, u32[]{:S(2)}, u32[]{:S(2)}) %collective-permute-start.15) | collective-permute-done | bytes 16416 | tf_op jit(solution)/shard_map/ppermute | solution.py:317
  254.1 4.8 %collective-permute-start.16 = (f32[64,128]{1,0:T(8,128)S(1)}, f32[64,128]{1,0:T(8,128)S(1)}, u32[]{:S(2)}, u32[]{:S(2)}) collective-permute-start(f32[64,128]{1,0:T(8,128)S(1)} %pad_maximum_fusion), channel_id=1, source_target_pairs={{0,16},{16,0},{32,48},{48,32},{64,80},{80,64},{96,112},{112,96},{1... | collective-permute-start | bytes 98312 | tf_op jit(solution)/shard_map/ppermute | solution.py:317
  260.8 3.6 %collective-permute-done.17 = s32[4,128]{1,0:T(4,128)S(1)} collective-permute-done((s32[4,128]{1,0:T(4,128)S(1)}, s32[4,128]{1,0:T(4,128)S(1)}, u32[]{:S(2)}, u32[]{:S(2)}) %collective-permute-start.17) | collective-permute-done | bytes 2080 | tf_op jit(solution)/shard_map/ppermute | solution.py:317
  266.4 4.4 %collective-permute-done.18 = s32[8,128]{1,0:T(8,128)S(1)} collective-permute-done((s32[8,128]{1,0:T(8,128)S(1)}, s32[8,128]{1,0:T(8,128)S(1)}, u32[]{:S(2)}, u32[]{:S(2)}) %collective-permute-start.18) | collective-permute-done | bytes 4128 | tf_op jit(solution)/shard_map/ppermute | solution.py:317
  270.8 5.4 %collective-permute-start.19 = (s32[16,128]{1,0:T(8,128)S(1)}, s32[16,128]{1,0:T(8,128)S(1)}, u32[]{:S(2)}, u32[]{:S(2)}) collective-permute-start(s32[16,128]{1,0:T(8,128)S(1)} %concatenate.25), channel_id=1, source_target_pairs={{0,256},{16,272},{32,288},{48,304},{64,320},{80,336},{96,352},{112... | collective-permute-start | bytes 24584 | tf_op jit(solution)/shard_map/ppermute | solution.py:317
  276.2 4.1 %collective-permute-done.19 = s32[16,128]{1,0:T(8,128)S(1)} collective-permute-done((s32[16,128]{1,0:T(8,128)S(1)}, s32[16,128]{1,0:T(8,128)S(1)}, u32[]{:S(2)}, u32[]{:S(2)}) %collective-permute-start.19) | collective-permute-done | bytes 8224 | tf_op jit(solution)/shard_map/ppermute | solution.py:317
  (55 shorter events, 37.4 us)
Async XLA Ops:
  0.6 9.1 %copy-start.3 = (s32[1,1,32,2]{2,3,1,0:T(2,128)S(1)}, s32[1,1,32,2]{2,3,1,0:T(2,128)}, u32[]{:S(2)}) copy-start(s32[1,1,32,2]{2,3,1,0:T(2,128)} %param.15) | copy-start | bytes 772
  0.6 48.6 %copy-start.4 = (s32[1,1,16,2]{2,3,1,0:T(2,128)S(1)}, s32[1,1,16,2]{2,3,1,0:T(2,128)}, u32[]{:S(2)}) copy-start(s32[1,1,16,2]{2,3,1,0:T(2,128)} %param.14) | copy-start | bytes 388
  0.7 48.7 %copy-start.2 = (s32[1,1,128]{2,1,0:T(1,128)S(1)}, s32[1,1,128]{2,1,0:T(1,128)}, u32[]{:S(2)}) copy-start(s32[1,1,128]{2,1,0:T(1,128)} %param.12) | copy-start | bytes 1540
  2.6 35.8 %all-to-all-start = ((bf16[8,512,128]{2,1,0:T(8,128)(2,1)}), bf16[8,512,128]{2,1,0:T(8,128)(2,1)S(1)}, u32[]{:S(2)}, u32[]{:S(2)}) async-start(bf16[8,512,128]{2,1,0:T(8,128)(2,1)} %shard_map.104), calls=%async_computation | async-start | bytes 2097152 | tf_op jit(solution)/shard_map/all_to_all | solution.py:338
  10.0 10.7 %collective-permute-start = (s32[1,128]{1,0:T(1,128)S(1)}, s32[1,128]{1,0:T(1,128)S(1)}, u32[]{:S(2)}, u32[]{:S(2)}) collective-permute-start(s32[1,128]{1,0:T(1,128)S(1)} %pad.4.need), channel_id=1, source_target_pairs={{0,48},{16,0},{32,16},{48,32},{64,112},{80,64},{96,80},{112,96},{1... | collective-permute-start | bytes 1544 | tf_op jit(solution)/shard_map/ppermute | solution.py:327
  12.4 8.3 %collective-permute-start.1 = (s32[1,128]{1,0:T(1,128)S(1)}, s32[1,128]{1,0:T(1,128)S(1)}, u32[]{:S(2)}, u32[]{:S(2)}) collective-permute-start(s32[1,128]{1,0:T(1,128)S(1)} %pad.4.need), channel_id=1, source_target_pairs={{0,32},{16,48},{32,0},{48,16},{64,96},{80,112},{96,64},{112,80},{1... | collective-permute-start | bytes 1544 | tf_op jit(solution)/shard_map/ppermute | solution.py:327
  17.1 5.5 %collective-permute-start.2 = (s32[1,128]{1,0:T(1,128)S(1)}, s32[1,128]{1,0:T(1,128)S(1)}, u32[]{:S(2)}, u32[]{:S(2)}) collective-permute-start(s32[1,128]{1,0:T(1,128)S(1)} %pad.4.need), channel_id=1, source_target_pairs={{0,16},{16,32},{32,48},{48,0},{64,80},{80,96},{96,112},{112,64},{1... | collective-permute-start | bytes 1544 | tf_op jit(solution)/shard_map/ppermute | solution.py:327
  40.2 18.4 %collective-permute-start.3 = (bf16[8,256,128]{2,1,0:T(8,128)(2,1)}, bf16[8,256,128]{2,1,0:T(8,128)(2,1)S(1)}, u32[]{:S(2)}, u32[]{:S(2)}) collective-permute-start(bf16[8,256,128]{2,1,0:T(8,128)(2,1)} %get-tuple-element.11), channel_id=1, source_target_pairs={{0,32},{16,48},{32,0},{48,16},{64,96},{80,112},{96,64},{112,80},{1... | collective-permute-start | bytes 1572872 | tf_op jit(solution)/shard_map/ppermute | solution.py:327
  42.6 26.3 %collective-permute-start.4 = (bf16[8,256,128]{2,1,0:T(8,128)(2,1)}, bf16[8,256,128]{2,1,0:T(8,128)(2,1)S(1)}, u32[]{:S(2)}, u32[]{:S(2)}) collective-permute-start(bf16[8,256,128]{2,1,0:T(8,128)(2,1)} %get-tuple-element.14), channel_id=1, source_target_pairs={{0,16},{16,32},{32,48},{48,0},{64,80},{80,96},{96,112},{112,64},{1... | collective-permute-start | bytes 1572872 | tf_op jit(solution)/shard_map/ppermute | solution.py:327
  46.6 22.3 %collective-permute-start.5 = (bf16[8,256,128]{2,1,0:T(8,128)(2,1)S(1)}, bf16[8,256,128]{2,1,0:T(8,128)(2,1)S(1)}, u32[]{:S(2)}, u32[]{:S(2)}) collective-permute-start(bf16[8,256,128]{2,1,0:T(8,128)(2,1)S(1)} %get-tuple-element.15), channel_id=1, source_target_pairs={{0,48},{16,0},{32,16},{48,32},{64,112},{80,64},{96,80},{112,96},{1... | collective-permute-start | bytes 1572872 | tf_op jit(solution)/shard_map/ppermute | solution.py:327
  72.8 41.0 %copy-start = (bf16[1,1,512,128]{3,2,1,0:T(8,128)(2,1)S(1)}, bf16[1,1,512,128]{3,2,1,0:T(8,128)(2,1)}, u32[]{:S(2)}) copy-start(bf16[1,1,512,128]{3,2,1,0:T(8,128)(2,1)} %param.9) | copy-start | bytes 393220
  72.8 41.0 %copy-start.1 = (bf16[128,128]{1,0:T(8,128)(2,1)S(1)}, bf16[128,128]{1,0:T(8,128)(2,1)}, u32[]{:S(2)}) copy-start(bf16[128,128]{1,0:T(8,128)(2,1)} %weight.1) | copy-start | bytes 98308
  153.3 127.7 %all-to-all-start.3 = ((bf16[32,256,128]{2,1,0:T(8,128)(2,1)}), bf16[32,256,128]{2,1,0:T(8,128)(2,1)S(1)}, u32[]{:S(2)}, u32[]{:S(2)}) async-start(bf16[32,256,128]{2,1,0:T(8,128)(2,1)} %shard_map.109), calls=%async_computation.3 | async-start | bytes 4194304 | tf_op jit(solution)/shard_map/all_to_all | solution.py:313
  158.3 6.2 %collective-permute-start.6 = (f32[64,128]{1,0:T(8,128)S(1)}, f32[64,128]{1,0:T(8,128)S(1)}, u32[]{:S(2)}, u32[]{:S(2)}) collective-permute-start(f32[64,128]{1,0:T(8,128)S(1)} %slice_select_fusion), channel_id=1, source_target_pairs={{0,16},{16,0},{32,48},{48,32},{64,80},{80,64},{96,112},{112,96},{1... | collective-permute-start | bytes 98312 | tf_op jit(solution)/shard_map/ppermute | solution.py:317
  164.5 7.3 %collective-permute-start.7 = (f32[32,128]{1,0:T(8,128)S(1)}, f32[32,128]{1,0:T(8,128)S(1)}, u32[]{:S(2)}, u32[]{:S(2)}) collective-permute-start(f32[32,128]{1,0:T(8,128)S(1)} %slice_select_fusion.1), channel_id=1, source_target_pairs={{0,32},{16,48},{32,0},{48,16},{64,96},{80,112},{96,64},{112,80},{1... | collective-permute-start | bytes 49160 | tf_op jit(solution)/shard_map/ppermute | solution.py:317
  171.8 33.8 %collective-permute-start.8 = (f32[32,128]{1,0:T(8,128)S(1)}, f32[32,128]{1,0:T(8,128)S(1)}, u32[]{:S(2)}, u32[]{:S(2)}) collective-permute-start(f32[32,128]{1,0:T(8,128)S(1)} %select_add_fusion.1), channel_id=1, source_target_pairs={{0,64},{16,80},{32,96},{48,112},{64,0},{80,16},{96,32},{112,48},{1... | collective-permute-start | bytes 49160 | tf_op jit(solution)/shard_map/ppermute | solution.py:317
  205.7 7.0 %collective-permute-start.9 = (f32[32,128]{1,0:T(8,128)S(1)}, f32[32,128]{1,0:T(8,128)S(1)}, u32[]{:S(2)}, u32[]{:S(2)}) collective-permute-start(f32[32,128]{1,0:T(8,128)S(1)} %add.31), channel_id=1, source_target_pairs={{0,128},{16,144},{32,160},{48,176},{64,192},{80,208},{96,224},{112... | collective-permute-start | bytes 49160 | tf_op jit(solution)/shard_map/ppermute | solution.py:317
  212.7 9.5 %collective-permute-start.10 = (f32[32,128]{1,0:T(8,128)S(1)}, f32[32,128]{1,0:T(8,128)S(1)}, u32[]{:S(2)}, u32[]{:S(2)}) collective-permute-start(f32[32,128]{1,0:T(8,128)S(1)} %add.32), channel_id=1, source_target_pairs={{0,256},{16,272},{32,288},{48,304},{64,320},{80,336},{96,352},{112... | collective-permute-start | bytes 49160 | tf_op jit(solution)/shard_map/ppermute | solution.py:317
  222.2 3.1 %collective-permute-start.11 = (f32[32,128]{1,0:T(8,128)S(1)}, f32[32,128]{1,0:T(8,128)S(1)}, u32[]{:S(2)}, u32[]{:S(2)}) collective-permute-start(f32[32,128]{1,0:T(8,128)S(1)} %add.33), channel_id=1, source_target_pairs={{0,1},{1,0},{2,3},{3,2},{4,5},{5,4},{6,7},{7,6},{8,9},{9,8},{10,11... | collective-permute-start | bytes 49160 | tf_op jit(solution)/shard_map/ppermute | solution.py:317
  225.3 5.6 %collective-permute-start.12 = (f32[32,128]{1,0:T(8,128)S(1)}, f32[32,128]{1,0:T(8,128)S(1)}, u32[]{:S(2)}, u32[]{:S(2)}) collective-permute-start(f32[32,128]{1,0:T(8,128)S(1)} %add.34), channel_id=1, source_target_pairs={{0,2},{1,3},{2,0},{3,1},{4,6},{5,7},{6,4},{7,5},{8,10},{9,11},{10,... | collective-permute-start | bytes 49160 | tf_op jit(solution)/shard_map/ppermute | solution.py:317
  230.9 6.5 %collective-permute-start.13 = (f32[32,128]{1,0:T(8,128)S(1)}, f32[32,128]{1,0:T(8,128)S(1)}, u32[]{:S(2)}, u32[]{:S(2)}) collective-permute-start(f32[32,128]{1,0:T(8,128)S(1)} %add.35), channel_id=1, source_target_pairs={{0,4},{1,5},{2,6},{3,7},{4,0},{5,1},{6,2},{7,3},{8,12},{9,13},{10,... | collective-permute-start | bytes 49160 | tf_op jit(solution)/shard_map/ppermute | solution.py:317
  237.4 9.5 %collective-permute-start.14 = (f32[32,128]{1,0:T(8,128)S(1)}, f32[32,128]{1,0:T(8,128)S(1)}, u32[]{:S(2)}, u32[]{:S(2)}) collective-permute-start(f32[32,128]{1,0:T(8,128)S(1)} %add.36), channel_id=1, source_target_pairs={{0,8},{1,9},{2,10},{3,11},{4,12},{5,13},{6,14},{7,15},{8,0},{9,1},... | collective-permute-start | bytes 49160 | tf_op jit(solution)/shard_map/ppermute | solution.py:317
  247.0 7.1 %collective-permute-start.15 = (f32[32,128]{1,0:T(8,128)S(1)}, f32[32,128]{1,0:T(8,128)S(1)}, u32[]{:S(2)}, u32[]{:S(2)}) collective-permute-start(f32[32,128]{1,0:T(8,128)S(1)} %add.37), channel_id=1, source_target_pairs={{0,32},{16,48},{32,0},{48,16},{64,96},{80,112},{96,64},{112,80},{1... | collective-permute-start | bytes 49160 | tf_op jit(solution)/shard_map/ppermute | solution.py:317
  254.1 26.2 %collective-permute-start.16 = (f32[64,128]{1,0:T(8,128)S(1)}, f32[64,128]{1,0:T(8,128)S(1)}, u32[]{:S(2)}, u32[]{:S(2)}) collective-permute-start(f32[64,128]{1,0:T(8,128)S(1)} %pad_maximum_fusion), channel_id=1, source_target_pairs={{0,16},{16,0},{32,48},{48,32},{64,80},{80,64},{96,112},{112,96},{1... | collective-permute-start | bytes 98312 | tf_op jit(solution)/shard_map/ppermute | solution.py:317
  258.9 5.5 %collective-permute-start.17 = (s32[4,128]{1,0:T(4,128)S(1)}, s32[4,128]{1,0:T(4,128)S(1)}, u32[]{:S(2)}, u32[]{:S(2)}) collective-permute-start(s32[4,128]{1,0:T(4,128)S(1)} %pad_add_fusion), channel_id=1, source_target_pairs={{0,64},{16,80},{32,96},{48,112},{64,0},{80,16},{96,32},{112,48},{1... | collective-permute-start | bytes 6152 | tf_op jit(solution)/shard_map/ppermute | solution.py:317
  264.4 6.4 %collective-permute-start.18 = (s32[8,128]{1,0:T(8,128)S(1)}, s32[8,128]{1,0:T(8,128)S(1)}, u32[]{:S(2)}, u32[]{:S(2)}) collective-permute-start(s32[8,128]{1,0:T(8,128)S(1)} %concatenate.24), channel_id=1, source_target_pairs={{0,128},{16,144},{32,160},{48,176},{64,192},{80,208},{96,224},{112... | collective-permute-start | bytes 12296 | tf_op jit(solution)/shard_map/ppermute | solution.py:317
  270.8 9.4 %collective-permute-start.19 = (s32[16,128]{1,0:T(8,128)S(1)}, s32[16,128]{1,0:T(8,128)S(1)}, u32[]{:S(2)}, u32[]{:S(2)}) collective-permute-start(s32[16,128]{1,0:T(8,128)S(1)} %concatenate.25), channel_id=1, source_target_pairs={{0,256},{16,272},{32,288},{48,304},{64,320},{80,336},{96,352},{112... | collective-permute-start | bytes 24584 | tf_op jit(solution)/shard_map/ppermute | solution.py:317

commit v8 on v7

--- a/solution.py
+++ b/solution.py
@@ -47,20 +47,32 @@
         copy.wait()
 
 
+def own_kernel(me, *refs):
+    peers = NX - 1
+    tables, feats, outs = refs[:peers], refs[peers], refs[peers + 1 :]
+    blk = outs[0].shape[0] // 2
+    for d in range(peers):
+        for k in range(2):
+            start = pl.multiple_of(tables[d][0, 2 * me[0, 0] + k] * blk, blk)
+            outs[d][k * blk : (k + 1) * blk, :] = feats[pl.ds(start, blk), :]
+
+
 def pick_kernel(me, *refs):
     peers = NX - 1
     tables, column, outs = refs[:peers], refs[peers], refs[peers + 1 :]
     blk = outs[0].shape[1] // 2
-    mine = me[0, 0] & (NX - 1)
-
-    def step(y, carry):
+    n = column.shape[0]
+    mine, row = me[0, 0] & (NX - 1), me[0, 0] >> 2
+
+    def step(i, carry):
+        y = (row + i + 1) & (n - 1)
         for d in range(peers):
             for k in range(2):
                 start = pl.multiple_of(tables[d][0, 2 * (NX * y + mine) + k] * blk, blk)
-                outs[d][y, k * blk : (k + 1) * blk, :] = column[y, pl.ds(start, blk), :]
-        return carry
-
-    lax.fori_loop(0, column.shape[0], step, 0)
+                outs[d][i, k * blk : (k + 1) * blk, :] = column[y, pl.ds(start, blk), :]
+        return carry
+
+    lax.fori_loop(0, n - 1, step, 0)
 
 
 def shipper(held, out, sems):
@@ -83,9 +95,10 @@
 
 
 def plan_kernel(col_slots, me, slots, live, plan):
-    mine = me[0, 0] & (NX - 1)
+    mine, row = me[0, 0] & (NX - 1), me[0, 0] >> 2
     shift = col_slots.bit_length() - 1
     spare = plan.shape[1] - 1
+    n_y = col_slots // (2 * NX)
 
     def scan(b, counts):
         slot = slots[0, b]
@@ -93,7 +106,8 @@
         piece = (mine - (col >> 1)) & (NX - 1)
         late = piece & 1
         count = jnp.where(late == 1, counts[1], counts[0])
-        feat = (piece >> 1) * (col_slots // NX) + ((col >> 3) << 1) + (col & 1)
+        turn = ((col >> 3) - row) & (n_y - 1)
+        feat = (piece >> 1) * (2 * n_y) + 2 * turn + (col & 1)
         plan[3 * late, count] = b
         plan[3 * late + 1, count] = feat
         plan[3 * late + 2, count] = slot >> shift
@@ -128,10 +142,10 @@
 
 
 def early_kernel(
-    me, plan, need, source, column, far, acc, late, values, arrived, sems, late_sems
+    me, plan, need, source, column, far0, far, acc, late, values, arrived, sems, late_sems
 ):
     blk = values.shape[1]
-    mine = me[0, 0] & (NX - 1)
+    mine, row = me[0, 0] & (NX - 1), me[0, 0] >> 2
     spare = plan.shape[1] - 1
     groups, late_groups = plan[0, spare], plan[3, spare]
 
@@ -154,16 +168,18 @@
     lax.fori_loop(0, groups, starter(0, values, sems), 0)
     lax.fori_loop(0, late_groups, starter(3, late, late_sems), 0)
     acc[...] = jnp.zeros_like(acc)
-    count = far.shape[0]
-
-    def place(y, carry):
+    n_y = column.shape[0]
+
+    def place(turn, carry):
+        y = (row + turn) & (n_y - 1)
         for k in range(2):
             start = pl.multiple_of(need[0, 2 * (NX * y + mine) + k] * blk, blk)
-            arrived[2 * y + k] = column[y, pl.ds(start, blk), :]
-            arrived[count + 2 * y + k] = far[2 * y + k]
-        return carry
-
-    lax.fori_loop(0, column.shape[0], place, 0)
+            arrived[2 * turn + k] = column[y, pl.ds(start, blk), :]
+        return carry
+
+    lax.fori_loop(0, n_y, place, 0)
+    arrived[2 * n_y : 2 * n_y + 2] = far0[...]
+    arrived[2 * n_y + 2 :] = far[...]
     accumulate(plan, 0, groups, waiter(values, sems), values, arrived, acc)
     done = waiter(late, late_sems)
 
@@ -174,14 +190,18 @@
     lax.fori_loop(0, late_groups, finish, 0)
 
 
-def late_kernel(plan, row_need, early, values, left, right, out, acc, arrived, held, out_sems):
+def late_kernel(
+    plan, row_need, early, values, left0, left, right0, right, out, acc, arrived, held, out_sems
+):
     n, _, width = out.shape
     blk = values.shape[1]
     spare = plan.shape[1] - 1
     acc[...] = jnp.zeros_like(acc)
-    count = left.shape[0]
-    arrived[:count] = left[...]
-    arrived[count:] = right[...]
+    count = 2 + left.shape[0]
+    arrived[:2] = left0[...]
+    arrived[2:count] = left[...]
+    arrived[count : count + 2] = right0[...]
+    arrived[count + 2 :] = right[...]
     accumulate(plan, 3, plan[3, spare], lambda g: None, values, arrived, acc)
     sub = lax.broadcasted_iota(jnp.int32, (EXTRA, width), 0)
     ship = shipper(held, out, out_sems)
@@ -345,9 +365,20 @@
     )
     need = jnp.pad(col_need[0, 0].reshape(1, -1), ((0, 0), (0, 128 - col_slots)))
     tables = [along_x(need, -d) for d in range(1, NX)]
+    own = call(
+        own_kernel,
+        [jax.ShapeDtypeStruct((cap * blk, width), BF16) for _ in tables],
+        [SMEM, *[SMEM for _ in tables], VMEM],
+        moved=1 << 20,
+        grant=PICK_GRANT,
+    )(me, *tables, features[0, 0])
+    firsts = {}
+    for d in (2, 1, 3):
+        first = along_x(own[d - 1], d)
+        firsts[d] = first.reshape(cap, blk, width)
     chosen = call(
         pick_kernel,
-        [jax.ShapeDtypeStruct((n_y, cap * blk, width), BF16) for _ in tables],
+        [jax.ShapeDtypeStruct((n_y - 1, cap * blk, width), BF16) for _ in tables],
         [SMEM, *[SMEM for _ in tables], VMEM],
         moved=4 << 20,
         grant=PICK_GRANT,
@@ -361,14 +392,14 @@
     pieces = {}
     for d in (2, 1, 3):
         piece = along_x(chosen[d - 1], d)
-        pieces[d] = piece.reshape(cap * n_y, blk, width)
+        pieces[d] = piece.reshape(cap * (n_y - 1), blk, width)
     early, late = call(
         early_kernel,
         (
             jax.ShapeDtypeStruct((row_slots + 1, blk, width), F32),
             jax.ShapeDtypeStruct(values.shape, BF16),
         ),
-        [SMEM, SMEM, SMEM, HBM, VMEM, VMEM],
+        [SMEM, SMEM, SMEM, HBM, VMEM, VMEM, VMEM],
         [
             pltpu.VMEM(values.shape, BF16),
             pltpu.VMEM((2 * cap * n_y, blk, width), BF16),
@@ -378,11 +409,11 @@
         flops=work,
         moved=8 << 20,
         grant=FORWARD_GRANT,
-    )(me, plan, need, values, column, pieces[2])
+    )(me, plan, need, values, column, firsts[2], pieces[2])
     partial = call(
         late_kernel,
         pltpu.HBM((n_cols, cap * blk + EXTRA, width), BF16),
-        [SMEM, SMEM, VMEM, VMEM, VMEM, VMEM],
+        [SMEM, SMEM, VMEM, VMEM, VMEM, VMEM, VMEM, VMEM],
         [
             pltpu.VMEM((row_slots + 1, blk, width), F32),
             pltpu.VMEM((2 * cap * n_y, blk, width), BF16),
@@ -393,7 +424,7 @@
         moved=8 << 20,
         out_spec=HBM,
         grant=FORWARD_GRANT,
-    )(plan, row_need[0, 0], early, late, pieces[1], pieces[3])
+    )(plan, row_need[0, 0], early, late, firsts[1], pieces[1], firsts[3], pieces[3])
     asked = jnp.concatenate([need, *tables], axis=0)
     bit = 1
     while bit < n_y:

time: 284 us -> 294 us (1.035)
  the two profiles are of different devices: /device:TPU:4 before, /device:TPU:40 now
where the time goes in v8:
time: 294 us; the launch traced here: 293 us
  waiting for transfers between devices  99.1 us (34%)
  starting transfers between devices  92.5 us (31%)
  blocking collectives  71.5 us (24%)
  Pallas kernels  27.1 us (9%)
    ppermute x14, waiting for transfers between devices, trade(): return lax.ppermute(array, axis, pairs)  79.2 us
    all_to_all x2, blocking collectives, swap(): return lax.all_to_all(array, axis, split_axis=0, concat_axis=0, tiled=True)  71.5 us
    ppermute x14, starting transfers between devices, trade(): return lax.ppermute(array, axis, pairs)  41.6 us
    ppermute x9, starting transfers between devices, along_x(): return lax.ppermute(array, 'gr', pairs)  31 us
    all_to_all x1, starting transfers between devices, swap(): return lax.all_to_all(array, axis, split_axis=0, concat_axis=0, tiled=True)  11 us
    ppermute x9, waiting for transfers between devices, along_x(): return lax.ppermute(array, 'gr', pairs)  10.6 us
    all_to_all x1, waiting for transfers between devices, on_device(): lax.all_to_all(copies, 'gr', split_axis=0, concat_axis=0, tiled=True, axi...  9.32 us
    all_to_all x1, starting transfers between devices, on_device(): lax.all_to_all(copies, 'gr', split_axis=0, concat_axis=0, tiled=True, axi...  8.84 us
  transfers between devices with their start and end apart: 25, of which 17 were waited for; matrix products, arithmetic and copies ran while one was open for 0% of the time, Pallas kernels for 3%

profile of v8, /device:TPU:40, one launch (start us, length us, event | category | flops | bytes accessed | tf_op | source)
XLA Modules:
  0.0 293.0 jit_solution(1549021493655439413)
XLA Ops:
  2.7 8.8 %all-to-all-start = ((bf16[8,512,128]{2,1,0:T(8,128)(2,1)}), bf16[8,512,128]{2,1,0:T(8,128)(2,1)S(1)}, u32[]{:S(2)}, u32[]{:S(2)}) async-start(bf16[8,512,128]{2,1,0:T(8,128)(2,1)} %shard_map.104), calls=%async_computation | async-start | bytes 2097152 | tf_op jit(solution)/shard_map/all_to_all | solution.py:358
  11.7 2.9 %collective-permute-start = (s32[1,128]{1,0:T(1,128)S(1)}, s32[1,128]{1,0:T(1,128)S(1)}, u32[]{:S(2)}, u32[]{:S(2)}) collective-permute-start(s32[1,128]{1,0:T(1,128)S(1)} %pad.4.need), channel_id=1, source_target_pairs={{0,48},{16,0},{32,16},{48,32},{64,112},{80,64},{96,80},{112,96},{1... | collective-permute-start | bytes 1544 | tf_op jit(solution)/shard_map/ppermute | solution.py:347
  17.4 2.8 collective-permute-start.2
  24.1 9.3 %all-to-all-done.refs_3_.column = bf16[8,512,128]{2,1,0:T(8,128)(2,1)S(1)} async-done(((bf16[8,512,128]{2,1,0:T(8,128)(2,1)}), bf16[8,512,128]{2,1,0:T(8,128)(2,1)S(1)}, u32[]{:S(2)}, u32[]{:S(2)}) %all-to-all-start) | async-done | bytes 1048608 | tf_op jit(solution)/shard_map/all_to_all | solution.py:358
  35.0 5.6 %collective-permute-start.4 = (bf16[7,256,128]{2,1,0:T(8,128)(2,1)}, bf16[7,256,128]{2,1,0:T(8,128)(2,1)S(1)}, u32[]{:S(2)}, u32[]{:S(2)}) collective-permute-start(bf16[7,256,128]{2,1,0:T(8,128)(2,1)} %get-tuple-element.15), channel_id=1, source_target_pairs={{0,32},{16,48},{32,0},{48,16},{64,96},{80,112},{96,64},{112,80},{1... | collective-permute-start | bytes 1376264 | tf_op jit(solution)/shard_map/ppermute | solution.py:347
  40.6 3.0 %collective-permute-start.8 = (bf16[7,256,128]{2,1,0:T(8,128)(2,1)}, bf16[7,256,128]{2,1,0:T(8,128)(2,1)S(1)}, u32[]{:S(2)}, u32[]{:S(2)}) collective-permute-start(bf16[7,256,128]{2,1,0:T(8,128)(2,1)} %get-tuple-element.21), channel_id=1, source_target_pairs={{0,48},{16,0},{32,16},{48,32},{64,112},{80,64},{96,80},{112,96},{1... | collective-permute-start | bytes 1376264 | tf_op jit(solution)/shard_map/ppermute | solution.py:347
  49.6 4.5 %collective-permute-start.5 = (bf16[256,128]{1,0:T(8,128)(2,1)S(1)}, bf16[256,128]{1,0:T(8,128)(2,1)S(1)}, u32[]{:S(2)}, u32[]{:S(2)}) collective-permute-start(bf16[256,128]{1,0:T(8,128)(2,1)S(1)} %get-tuple-element.18), channel_id=1, source_target_pairs={{0,16},{16,32},{32,48},{48,0},{64,80},{80,96},{96,112},{112,64},{1... | collective-permute-start | bytes 196616 | tf_op jit(solution)/shard_map/ppermute | solution.py:347
  54.1 6.7 %collective-permute-done.3 = bf16[256,128]{1,0:T(8,128)(2,1)S(1)} collective-permute-done((bf16[256,128]{1,0:T(8,128)(2,1)S(1)}, bf16[256,128]{1,0:T(8,128)(2,1)S(1)}, u32[]{:S(2)}, u32[]{:S(2)}) %collective-permute-start.3) | collective-permute-done | bytes 65568 | tf_op jit(solution)/shard_map/ppermute | solution.py:347
  60.8 4.1 %collective-permute-start.7 = (bf16[256,128]{1,0:T(8,128)(2,1)S(1)}, bf16[256,128]{1,0:T(8,128)(2,1)S(1)}, u32[]{:S(2)}, u32[]{:S(2)}) collective-permute-start(bf16[256,128]{1,0:T(8,128)(2,1)S(1)} %get-tuple-element.20), channel_id=1, source_target_pairs={{0,48},{16,0},{32,16},{48,32},{64,112},{80,64},{96,80},{112,96},{1... | collective-permute-start | bytes 196616 | tf_op jit(solution)/shard_map/ppermute | solution.py:347
  65.7 4.2 %shard_map.103.plan = s32[6,144]{1,0:T(8,128)S(1)} custom-call(s32[1,1]{1,0:T(1,128)} %bitcast.me, s32[1,128]{1,0:T(1,128)S(1)} %bitcast.27, s32[1,1]{1,0:T(1,128)S(6)} %copy.15.live), custom_call_target="tpu_custom_call" | custom-call | tf_op jit(solution)/shard_map/pallas_call | solution.py:386
  69.9 3.7 %shard_map.107 = (f32[33,128,128]{2,1,0:T(8,128)S(1)}, bf16[128,128,128]{2,1,0:T(8,128)(2,1)S(1)}) custom-call(s32[1,1]{1,0:T(1,128)} %bitcast.me, s32[6,144]{1,0:T(8,128)S(1)} %shard_map.103.plan, s32[1,128]{1,0:T(1,128)S(1)} %pad.4.need, bf16[128,128,128]{2,1,0:T(8,128)(2,1)} %bitcast.29, bf16[8,512,128]{2,1,0:T(8,128)(2,1)S(1)} %all-to-all-done.refs_3_.column, ...), custom_call_target="tpu_custom_call" | custom-call | flops 536870912 | bytes 8388608 | tf_op jit(solution)/shard_map/pallas_call | solution.py:396
  73.7 4.2 %shard_map.108 = bf16[16,272,128]{2,1,0:T(8,128)(2,1)} custom-call(s32[6,144]{1,0:T(8,128)S(1)} %shard_map.103.plan, s32[16,2]{1,0:T(8,128)S(1)} %copy.14.row_need, f32[33,128,128]{2,1,0:T(8,128)S(1)} %get-tuple-element.16.early, bf16[128,128,128]{2,1,0:T(8,128)(2,1)S(1)} %get-tuple-element.17.values, bf16[2,128,128]{2,1,0:T(8,128)(2,1)S(1)} %bitcast.24, ...), custom_call_target="tpu_custom_call" | custom-call | flops 268435456 | bytes 8388608 | tf_op jit(solution)/shard_map/pallas_call | solution.py:413
  77.9 40.7 %all_to_all.20.arrived = bf16[16,272,128]{2,1,0:T(8,128)(2,1)S(1)} all-to-all(bf16[16,272,128]{2,1,0:T(8,128)(2,1)} %shard_map.108), channel_id=1, replica_groups=mesh['gr'=32,'gc'=16] {'gc'}, dimensions={0} | all-to-all | bytes 2228224 | tf_op jit(solution)/shard_map/all_to_all | solution.py:333
  121.4 30.8 %all_to_all.21 = bf16[16,256,128]{2,1,0:T(8,128)(2,1)S(1)} all-to-all(bf16[16,256,128]{2,1,0:T(8,128)(2,1)} %get-tuple-element.24), channel_id=1, replica_groups=mesh['gr'=32,'gc'=16] {'gc'}, dimensions={0} | all-to-all | bytes 2097152 | tf_op jit(solution)/shard_map/all_to_all | solution.py:333
  152.1 6.0 %shard_map.110 = bf16[32,256,128]{2,1,0:T(8,128)(2,1)} custom-call(s32[1,128]{1,0:T(1,128)S(1)} %bitcast.28, s32[1,1]{1,0:T(1,128)S(6)} %copy.15.live, bf16[128,128,128]{2,1,0:T(8,128)(2,1)} %bitcast.30, bf16[32,128,128]{2,1,0:T(8,128)(2,1)S(1)} %bitcast.17), custom_call_target="tpu_custom_call" | custom-call | flops 536870912 | bytes 8388608 | tf_op jit(solution)/shard_map/pallas_call | solution.py:468
  158.2 11.0 %all-to-all-start.3 = ((bf16[32,256,128]{2,1,0:T(8,128)(2,1)}), bf16[32,256,128]{2,1,0:T(8,128)(2,1)S(1)}, u32[]{:S(2)}, u32[]{:S(2)}) async-start(bf16[32,256,128]{2,1,0:T(8,128)(2,1)} %shard_map.110), calls=%async_computation.3 | async-start | bytes 4194304 | tf_op jit(solution)/shard_map/all_to_all | solution.py:333
  169.2 3.4 %collective-permute-start.9 = (f32[64,128]{1,0:T(8,128)S(1)}, f32[64,128]{1,0:T(8,128)S(1)}, u32[]{:S(2)}, u32[]{:S(2)}) collective-permute-start(f32[64,128]{1,0:T(8,128)S(1)} %slice_select_fusion), channel_id=1, source_target_pairs={{0,16},{16,0},{32,48},{48,32},{64,80},{80,64},{96,112},{112,96},{1... | collective-permute-start | bytes 98312 | tf_op jit(solution)/shard_map/ppermute | solution.py:337
  172.6 6.5 %collective-permute-done.9 = f32[64,128]{1,0:T(8,128)S(1)} collective-permute-done((f32[64,128]{1,0:T(8,128)S(1)}, f32[64,128]{1,0:T(8,128)S(1)}, u32[]{:S(2)}, u32[]{:S(2)}) %collective-permute-start.9) | collective-permute-done | bytes 32800 | tf_op jit(solution)/shard_map/ppermute | solution.py:337
  179.1 3.5 %collective-permute-start.10 = (f32[32,128]{1,0:T(8,128)S(1)}, f32[32,128]{1,0:T(8,128)S(1)}, u32[]{:S(2)}, u32[]{:S(2)}) collective-permute-start(f32[32,128]{1,0:T(8,128)S(1)} %slice_select_fusion.1), channel_id=1, source_target_pairs={{0,32},{16,48},{32,0},{48,16},{64,96},{80,112},{96,64},{112,80},{1... | collective-permute-start | bytes 49160 | tf_op jit(solution)/shard_map/ppermute | solution.py:337
  182.6 4.0 %collective-permute-done.10 = f32[32,128]{1,0:T(8,128)S(1)} collective-permute-done((f32[32,128]{1,0:T(8,128)S(1)}, f32[32,128]{1,0:T(8,128)S(1)}, u32[]{:S(2)}, u32[]{:S(2)}) %collective-permute-start.10) | collective-permute-done | bytes 16416 | tf_op jit(solution)/shard_map/ppermute | solution.py:337
  186.6 6.1 %collective-permute-start.11 = (f32[32,128]{1,0:T(8,128)S(1)}, f32[32,128]{1,0:T(8,128)S(1)}, u32[]{:S(2)}, u32[]{:S(2)}) collective-permute-start(f32[32,128]{1,0:T(8,128)S(1)} %select_add_fusion.1), channel_id=1, source_target_pairs={{0,64},{16,80},{32,96},{48,112},{64,0},{80,16},{96,32},{112,48},{1... | collective-permute-start | bytes 49160 | tf_op jit(solution)/shard_map/ppermute | solution.py:337
  192.8 24.0 %collective-permute-done.11 = f32[32,128]{1,0:T(8,128)S(1)} collective-permute-done((f32[32,128]{1,0:T(8,128)S(1)}, f32[32,128]{1,0:T(8,128)S(1)}, u32[]{:S(2)}, u32[]{:S(2)}) %collective-permute-start.11) | collective-permute-done | bytes 16416 | tf_op jit(solution)/shard_map/ppermute | solution.py:337
  218.7 4.6 %collective-permute-done.12 = f32[32,128]{1,0:T(8,128)S(1)} collective-permute-done((f32[32,128]{1,0:T(8,128)S(1)}, f32[32,128]{1,0:T(8,128)S(1)}, u32[]{:S(2)}, u32[]{:S(2)}) %collective-permute-start.12) | collective-permute-done | bytes 16416 | tf_op jit(solution)/shard_map/ppermute | solution.py:337
  225.5 7.4 %collective-permute-done.13 = f32[32,128]{1,0:T(8,128)S(1)} collective-permute-done((f32[32,128]{1,0:T(8,128)S(1)}, f32[32,128]{1,0:T(8,128)S(1)}, u32[]{:S(2)}, u32[]{:S(2)}) %collective-permute-start.13) | collective-permute-done | bytes 16416 | tf_op jit(solution)/shard_map/ppermute | solution.py:337
  237.9 3.7 %collective-permute-done.15 = f32[32,128]{1,0:T(8,128)S(1)} collective-permute-done((f32[32,128]{1,0:T(8,128)S(1)}, f32[32,128]{1,0:T(8,128)S(1)}, u32[]{:S(2)}, u32[]{:S(2)}) %collective-permute-start.15) | collective-permute-done | bytes 16416 | tf_op jit(solution)/shard_map/ppermute | solution.py:337
  244.1 4.0 %collective-permute-done.16 = f32[32,128]{1,0:T(8,128)S(1)} collective-permute-done((f32[32,128]{1,0:T(8,128)S(1)}, f32[32,128]{1,0:T(8,128)S(1)}, u32[]{:S(2)}, u32[]{:S(2)}) %collective-permute-start.16) | collective-permute-done | bytes 16416 | tf_op jit(solution)/shard_map/ppermute | solution.py:337
  250.8 6.9 %collective-permute-done.17 = f32[32,128]{1,0:T(8,128)S(1)} collective-permute-done((f32[32,128]{1,0:T(8,128)S(1)}, f32[32,128]{1,0:T(8,128)S(1)}, u32[]{:S(2)}, u32[]{:S(2)}) %collective-permute-start.17) | collective-permute-done | bytes 16416 | tf_op jit(solution)/shard_map/ppermute | solution.py:337
  257.7 5.5 %collective-permute-start.18 = (f32[32,128]{1,0:T(8,128)S(1)}, f32[32,128]{1,0:T(8,128)S(1)}, u32[]{:S(2)}, u32[]{:S(2)}) collective-permute-start(f32[32,128]{1,0:T(8,128)S(1)} %add.37), channel_id=1, source_target_pairs={{0,32},{16,48},{32,0},{48,16},{64,96},{80,112},{96,64},{112,80},{1... | collective-permute-start | bytes 49160 | tf_op jit(solution)/shard_map/ppermute | solution.py:337
  264.9 3.9 %collective-permute-start.19 = (f32[64,128]{1,0:T(8,128)S(1)}, f32[64,128]{1,0:T(8,128)S(1)}, u32[]{:S(2)}, u32[]{:S(2)}) collective-permute-start(f32[64,128]{1,0:T(8,128)S(1)} %pad_maximum_fusion), channel_id=1, source_target_pairs={{0,16},{16,0},{32,48},{48,32},{64,80},{80,64},{96,112},{112,96},{1... | collective-permute-start | bytes 98312 | tf_op jit(solution)/shard_map/ppermute | solution.py:337
  270.8 3.6 %collective-permute-done.20 = s32[4,128]{1,0:T(4,128)S(1)} collective-permute-done((s32[4,128]{1,0:T(4,128)S(1)}, s32[4,128]{1,0:T(4,128)S(1)}, u32[]{:S(2)}, u32[]{:S(2)}) %collective-permute-start.20) | collective-permute-done | bytes 2080 | tf_op jit(solution)/shard_map/ppermute | solution.py:337
  276.5 4.2 %collective-permute-done.21 = s32[8,128]{1,0:T(8,128)S(1)} collective-permute-done((s32[8,128]{1,0:T(8,128)S(1)}, s32[8,128]{1,0:T(8,128)S(1)}, u32[]{:S(2)}, u32[]{:S(2)}) %collective-permute-start.21) | collective-permute-done | bytes 4128 | tf_op jit(solution)/shard_map/ppermute | solution.py:337
  282.8 7.5 %collective-permute-done.22 = s32[16,128]{1,0:T(8,128)S(1)} collective-permute-done((s32[16,128]{1,0:T(8,128)S(1)}, s32[16,128]{1,0:T(8,128)S(1)}, u32[]{:S(2)}, u32[]{:S(2)}) %collective-permute-start.22) | collective-permute-done | bytes 8224 | tf_op jit(solution)/shard_map/ppermute | solution.py:337
  (64 shorter events, 44.0 us)
Async XLA Ops:
  0.6 10.9 %copy-start.4 = (s32[1,1,32,2]{2,3,1,0:T(2,128)S(1)}, s32[1,1,32,2]{2,3,1,0:T(2,128)}, u32[]{:S(2)}) copy-start(s32[1,1,32,2]{2,3,1,0:T(2,128)} %param.15) | copy-start | bytes 772
  0.6 45.8 %copy-start = (bf16[1,1,512,128]{3,2,1,0:T(8,128)(2,1)S(1)}, bf16[1,1,512,128]{3,2,1,0:T(8,128)(2,1)}, u32[]{:S(2)}) copy-start(bf16[1,1,512,128]{3,2,1,0:T(8,128)(2,1)} %param.8) | copy-start | bytes 393220
  0.7 64.9 %copy-start.5 = (s32[1,1,16,2]{2,3,1,0:T(2,128)S(1)}, s32[1,1,16,2]{2,3,1,0:T(2,128)}, u32[]{:S(2)}) copy-start(s32[1,1,16,2]{2,3,1,0:T(2,128)} %param.14) | copy-start | bytes 388
  0.7 65.0 %copy-start.3 = (s32[1,1,128]{2,1,0:T(1,128)S(1)}, s32[1,1,128]{2,1,0:T(1,128)}, u32[]{:S(2)}) copy-start(s32[1,1,128]{2,1,0:T(1,128)} %param.12) | copy-start | bytes 1540
  2.7 30.7 %all-to-all-start = ((bf16[8,512,128]{2,1,0:T(8,128)(2,1)}), bf16[8,512,128]{2,1,0:T(8,128)(2,1)S(1)}, u32[]{:S(2)}, u32[]{:S(2)}) async-start(bf16[8,512,128]{2,1,0:T(8,128)(2,1)} %shard_map.104), calls=%async_computation | async-start | bytes 2097152 | tf_op jit(solution)/shard_map/all_to_all | solution.py:358
  11.7 8.5 %collective-permute-start = (s32[1,128]{1,0:T(1,128)S(1)}, s32[1,128]{1,0:T(1,128)S(1)}, u32[]{:S(2)}, u32[]{:S(2)}) collective-permute-start(s32[1,128]{1,0:T(1,128)S(1)} %pad.4.need), channel_id=1, source_target_pairs={{0,48},{16,0},{32,16},{48,32},{64,112},{80,64},{96,80},{112,96},{1... | collective-permute-start | bytes 1544 | tf_op jit(solution)/shard_map/ppermute | solution.py:347
  14.7 7.0 %collective-permute-start.1 = (s32[1,128]{1,0:T(1,128)S(1)}, s32[1,128]{1,0:T(1,128)S(1)}, u32[]{:S(2)}, u32[]{:S(2)}) collective-permute-start(s32[1,128]{1,0:T(1,128)S(1)} %pad.4.need), channel_id=1, source_target_pairs={{0,32},{16,48},{32,0},{48,16},{64,96},{80,112},{96,64},{112,80},{1... | collective-permute-start | bytes 1544 | tf_op jit(solution)/shard_map/ppermute | solution.py:347
  17.4 6.7 %collective-permute-start.2 = (s32[1,128]{1,0:T(1,128)S(1)}, s32[1,128]{1,0:T(1,128)S(1)}, u32[]{:S(2)}, u32[]{:S(2)}) collective-permute-start(s32[1,128]{1,0:T(1,128)S(1)} %pad.4.need), channel_id=1, source_target_pairs={{0,16},{16,32},{32,48},{48,0},{64,80},{80,96},{96,112},{112,64},{1... | collective-permute-start | bytes 1544 | tf_op jit(solution)/shard_map/ppermute | solution.py:347
  35.0 34.9 %collective-permute-start.4 = (bf16[7,256,128]{2,1,0:T(8,128)(2,1)}, bf16[7,256,128]{2,1,0:T(8,128)(2,1)S(1)}, u32[]{:S(2)}, u32[]{:S(2)}) collective-permute-start(bf16[7,256,128]{2,1,0:T(8,128)(2,1)} %get-tuple-element.15), channel_id=1, source_target_pairs={{0,32},{16,48},{32,0},{48,16},{64,96},{80,112},{96,64},{112,80},{1... | collective-permute-start | bytes 1376264 | tf_op jit(solution)/shard_map/ppermute | solution.py:347
  40.6 33.0 %collective-permute-start.8 = (bf16[7,256,128]{2,1,0:T(8,128)(2,1)}, bf16[7,256,128]{2,1,0:T(8,128)(2,1)S(1)}, u32[]{:S(2)}, u32[]{:S(2)}) collective-permute-start(bf16[7,256,128]{2,1,0:T(8,128)(2,1)} %get-tuple-element.21), channel_id=1, source_target_pairs={{0,48},{16,0},{32,16},{48,32},{64,112},{80,64},{96,80},{112,96},{1... | collective-permute-start | bytes 1376264 | tf_op jit(solution)/shard_map/ppermute | solution.py:347
  43.7 30.0 %collective-permute-start.6 = (bf16[7,256,128]{2,1,0:T(8,128)(2,1)S(1)}, bf16[7,256,128]{2,1,0:T(8,128)(2,1)S(1)}, u32[]{:S(2)}, u32[]{:S(2)}) collective-permute-start(bf16[7,256,128]{2,1,0:T(8,128)(2,1)S(1)} %get-tuple-element.19), channel_id=1, source_target_pairs={{0,16},{16,32},{32,48},{48,0},{64,80},{80,96},{96,112},{112,64},{1... | collective-permute-start | bytes 1376264 | tf_op jit(solution)/shard_map/ppermute | solution.py:347
  47.1 13.8 %collective-permute-start.3 = (bf16[256,128]{1,0:T(8,128)(2,1)S(1)}, bf16[256,128]{1,0:T(8,128)(2,1)S(1)}, u32[]{:S(2)}, u32[]{:S(2)}) collective-permute-start(bf16[256,128]{1,0:T(8,128)(2,1)S(1)} %get-tuple-element.14), channel_id=1, source_target_pairs={{0,32},{16,48},{32,0},{48,16},{64,96},{80,112},{96,64},{112,80},{1... | collective-permute-start | bytes 196616 | tf_op jit(solution)/shard_map/ppermute | solution.py:347
  49.6 24.0 %collective-permute-start.5 = (bf16[256,128]{1,0:T(8,128)(2,1)S(1)}, bf16[256,128]{1,0:T(8,128)(2,1)S(1)}, u32[]{:S(2)}, u32[]{:S(2)}) collective-permute-start(bf16[256,128]{1,0:T(8,128)(2,1)S(1)} %get-tuple-element.18), channel_id=1, source_target_pairs={{0,16},{16,32},{32,48},{48,0},{64,80},{80,96},{96,112},{112,64},{1... | collective-permute-start | bytes 196616 | tf_op jit(solution)/shard_map/ppermute | solution.py:347
  60.8 12.8 %collective-permute-start.7 = (bf16[256,128]{1,0:T(8,128)(2,1)S(1)}, bf16[256,128]{1,0:T(8,128)(2,1)S(1)}, u32[]{:S(2)}, u32[]{:S(2)}) collective-permute-start(bf16[256,128]{1,0:T(8,128)(2,1)S(1)} %get-tuple-element.20), channel_id=1, source_target_pairs={{0,48},{16,0},{32,16},{48,32},{64,112},{80,64},{96,80},{112,96},{1... | collective-permute-start | bytes 196616 | tf_op jit(solution)/shard_map/ppermute | solution.py:347
  77.9 40.7 %copy-start.1 = (bf16[1,1,512,128]{3,2,1,0:T(8,128)(2,1)S(1)}, bf16[1,1,512,128]{3,2,1,0:T(8,128)(2,1)}, u32[]{:S(2)}) copy-start(bf16[1,1,512,128]{3,2,1,0:T(8,128)(2,1)} %param.9) | copy-start | bytes 393220
  77.9 40.7 %copy-start.2 = (bf16[128,128]{1,0:T(8,128)(2,1)S(1)}, bf16[128,128]{1,0:T(8,128)(2,1)}, u32[]{:S(2)}) copy-start(bf16[128,128]{1,0:T(8,128)(2,1)} %weight.1) | copy-start | bytes 98308
  158.2 132.8 %all-to-all-start.3 = ((bf16[32,256,128]{2,1,0:T(8,128)(2,1)}), bf16[32,256,128]{2,1,0:T(8,128)(2,1)S(1)}, u32[]{:S(2)}, u32[]{:S(2)}) async-start(bf16[32,256,128]{2,1,0:T(8,128)(2,1)} %shard_map.110), calls=%async_computation.3 | async-start | bytes 4194304 | tf_op jit(solution)/shard_map/all_to_all | solution.py:333
  169.2 9.9 %collective-permute-start.9 = (f32[64,128]{1,0:T(8,128)S(1)}, f32[64,128]{1,0:T(8,128)S(1)}, u32[]{:S(2)}, u32[]{:S(2)}) collective-permute-start(f32[64,128]{1,0:T(8,128)S(1)} %slice_select_fusion), channel_id=1, source_target_pairs={{0,16},{16,0},{32,48},{48,32},{64,80},{80,64},{96,112},{112,96},{1... | collective-permute-start | bytes 98312 | tf_op jit(solution)/shard_map/ppermute | solution.py:337
  179.1 7.5 %collective-permute-start.10 = (f32[32,128]{1,0:T(8,128)S(1)}, f32[32,128]{1,0:T(8,128)S(1)}, u32[]{:S(2)}, u32[]{:S(2)}) collective-permute-start(f32[32,128]{1,0:T(8,128)S(1)} %slice_select_fusion.1), channel_id=1, source_target_pairs={{0,32},{16,48},{32,0},{48,16},{64,96},{80,112},{96,64},{112,80},{1... | collective-permute-start | bytes 49160 | tf_op jit(solution)/shard_map/ppermute | solution.py:337
  186.6 30.1 %collective-permute-start.11 = (f32[32,128]{1,0:T(8,128)S(1)}, f32[32,128]{1,0:T(8,128)S(1)}, u32[]{:S(2)}, u32[]{:S(2)}) collective-permute-start(f32[32,128]{1,0:T(8,128)S(1)} %select_add_fusion.1), channel_id=1, source_target_pairs={{0,64},{16,80},{32,96},{48,112},{64,0},{80,16},{96,32},{112,48},{1... | collective-permute-start | bytes 49160 | tf_op jit(solution)/shard_map/ppermute | solution.py:337
  216.7 6.5 %collective-permute-start.12 = (f32[32,128]{1,0:T(8,128)S(1)}, f32[32,128]{1,0:T(8,128)S(1)}, u32[]{:S(2)}, u32[]{:S(2)}) collective-permute-start(f32[32,128]{1,0:T(8,128)S(1)} %add.31), channel_id=1, source_target_pairs={{0,128},{16,144},{32,160},{48,176},{64,192},{80,208},{96,224},{112... | collective-permute-start | bytes 49160 | tf_op jit(solution)/shard_map/ppermute | solution.py:337
  223.3 9.7 %collective-permute-start.13 = (f32[32,128]{1,0:T(8,128)S(1)}, f32[32,128]{1,0:T(8,128)S(1)}, u32[]{:S(2)}, u32[]{:S(2)}) collective-permute-start(f32[32,128]{1,0:T(8,128)S(1)} %add.32), channel_id=1, source_target_pairs={{0,256},{16,272},{32,288},{48,304},{64,320},{80,336},{96,352},{112... | collective-permute-start | bytes 49160 | tf_op jit(solution)/shard_map/ppermute | solution.py:337
  232.9 3.1 %collective-permute-start.14 = (f32[32,128]{1,0:T(8,128)S(1)}, f32[32,128]{1,0:T(8,128)S(1)}, u32[]{:S(2)}, u32[]{:S(2)}) collective-permute-start(f32[32,128]{1,0:T(8,128)S(1)} %add.33), channel_id=1, source_target_pairs={{0,1},{1,0},{2,3},{3,2},{4,5},{5,4},{6,7},{7,6},{8,9},{9,8},{10,11... | collective-permute-start | bytes 49160 | tf_op jit(solution)/shard_map/ppermute | solution.py:337
  236.0 5.6 %collective-permute-start.15 = (f32[32,128]{1,0:T(8,128)S(1)}, f32[32,128]{1,0:T(8,128)S(1)}, u32[]{:S(2)}, u32[]{:S(2)}) collective-permute-start(f32[32,128]{1,0:T(8,128)S(1)} %add.34), channel_id=1, source_target_pairs={{0,2},{1,3},{2,0},{3,1},{4,6},{5,7},{6,4},{7,5},{8,10},{9,11},{10,... | collective-permute-start | bytes 49160 | tf_op jit(solution)/shard_map/ppermute | solution.py:337
  241.6 6.5 %collective-permute-start.16 = (f32[32,128]{1,0:T(8,128)S(1)}, f32[32,128]{1,0:T(8,128)S(1)}, u32[]{:S(2)}, u32[]{:S(2)}) collective-permute-start(f32[32,128]{1,0:T(8,128)S(1)} %add.35), channel_id=1, source_target_pairs={{0,4},{1,5},{2,6},{3,7},{4,0},{5,1},{6,2},{7,3},{8,12},{9,13},{10,... | collective-permute-start | bytes 49160 | tf_op jit(solution)/shard_map/ppermute | solution.py:337
  248.2 9.5 %collective-permute-start.17 = (f32[32,128]{1,0:T(8,128)S(1)}, f32[32,128]{1,0:T(8,128)S(1)}, u32[]{:S(2)}, u32[]{:S(2)}) collective-permute-start(f32[32,128]{1,0:T(8,128)S(1)} %add.36), channel_id=1, source_target_pairs={{0,8},{1,9},{2,10},{3,11},{4,12},{5,13},{6,14},{7,15},{8,0},{9,1},... | collective-permute-start | bytes 49160 | tf_op jit(solution)/shard_map/ppermute | solution.py:337
  257.7 7.2 %collective-permute-start.18 = (f32[32,128]{1,0:T(8,128)S(1)}, f32[32,128]{1,0:T(8,128)S(1)}, u32[]{:S(2)}, u32[]{:S(2)}) collective-permute-start(f32[32,128]{1,0:T(8,128)S(1)} %add.37), channel_id=1, source_target_pairs={{0,32},{16,48},{32,0},{48,16},{64,96},{80,112},{96,64},{112,80},{1... | collective-permute-start | bytes 49160 | tf_op jit(solution)/shard_map/ppermute | solution.py:337
  264.9 25.3 %collective-permute-start.19 = (f32[64,128]{1,0:T(8,128)S(1)}, f32[64,128]{1,0:T(8,128)S(1)}, u32[]{:S(2)}, u32[]{:S(2)}) collective-permute-start(f32[64,128]{1,0:T(8,128)S(1)} %pad_maximum_fusion), channel_id=1, source_target_pairs={{0,16},{16,0},{32,48},{48,32},{64,80},{80,64},{96,112},{112,96},{1... | collective-permute-start | bytes 98312 | tf_op jit(solution)/shard_map/ppermute | solution.py:337
  268.9 5.5 %collective-permute-start.20 = (s32[4,128]{1,0:T(4,128)S(1)}, s32[4,128]{1,0:T(4,128)S(1)}, u32[]{:S(2)}, u32[]{:S(2)}) collective-permute-start(s32[4,128]{1,0:T(4,128)S(1)} %pad_add_fusion), channel_id=1, source_target_pairs={{0,64},{16,80},{32,96},{48,112},{64,0},{80,16},{96,32},{112,48},{1... | collective-permute-start | bytes 6152 | tf_op jit(solution)/shard_map/ppermute | solution.py:337
  274.4 6.4 %collective-permute-start.21 = (s32[8,128]{1,0:T(8,128)S(1)}, s32[8,128]{1,0:T(8,128)S(1)}, u32[]{:S(2)}, u32[]{:S(2)}) collective-permute-start(s32[8,128]{1,0:T(8,128)S(1)} %concatenate.24), channel_id=1, source_target_pairs={{0,128},{16,144},{32,160},{48,176},{64,192},{80,208},{96,224},{112... | collective-permute-start | bytes 12296 | tf_op jit(solution)/shard_map/ppermute | solution.py:337
  280.8 9.4 %collective-permute-start.22 = (s32[16,128]{1,0:T(8,128)S(1)}, s32[16,128]{1,0:T(8,128)S(1)}, u32[]{:S(2)}, u32[]{:S(2)}) collective-permute-start(s32[16,128]{1,0:T(8,128)S(1)} %concatenate.25), channel_id=1, source_target_pairs={{0,256},{16,272},{32,288},{48,304},{64,320},{80,336},{96,352},{112... | collective-permute-start | bytes 24584 | tf_op jit(solution)/shard_map/ppermute | solution.py:337

commit v9 on v8

--- a/solution.py
+++ b/solution.py
@@ -12,7 +12,7 @@
 EXTRA = 16
 NX = 4
 GROUP = 8
-WIDE = 16
+WIDE = 32
 BATCH = 2
 PARTS = 4
 ROWS = 32
@@ -124,21 +124,24 @@
 
 
 def accumulate(plan, first, groups, ready, values, feats, acc):
-    def group(g, carry):
-        ready(g)
-        for start in range(0, GROUP, BATCH):
-            terms = []
-            for u in range(start, start + BATCH):
-                b = g * GROUP + u
-                term = jnp.dot(
-                    values[b], feats[plan[first + 1, b]], preferred_element_type=F32
-                )
-                terms.append((plan[first + 2, b], term))
-            for row, term in terms:
-                acc[row] += term
-        return carry
-
-    lax.fori_loop(0, groups, group, 0)
+    def take(g, count):
+        for part in range(count):
+            ready(g + part)
+        for u in range(count * GROUP):
+            b = g * GROUP + u
+            term = jnp.dot(values[b], feats[plan[first + 1, b]], preferred_element_type=F32)
+            acc[plan[first + 2, b]] += term
+
+    def pair(g, carry):
+        take(2 * g, 2)
+        return carry
+
+    def single(g, carry):
+        take(groups - 1, 1)
+        return carry
+
+    lax.fori_loop(0, groups >> 1, pair, 0)
+    lax.fori_loop(0, groups & 1, single, 0)
 
 
 def early_kernel(
@@ -297,23 +300,25 @@
         ship(r)
 
 
-def final_kernel(me, asked, arrived, out, acc):
+def final_kernel(me, asked, arrived, out, acc, more):
     n, rows, _ = arrived.shape
     blk = rows // 2
     mine = me[0, 0]
     acc[...] = jnp.zeros_like(acc)
+    more[...] = jnp.zeros_like(more)
 
     def step(r, carry):
         ring = (r - mine) & (NX - 1)
         place = ((r ^ mine) & ~(NX - 1)) | ring
-        for k in range(2):
-            term = arrived[r, k * blk : (k + 1) * blk, :].astype(F32)
-            acc[asked[place, 2 * mine + k]] += term
-        return carry
-
-    lax.fori_loop(0, n, step, 0, unroll=2)
+        first = arrived[r, :blk, :].astype(F32)
+        second = arrived[r, blk:, :].astype(F32)
+        acc[asked[place, 2 * mine]] += first
+        more[asked[place, 2 * mine + 1]] += second
+        return carry
+
+    lax.fori_loop(0, n, step, 0, unroll=4)
     for q in range(acc.shape[0]):
-        out[q * blk : (q + 1) * blk, :] = acc[q].astype(BF16)
+        out[q * blk : (q + 1) * blk, :] = (acc[q] + more[q]).astype(BF16)
 
 
 def on_device(features, out_grad, weight, block_values, block_slot, live_count, row_need, col_need):
@@ -486,7 +491,7 @@
         final_kernel,
         jax.ShapeDtypeStruct((local, width), BF16),
         [SMEM, SMEM, VMEM],
-        [pltpu.VMEM((per_dev, blk, width), F32)],
+        [pltpu.VMEM((per_dev, blk, width), F32), pltpu.VMEM((per_dev, blk, width), F32)],
         moved=4 << 20,
     )(me, asked, returned)
     return (

time: 294 us -> 292 us (level)
  no operation moved by 1% of the time
where the time goes in v9:
time: 292 us; the launch traced here: 291 us
  waiting for transfers between devices  96.8 us (33%)
  starting transfers between devices  94.8 us (32%)
  blocking collectives  71.4 us (24%)
  Pallas kernels  25.4 us (9%)
    ppermute x14, waiting for transfers between devices, trade(): return lax.ppermute(array, axis, pairs)  76.8 us
    all_to_all x2, blocking collectives, swap(): return lax.all_to_all(array, axis, split_axis=0, concat_axis=0, tiled=True)  71.4 us
    ppermute x14, starting transfers between devices, trade(): return lax.ppermute(array, axis, pairs)  44 us
    ppermute x9, starting transfers between devices, along_x(): return lax.ppermute(array, 'gr', pairs)  31 us
    all_to_all x1, starting transfers between devices, swap(): return lax.all_to_all(array, axis, split_axis=0, concat_axis=0, tiled=True)  11 us
    ppermute x9, waiting for transfers between devices, along_x(): return lax.ppermute(array, 'gr', pairs)  10.6 us
    all_to_all x1, waiting for transfers between devices, on_device(): lax.all_to_all(copies, 'gr', split_axis=0, concat_axis=0, tiled=True, axi...  9.32 us
    all_to_all x1, starting transfers between devices, on_device(): lax.all_to_all(copies, 'gr', split_axis=0, concat_axis=0, tiled=True, axi...  8.84 us
  transfers between devices with their start and end apart: 25, of which 17 were waited for; matrix products, arithmetic and copies ran while one was open for 0% of the time, Pallas kernels for 3%

profile of v9, /device:TPU:40, one launch (start us, length us, event | category | flops | bytes accessed | tf_op | source)
XLA Modules:
  0.0 291.2 jit_solution(7926657417400945777)
XLA Ops:
  2.7 8.8 %all-to-all-start = ((bf16[8,512,128]{2,1,0:T(8,128)(2,1)}), bf16[8,512,128]{2,1,0:T(8,128)(2,1)S(1)}, u32[]{:S(2)}, u32[]{:S(2)}) async-start(bf16[8,512,128]{2,1,0:T(8,128)(2,1)} %shard_map.104), calls=%async_computation | async-start | bytes 2097152 | tf_op jit(solution)/shard_map/all_to_all | solution.py:363
  24.1 9.3 %all-to-all-done.refs_3_.column = bf16[8,512,128]{2,1,0:T(8,128)(2,1)S(1)} async-done(((bf16[8,512,128]{2,1,0:T(8,128)(2,1)}), bf16[8,512,128]{2,1,0:T(8,128)(2,1)S(1)}, u32[]{:S(2)}, u32[]{:S(2)}) %all-to-all-start) | async-done | bytes 1048608 | tf_op jit(solution)/shard_map/all_to_all | solution.py:363
  35.0 5.6 %collective-permute-start.4 = (bf16[7,256,128]{2,1,0:T(8,128)(2,1)}, bf16[7,256,128]{2,1,0:T(8,128)(2,1)S(1)}, u32[]{:S(2)}, u32[]{:S(2)}) collective-permute-start(bf16[7,256,128]{2,1,0:T(8,128)(2,1)} %get-tuple-element.15), channel_id=1, source_target_pairs={{0,32},{16,48},{32,0},{48,16},{64,96},{80,112},{96,64},{112,80},{1... | collective-permute-start | bytes 1376264 | tf_op jit(solution)/shard_map/ppermute | solution.py:352
  40.6 3.0 %collective-permute-start.8 = (bf16[7,256,128]{2,1,0:T(8,128)(2,1)}, bf16[7,256,128]{2,1,0:T(8,128)(2,1)S(1)}, u32[]{:S(2)}, u32[]{:S(2)}) collective-permute-start(bf16[7,256,128]{2,1,0:T(8,128)(2,1)} %get-tuple-element.21), channel_id=1, source_target_pairs={{0,48},{16,0},{32,16},{48,32},{64,112},{80,64},{96,80},{112,96},{1... | collective-permute-start | bytes 1376264 | tf_op jit(solution)/shard_map/ppermute | solution.py:352
  49.6 4.5 %collective-permute-start.5 = (bf16[256,128]{1,0:T(8,128)(2,1)S(1)}, bf16[256,128]{1,0:T(8,128)(2,1)S(1)}, u32[]{:S(2)}, u32[]{:S(2)}) collective-permute-start(bf16[256,128]{1,0:T(8,128)(2,1)S(1)} %get-tuple-element.18), channel_id=1, source_target_pairs={{0,16},{16,32},{32,48},{48,0},{64,80},{80,96},{96,112},{112,64},{1... | collective-permute-start | bytes 196616 | tf_op jit(solution)/shard_map/ppermute | solution.py:352
  54.1 6.7 %collective-permute-done.3 = bf16[256,128]{1,0:T(8,128)(2,1)S(1)} collective-permute-done((bf16[256,128]{1,0:T(8,128)(2,1)S(1)}, bf16[256,128]{1,0:T(8,128)(2,1)S(1)}, u32[]{:S(2)}, u32[]{:S(2)}) %collective-permute-start.3) | collective-permute-done | bytes 65568 | tf_op jit(solution)/shard_map/ppermute | solution.py:352
  60.8 4.1 %collective-permute-start.7 = (bf16[256,128]{1,0:T(8,128)(2,1)S(1)}, bf16[256,128]{1,0:T(8,128)(2,1)S(1)}, u32[]{:S(2)}, u32[]{:S(2)}) collective-permute-start(bf16[256,128]{1,0:T(8,128)(2,1)S(1)} %get-tuple-element.20), channel_id=1, source_target_pairs={{0,48},{16,0},{32,16},{48,32},{64,112},{80,64},{96,80},{112,96},{1... | collective-permute-start | bytes 196616 | tf_op jit(solution)/shard_map/ppermute | solution.py:352
  65.7 4.2 %shard_map.103.plan = s32[6,144]{1,0:T(8,128)S(1)} custom-call(s32[1,1]{1,0:T(1,128)} %bitcast.me, s32[1,128]{1,0:T(1,128)S(1)} %bitcast.27, s32[1,1]{1,0:T(1,128)S(6)} %copy.15.live), custom_call_target="tpu_custom_call" | custom-call | tf_op jit(solution)/shard_map/pallas_call | solution.py:391
  69.9 3.3 %shard_map.107 = (f32[33,128,128]{2,1,0:T(8,128)S(1)}, bf16[128,128,128]{2,1,0:T(8,128)(2,1)S(1)}) custom-call(s32[1,1]{1,0:T(1,128)} %bitcast.me, s32[6,144]{1,0:T(8,128)S(1)} %shard_map.103.plan, s32[1,128]{1,0:T(1,128)S(1)} %pad.4.need, bf16[128,128,128]{2,1,0:T(8,128)(2,1)} %bitcast.29, bf16[8,512,128]{2,1,0:T(8,128)(2,1)S(1)} %all-to-all-done.refs_3_.column, ...), custom_call_target="tpu_custom_call" | custom-call | flops 536870912 | bytes 8388608 | tf_op jit(solution)/shard_map/pallas_call | solution.py:401
  73.3 3.6 %shard_map.108 = bf16[16,272,128]{2,1,0:T(8,128)(2,1)} custom-call(s32[6,144]{1,0:T(8,128)S(1)} %shard_map.103.plan, s32[16,2]{1,0:T(8,128)S(1)} %copy.14.row_need, f32[33,128,128]{2,1,0:T(8,128)S(1)} %get-tuple-element.16.early, bf16[128,128,128]{2,1,0:T(8,128)(2,1)S(1)} %get-tuple-element.17.values, bf16[2,128,128]{2,1,0:T(8,128)(2,1)S(1)} %bitcast.24, ...), custom_call_target="tpu_custom_call" | custom-call | flops 268435456 | bytes 8388608 | tf_op jit(solution)/shard_map/pallas_call | solution.py:418
  76.9 40.7 %all_to_all.20.arrived = bf16[16,272,128]{2,1,0:T(8,128)(2,1)S(1)} all-to-all(bf16[16,272,128]{2,1,0:T(8,128)(2,1)} %shard_map.108), channel_id=1, replica_groups=mesh['gr'=32,'gc'=16] {'gc'}, dimensions={0} | all-to-all | bytes 2228224 | tf_op jit(solution)/shard_map/all_to_all | solution.py:338
  120.3 30.8 %all_to_all.21 = bf16[16,256,128]{2,1,0:T(8,128)(2,1)S(1)} all-to-all(bf16[16,256,128]{2,1,0:T(8,128)(2,1)} %get-tuple-element.24), channel_id=1, replica_groups=mesh['gr'=32,'gc'=16] {'gc'}, dimensions={0} | all-to-all | bytes 2097152 | tf_op jit(solution)/shard_map/all_to_all | solution.py:338
  151.1 5.4 %shard_map.110 = bf16[32,256,128]{2,1,0:T(8,128)(2,1)} custom-call(s32[1,128]{1,0:T(1,128)S(1)} %bitcast.28, s32[1,1]{1,0:T(1,128)S(6)} %copy.15.live, bf16[128,128,128]{2,1,0:T(8,128)(2,1)} %bitcast.30, bf16[32,128,128]{2,1,0:T(8,128)(2,1)S(1)} %bitcast.17), custom_call_target="tpu_custom_call" | custom-call | flops 536870912 | bytes 8388608 | tf_op jit(solution)/shard_map/pallas_call | solution.py:473
  156.5 11.0 %all-to-all-start.3 = ((bf16[32,256,128]{2,1,0:T(8,128)(2,1)}), bf16[32,256,128]{2,1,0:T(8,128)(2,1)S(1)}, u32[]{:S(2)}, u32[]{:S(2)}) async-start(bf16[32,256,128]{2,1,0:T(8,128)(2,1)} %shard_map.110), calls=%async_computation.3 | async-start | bytes 4194304 | tf_op jit(solution)/shard_map/all_to_all | solution.py:338
  167.5 3.4 %collective-permute-start.9 = (f32[64,128]{1,0:T(8,128)S(1)}, f32[64,128]{1,0:T(8,128)S(1)}, u32[]{:S(2)}, u32[]{:S(2)}) collective-permute-start(f32[64,128]{1,0:T(8,128)S(1)} %slice_select_fusion), channel_id=1, source_target_pairs={{0,16},{16,0},{32,48},{48,32},{64,80},{80,64},{96,112},{112,96},{1... | collective-permute-start | bytes 98312 | tf_op jit(solution)/shard_map/ppermute | solution.py:342
  170.9 6.5 %collective-permute-done.9 = f32[64,128]{1,0:T(8,128)S(1)} collective-permute-done((f32[64,128]{1,0:T(8,128)S(1)}, f32[64,128]{1,0:T(8,128)S(1)}, u32[]{:S(2)}, u32[]{:S(2)}) %collective-permute-start.9) | collective-permute-done | bytes 32800 | tf_op jit(solution)/shard_map/ppermute | solution.py:342
  177.4 3.5 %collective-permute-start.10 = (f32[32,128]{1,0:T(8,128)S(1)}, f32[32,128]{1,0:T(8,128)S(1)}, u32[]{:S(2)}, u32[]{:S(2)}) collective-permute-start(f32[32,128]{1,0:T(8,128)S(1)} %slice_select_fusion.1), channel_id=1, source_target_pairs={{0,32},{16,48},{32,0},{48,16},{64,96},{80,112},{96,64},{112,80},{1... | collective-permute-start | bytes 49160 | tf_op jit(solution)/shard_map/ppermute | solution.py:342
  180.9 4.0 %collective-permute-done.10 = f32[32,128]{1,0:T(8,128)S(1)} collective-permute-done((f32[32,128]{1,0:T(8,128)S(1)}, f32[32,128]{1,0:T(8,128)S(1)}, u32[]{:S(2)}, u32[]{:S(2)}) %collective-permute-start.10) | collective-permute-done | bytes 16416 | tf_op jit(solution)/shard_map/ppermute | solution.py:342
  184.9 6.1 %collective-permute-start.11 = (f32[32,128]{1,0:T(8,128)S(1)}, f32[32,128]{1,0:T(8,128)S(1)}, u32[]{:S(2)}, u32[]{:S(2)}) collective-permute-start(f32[32,128]{1,0:T(8,128)S(1)} %select_add_fusion.1), channel_id=1, source_target_pairs={{0,64},{16,80},{32,96},{48,112},{64,0},{80,16},{96,32},{112,48},{1... | collective-permute-start | bytes 49160 | tf_op jit(solution)/shard_map/ppermute | solution.py:342
  191.1 24.0 %collective-permute-done.11 = f32[32,128]{1,0:T(8,128)S(1)} collective-permute-done((f32[32,128]{1,0:T(8,128)S(1)}, f32[32,128]{1,0:T(8,128)S(1)}, u32[]{:S(2)}, u32[]{:S(2)}) %collective-permute-start.11) | collective-permute-done | bytes 16416 | tf_op jit(solution)/shard_map/ppermute | solution.py:342
  217.0 4.6 %collective-permute-done.12 = f32[32,128]{1,0:T(8,128)S(1)} collective-permute-done((f32[32,128]{1,0:T(8,128)S(1)}, f32[32,128]{1,0:T(8,128)S(1)}, u32[]{:S(2)}, u32[]{:S(2)}) %collective-permute-start.12) | collective-permute-done | bytes 16416 | tf_op jit(solution)/shard_map/ppermute | solution.py:342
  223.8 7.4 %collective-permute-done.13 = f32[32,128]{1,0:T(8,128)S(1)} collective-permute-done((f32[32,128]{1,0:T(8,128)S(1)}, f32[32,128]{1,0:T(8,128)S(1)}, u32[]{:S(2)}, u32[]{:S(2)}) %collective-permute-start.13) | collective-permute-done | bytes 16416 | tf_op jit(solution)/shard_map/ppermute | solution.py:342
  236.2 3.7 %collective-permute-done.15 = f32[32,128]{1,0:T(8,128)S(1)} collective-permute-done((f32[32,128]{1,0:T(8,128)S(1)}, f32[32,128]{1,0:T(8,128)S(1)}, u32[]{:S(2)}, u32[]{:S(2)}) %collective-permute-start.15) | collective-permute-done | bytes 16416 | tf_op jit(solution)/shard_map/ppermute | solution.py:342
  240.0 3.0 %collective-permute-start.16 = (f32[32,128]{1,0:T(8,128)S(1)}, f32[32,128]{1,0:T(8,128)S(1)}, u32[]{:S(2)}, u32[]{:S(2)}) collective-permute-start(f32[32,128]{1,0:T(8,128)S(1)} %add.35), channel_id=1, source_target_pairs={{0,4},{1,5},{2,6},{3,7},{4,0},{5,1},{6,2},{7,3},{8,12},{9,13},{10,... | collective-permute-start | bytes 49160 | tf_op jit(solution)/shard_map/ppermute | solution.py:342
  242.9 3.5 %collective-permute-done.16 = f32[32,128]{1,0:T(8,128)S(1)} collective-permute-done((f32[32,128]{1,0:T(8,128)S(1)}, f32[32,128]{1,0:T(8,128)S(1)}, u32[]{:S(2)}, u32[]{:S(2)}) %collective-permute-start.16) | collective-permute-done | bytes 16416 | tf_op jit(solution)/shard_map/ppermute | solution.py:342
  246.5 4.5 %collective-permute-start.17 = (f32[32,128]{1,0:T(8,128)S(1)}, f32[32,128]{1,0:T(8,128)S(1)}, u32[]{:S(2)}, u32[]{:S(2)}) collective-permute-start(f32[32,128]{1,0:T(8,128)S(1)} %add.36), channel_id=1, source_target_pairs={{0,8},{1,9},{2,10},{3,11},{4,12},{5,13},{6,14},{7,15},{8,0},{9,1},... | collective-permute-start | bytes 49160 | tf_op jit(solution)/shard_map/ppermute | solution.py:342
  251.0 5.0 %collective-permute-done.17 = f32[32,128]{1,0:T(8,128)S(1)} collective-permute-done((f32[32,128]{1,0:T(8,128)S(1)}, f32[32,128]{1,0:T(8,128)S(1)}, u32[]{:S(2)}, u32[]{:S(2)}) %collective-permute-start.17) | collective-permute-done | bytes 16416 | tf_op jit(solution)/shard_map/ppermute | solution.py:342
  256.0 5.5 %collective-permute-start.18 = (f32[32,128]{1,0:T(8,128)S(1)}, f32[32,128]{1,0:T(8,128)S(1)}, u32[]{:S(2)}, u32[]{:S(2)}) collective-permute-start(f32[32,128]{1,0:T(8,128)S(1)} %add.37), channel_id=1, source_target_pairs={{0,32},{16,48},{32,0},{48,16},{64,96},{80,112},{96,64},{112,80},{1... | collective-permute-start | bytes 49160 | tf_op jit(solution)/shard_map/ppermute | solution.py:342
  263.2 3.9 %collective-permute-start.19 = (f32[64,128]{1,0:T(8,128)S(1)}, f32[64,128]{1,0:T(8,128)S(1)}, u32[]{:S(2)}, u32[]{:S(2)}) collective-permute-start(f32[64,128]{1,0:T(8,128)S(1)} %pad_maximum_fusion), channel_id=1, source_target_pairs={{0,16},{16,0},{32,48},{48,32},{64,80},{80,64},{96,112},{112,96},{1... | collective-permute-start | bytes 98312 | tf_op jit(solution)/shard_map/ppermute | solution.py:342
  269.1 3.6 %collective-permute-done.20 = s32[4,128]{1,0:T(4,128)S(1)} collective-permute-done((s32[4,128]{1,0:T(4,128)S(1)}, s32[4,128]{1,0:T(4,128)S(1)}, u32[]{:S(2)}, u32[]{:S(2)}) %collective-permute-start.20) | collective-permute-done | bytes 2080 | tf_op jit(solution)/shard_map/ppermute | solution.py:342
  274.8 4.2 %collective-permute-done.21 = s32[8,128]{1,0:T(8,128)S(1)} collective-permute-done((s32[8,128]{1,0:T(8,128)S(1)}, s32[8,128]{1,0:T(8,128)S(1)}, u32[]{:S(2)}, u32[]{:S(2)}) %collective-permute-start.21) | collective-permute-done | bytes 4128 | tf_op jit(solution)/shard_map/ppermute | solution.py:342
  281.1 7.5 %collective-permute-done.22 = s32[16,128]{1,0:T(8,128)S(1)} collective-permute-done((s32[16,128]{1,0:T(8,128)S(1)}, s32[16,128]{1,0:T(8,128)S(1)}, u32[]{:S(2)}, u32[]{:S(2)}) %collective-permute-start.22) | collective-permute-done | bytes 8224 | tf_op jit(solution)/shard_map/ppermute | solution.py:342
  (64 shorter events, 44.5 us)
Async XLA Ops:
  0.6 10.9 %copy-start.4 = (s32[1,1,32,2]{2,3,1,0:T(2,128)S(1)}, s32[1,1,32,2]{2,3,1,0:T(2,128)}, u32[]{:S(2)}) copy-start(s32[1,1,32,2]{2,3,1,0:T(2,128)} %param.15) | copy-start | bytes 772
  0.6 45.8 %copy-start = (bf16[1,1,512,128]{3,2,1,0:T(8,128)(2,1)S(1)}, bf16[1,1,512,128]{3,2,1,0:T(8,128)(2,1)}, u32[]{:S(2)}) copy-start(bf16[1,1,512,128]{3,2,1,0:T(8,128)(2,1)} %param.8) | copy-start | bytes 393220
  0.7 64.9 %copy-start.5 = (s32[1,1,16,2]{2,3,1,0:T(2,128)S(1)}, s32[1,1,16,2]{2,3,1,0:T(2,128)}, u32[]{:S(2)}) copy-start(s32[1,1,16,2]{2,3,1,0:T(2,128)} %param.14) | copy-start | bytes 388
  0.7 65.0 %copy-start.3 = (s32[1,1,128]{2,1,0:T(1,128)S(1)}, s32[1,1,128]{2,1,0:T(1,128)}, u32[]{:S(2)}) copy-start(s32[1,1,128]{2,1,0:T(1,128)} %param.12) | copy-start | bytes 1540
  2.7 30.7 %all-to-all-start = ((bf16[8,512,128]{2,1,0:T(8,128)(2,1)}), bf16[8,512,128]{2,1,0:T(8,128)(2,1)S(1)}, u32[]{:S(2)}, u32[]{:S(2)}) async-start(bf16[8,512,128]{2,1,0:T(8,128)(2,1)} %shard_map.104), calls=%async_computation | async-start | bytes 2097152 | tf_op jit(solution)/shard_map/all_to_all | solution.py:363
  11.7 8.5 %collective-permute-start = (s32[1,128]{1,0:T(1,128)S(1)}, s32[1,128]{1,0:T(1,128)S(1)}, u32[]{:S(2)}, u32[]{:S(2)}) collective-permute-start(s32[1,128]{1,0:T(1,128)S(1)} %pad.4.need), channel_id=1, source_target_pairs={{0,48},{16,0},{32,16},{48,32},{64,112},{80,64},{96,80},{112,96},{1... | collective-permute-start | bytes 1544 | tf_op jit(solution)/shard_map/ppermute | solution.py:352
  14.7 7.0 %collective-permute-start.1 = (s32[1,128]{1,0:T(1,128)S(1)}, s32[1,128]{1,0:T(1,128)S(1)}, u32[]{:S(2)}, u32[]{:S(2)}) collective-permute-start(s32[1,128]{1,0:T(1,128)S(1)} %pad.4.need), channel_id=1, source_target_pairs={{0,32},{16,48},{32,0},{48,16},{64,96},{80,112},{96,64},{112,80},{1... | collective-permute-start | bytes 1544 | tf_op jit(solution)/shard_map/ppermute | solution.py:352
  17.4 6.7 %collective-permute-start.2 = (s32[1,128]{1,0:T(1,128)S(1)}, s32[1,128]{1,0:T(1,128)S(1)}, u32[]{:S(2)}, u32[]{:S(2)}) collective-permute-start(s32[1,128]{1,0:T(1,128)S(1)} %pad.4.need), channel_id=1, source_target_pairs={{0,16},{16,32},{32,48},{48,0},{64,80},{80,96},{96,112},{112,64},{1... | collective-permute-start | bytes 1544 | tf_op jit(solution)/shard_map/ppermute | solution.py:352
  35.0 34.9 %collective-permute-start.4 = (bf16[7,256,128]{2,1,0:T(8,128)(2,1)}, bf16[7,256,128]{2,1,0:T(8,128)(2,1)S(1)}, u32[]{:S(2)}, u32[]{:S(2)}) collective-permute-start(bf16[7,256,128]{2,1,0:T(8,128)(2,1)} %get-tuple-element.15), channel_id=1, source_target_pairs={{0,32},{16,48},{32,0},{48,16},{64,96},{80,112},{96,64},{112,80},{1... | collective-permute-start | bytes 1376264 | tf_op jit(solution)/shard_map/ppermute | solution.py:352
  40.6 32.6 %collective-permute-start.8 = (bf16[7,256,128]{2,1,0:T(8,128)(2,1)}, bf16[7,256,128]{2,1,0:T(8,128)(2,1)S(1)}, u32[]{:S(2)}, u32[]{:S(2)}) collective-permute-start(bf16[7,256,128]{2,1,0:T(8,128)(2,1)} %get-tuple-element.21), channel_id=1, source_target_pairs={{0,48},{16,0},{32,16},{48,32},{64,112},{80,64},{96,80},{112,96},{1... | collective-permute-start | bytes 1376264 | tf_op jit(solution)/shard_map/ppermute | solution.py:352
  43.7 29.6 %collective-permute-start.6 = (bf16[7,256,128]{2,1,0:T(8,128)(2,1)S(1)}, bf16[7,256,128]{2,1,0:T(8,128)(2,1)S(1)}, u32[]{:S(2)}, u32[]{:S(2)}) collective-permute-start(bf16[7,256,128]{2,1,0:T(8,128)(2,1)S(1)} %get-tuple-element.19), channel_id=1, source_target_pairs={{0,16},{16,32},{32,48},{48,0},{64,80},{80,96},{96,112},{112,64},{1... | collective-permute-start | bytes 1376264 | tf_op jit(solution)/shard_map/ppermute | solution.py:352
  47.1 13.8 %collective-permute-start.3 = (bf16[256,128]{1,0:T(8,128)(2,1)S(1)}, bf16[256,128]{1,0:T(8,128)(2,1)S(1)}, u32[]{:S(2)}, u32[]{:S(2)}) collective-permute-start(bf16[256,128]{1,0:T(8,128)(2,1)S(1)} %get-tuple-element.14), channel_id=1, source_target_pairs={{0,32},{16,48},{32,0},{48,16},{64,96},{80,112},{96,64},{112,80},{1... | collective-permute-start | bytes 196616 | tf_op jit(solution)/shard_map/ppermute | solution.py:352
  49.6 23.6 %collective-permute-start.5 = (bf16[256,128]{1,0:T(8,128)(2,1)S(1)}, bf16[256,128]{1,0:T(8,128)(2,1)S(1)}, u32[]{:S(2)}, u32[]{:S(2)}) collective-permute-start(bf16[256,128]{1,0:T(8,128)(2,1)S(1)} %get-tuple-element.18), channel_id=1, source_target_pairs={{0,16},{16,32},{32,48},{48,0},{64,80},{80,96},{96,112},{112,64},{1... | collective-permute-start | bytes 196616 | tf_op jit(solution)/shard_map/ppermute | solution.py:352
  60.8 12.4 %collective-permute-start.7 = (bf16[256,128]{1,0:T(8,128)(2,1)S(1)}, bf16[256,128]{1,0:T(8,128)(2,1)S(1)}, u32[]{:S(2)}, u32[]{:S(2)}) collective-permute-start(bf16[256,128]{1,0:T(8,128)(2,1)S(1)} %get-tuple-element.20), channel_id=1, source_target_pairs={{0,48},{16,0},{32,16},{48,32},{64,112},{80,64},{96,80},{112,96},{1... | collective-permute-start | bytes 196616 | tf_op jit(solution)/shard_map/ppermute | solution.py:352
  76.9 40.7 %copy-start.1 = (bf16[1,1,512,128]{3,2,1,0:T(8,128)(2,1)S(1)}, bf16[1,1,512,128]{3,2,1,0:T(8,128)(2,1)}, u32[]{:S(2)}) copy-start(bf16[1,1,512,128]{3,2,1,0:T(8,128)(2,1)} %param.9) | copy-start | bytes 393220
  76.9 40.7 %copy-start.2 = (bf16[128,128]{1,0:T(8,128)(2,1)S(1)}, bf16[128,128]{1,0:T(8,128)(2,1)}, u32[]{:S(2)}) copy-start(bf16[128,128]{1,0:T(8,128)(2,1)} %weight.1) | copy-start | bytes 98308
  156.5 132.8 %all-to-all-start.3 = ((bf16[32,256,128]{2,1,0:T(8,128)(2,1)}), bf16[32,256,128]{2,1,0:T(8,128)(2,1)S(1)}, u32[]{:S(2)}, u32[]{:S(2)}) async-start(bf16[32,256,128]{2,1,0:T(8,128)(2,1)} %shard_map.110), calls=%async_computation.3 | async-start | bytes 4194304 | tf_op jit(solution)/shard_map/all_to_all | solution.py:338
  167.5 9.9 %collective-permute-start.9 = (f32[64,128]{1,0:T(8,128)S(1)}, f32[64,128]{1,0:T(8,128)S(1)}, u32[]{:S(2)}, u32[]{:S(2)}) collective-permute-start(f32[64,128]{1,0:T(8,128)S(1)} %slice_select_fusion), channel_id=1, source_target_pairs={{0,16},{16,0},{32,48},{48,32},{64,80},{80,64},{96,112},{112,96},{1... | collective-permute-start | bytes 98312 | tf_op jit(solution)/shard_map/ppermute | solution.py:342
  177.4 7.5 %collective-permute-start.10 = (f32[32,128]{1,0:T(8,128)S(1)}, f32[32,128]{1,0:T(8,128)S(1)}, u32[]{:S(2)}, u32[]{:S(2)}) collective-permute-start(f32[32,128]{1,0:T(8,128)S(1)} %slice_select_fusion.1), channel_id=1, source_target_pairs={{0,32},{16,48},{32,0},{48,16},{64,96},{80,112},{96,64},{112,80},{1... | collective-permute-start | bytes 49160 | tf_op jit(solution)/shard_map/ppermute | solution.py:342
  184.9 30.1 %collective-permute-start.11 = (f32[32,128]{1,0:T(8,128)S(1)}, f32[32,128]{1,0:T(8,128)S(1)}, u32[]{:S(2)}, u32[]{:S(2)}) collective-permute-start(f32[32,128]{1,0:T(8,128)S(1)} %select_add_fusion.1), channel_id=1, source_target_pairs={{0,64},{16,80},{32,96},{48,112},{64,0},{80,16},{96,32},{112,48},{1... | collective-permute-start | bytes 49160 | tf_op jit(solution)/shard_map/ppermute | solution.py:342
  215.1 6.5 %collective-permute-start.12 = (f32[32,128]{1,0:T(8,128)S(1)}, f32[32,128]{1,0:T(8,128)S(1)}, u32[]{:S(2)}, u32[]{:S(2)}) collective-permute-start(f32[32,128]{1,0:T(8,128)S(1)} %add.31), channel_id=1, source_target_pairs={{0,128},{16,144},{32,160},{48,176},{64,192},{80,208},{96,224},{112... | collective-permute-start | bytes 49160 | tf_op jit(solution)/shard_map/ppermute | solution.py:342
  221.6 9.7 %collective-permute-start.13 = (f32[32,128]{1,0:T(8,128)S(1)}, f32[32,128]{1,0:T(8,128)S(1)}, u32[]{:S(2)}, u32[]{:S(2)}) collective-permute-start(f32[32,128]{1,0:T(8,128)S(1)} %add.32), channel_id=1, source_target_pairs={{0,256},{16,272},{32,288},{48,304},{64,320},{80,336},{96,352},{112... | collective-permute-start | bytes 49160 | tf_op jit(solution)/shard_map/ppermute | solution.py:342
  231.3 3.1 %collective-permute-start.14 = (f32[32,128]{1,0:T(8,128)S(1)}, f32[32,128]{1,0:T(8,128)S(1)}, u32[]{:S(2)}, u32[]{:S(2)}) collective-permute-start(f32[32,128]{1,0:T(8,128)S(1)} %add.33), channel_id=1, source_target_pairs={{0,1},{1,0},{2,3},{3,2},{4,5},{5,4},{6,7},{7,6},{8,9},{9,8},{10,11... | collective-permute-start | bytes 49160 | tf_op jit(solution)/shard_map/ppermute | solution.py:342
  234.3 5.6 %collective-permute-start.15 = (f32[32,128]{1,0:T(8,128)S(1)}, f32[32,128]{1,0:T(8,128)S(1)}, u32[]{:S(2)}, u32[]{:S(2)}) collective-permute-start(f32[32,128]{1,0:T(8,128)S(1)} %add.34), channel_id=1, source_target_pairs={{0,2},{1,3},{2,0},{3,1},{4,6},{5,7},{6,4},{7,5},{8,10},{9,11},{10,... | collective-permute-start | bytes 49160 | tf_op jit(solution)/shard_map/ppermute | solution.py:342
  240.0 6.5 %collective-permute-start.16 = (f32[32,128]{1,0:T(8,128)S(1)}, f32[32,128]{1,0:T(8,128)S(1)}, u32[]{:S(2)}, u32[]{:S(2)}) collective-permute-start(f32[32,128]{1,0:T(8,128)S(1)} %add.35), channel_id=1, source_target_pairs={{0,4},{1,5},{2,6},{3,7},{4,0},{5,1},{6,2},{7,3},{8,12},{9,13},{10,... | collective-permute-start | bytes 49160 | tf_op jit(solution)/shard_map/ppermute | solution.py:342
  246.5 9.5 %collective-permute-start.17 = (f32[32,128]{1,0:T(8,128)S(1)}, f32[32,128]{1,0:T(8,128)S(1)}, u32[]{:S(2)}, u32[]{:S(2)}) collective-permute-start(f32[32,128]{1,0:T(8,128)S(1)} %add.36), channel_id=1, source_target_pairs={{0,8},{1,9},{2,10},{3,11},{4,12},{5,13},{6,14},{7,15},{8,0},{9,1},... | collective-permute-start | bytes 49160 | tf_op jit(solution)/shard_map/ppermute | solution.py:342
  256.0 7.2 %collective-permute-start.18 = (f32[32,128]{1,0:T(8,128)S(1)}, f32[32,128]{1,0:T(8,128)S(1)}, u32[]{:S(2)}, u32[]{:S(2)}) collective-permute-start(f32[32,128]{1,0:T(8,128)S(1)} %add.37), channel_id=1, source_target_pairs={{0,32},{16,48},{32,0},{48,16},{64,96},{80,112},{96,64},{112,80},{1... | collective-permute-start | bytes 49160 | tf_op jit(solution)/shard_map/ppermute | solution.py:342
  263.2 25.3 %collective-permute-start.19 = (f32[64,128]{1,0:T(8,128)S(1)}, f32[64,128]{1,0:T(8,128)S(1)}, u32[]{:S(2)}, u32[]{:S(2)}) collective-permute-start(f32[64,128]{1,0:T(8,128)S(1)} %pad_maximum_fusion), channel_id=1, source_target_pairs={{0,16},{16,0},{32,48},{48,32},{64,80},{80,64},{96,112},{112,96},{1... | collective-permute-start | bytes 98312 | tf_op jit(solution)/shard_map/ppermute | solution.py:342
  267.2 5.5 %collective-permute-start.20 = (s32[4,128]{1,0:T(4,128)S(1)}, s32[4,128]{1,0:T(4,128)S(1)}, u32[]{:S(2)}, u32[]{:S(2)}) collective-permute-start(s32[4,128]{1,0:T(4,128)S(1)} %pad_add_fusion), channel_id=1, source_target_pairs={{0,64},{16,80},{32,96},{48,112},{64,0},{80,16},{96,32},{112,48},{1... | collective-permute-start | bytes 6152 | tf_op jit(solution)/shard_map/ppermute | solution.py:342
  272.7 6.4 %collective-permute-start.21 = (s32[8,128]{1,0:T(8,128)S(1)}, s32[8,128]{1,0:T(8,128)S(1)}, u32[]{:S(2)}, u32[]{:S(2)}) collective-permute-start(s32[8,128]{1,0:T(8,128)S(1)} %concatenate.24), channel_id=1, source_target_pairs={{0,128},{16,144},{32,160},{48,176},{64,192},{80,208},{96,224},{112... | collective-permute-start | bytes 12296 | tf_op jit(solution)/shard_map/ppermute | solution.py:342
  279.1 9.4 %collective-permute-start.22 = (s32[16,128]{1,0:T(8,128)S(1)}, s32[16,128]{1,0:T(8,128)S(1)}, u32[]{:S(2)}, u32[]{:S(2)}) collective-permute-start(s32[16,128]{1,0:T(8,128)S(1)} %concatenate.25), channel_id=1, source_target_pairs={{0,256},{16,272},{32,288},{48,304},{64,320},{80,336},{96,352},{112... | collective-permute-start | bytes 24584 | tf_op jit(solution)/shard_map/ppermute | solution.py:342

commit v10 on v9

--- a/solution.py
+++ b/solution.py
@@ -38,11 +38,19 @@
     )
 
 
-def repeat_kernel(feats, out, sems):
+def repeat_kernel(feats, out, held, load_sems, sems):
     n = out.shape[0]
-    copies = [pltpu.make_async_copy(feats, out.at[y], sems.at[y]) for y in range(n)]
-    for copy in copies:
-        copy.start()
+    size = feats.shape[0] // PARTS
+    parts = [pl.ds(p * size, size) for p in range(PARTS)]
+    loads = [pltpu.make_async_copy(feats.at[p], held.at[p], load_sems.at[i]) for i, p in enumerate(parts)]
+    for load in loads:
+        load.start()
+    copies = []
+    for i, p in enumerate(parts):
+        loads[i].wait()
+        for y in range(n):
+            copies.append(pltpu.make_async_copy(held.at[p], out.at[y, p], sems.at[i, y]))
+            copies[-1].start()
     for copy in copies:
         copy.wait()
 
@@ -354,8 +362,12 @@
     copies = call(
         repeat_kernel,
         jax.ShapeDtypeStruct((n_y, local, width), BF16),
-        [VMEM],
-        [pltpu.SemaphoreType.DMA((n_y,))],
+        [HBM],
+        [
+            pltpu.VMEM((local, width), BF16),
+            pltpu.SemaphoreType.DMA((PARTS,)),
+            pltpu.SemaphoreType.DMA((PARTS, n_y)),
+        ],
         moved=2 << 20,
         out_spec=HBM,
         grant=60,

time: 292 us -> 292 us (level)
  no operation moved by 1% of the time
where the time goes in v10:
time: 292 us; the launch traced here: 291 us
  waiting for transfers between devices  96.8 us (33%)
  starting transfers between devices  94.8 us (32%)
  blocking collectives  71.4 us (24%)
  Pallas kernels  25.5 us (9%)
    ppermute x14, waiting for transfers between devices, trade(): return lax.ppermute(array, axis, pairs)  76.8 us
    all_to_all x2, blocking collectives, swap(): return lax.all_to_all(array, axis, split_axis=0, concat_axis=0, tiled=True)  71.4 us
    ppermute x14, starting transfers between devices, trade(): return lax.ppermute(array, axis, pairs)  43.9 us
    ppermute x9, starting transfers between devices, along_x(): return lax.ppermute(array, 'gr', pairs)  31 us
    all_to_all x1, starting transfers between devices, swap(): return lax.all_to_all(array, axis, split_axis=0, concat_axis=0, tiled=True)  11 us
    ppermute x9, waiting for transfers between devices, along_x(): return lax.ppermute(array, 'gr', pairs)  10.6 us
    all_to_all x1, waiting for transfers between devices, on_device(): lax.all_to_all(copies, 'gr', split_axis=0, concat_axis=0, tiled=True, axi...  9.32 us
    all_to_all x1, starting transfers between devices, on_device(): lax.all_to_all(copies, 'gr', split_axis=0, concat_axis=0, tiled=True, axi...  8.84 us
  transfers between devices with their start and end apart: 25, of which 17 were waited for; matrix products, arithmetic and copies ran while one was open for 0% of the time, Pallas kernels for 3%

profile of v10, /device:TPU:40, one launch (start us, length us, event | category | flops | bytes accessed | tf_op | source)
XLA Modules:
  0.0 291.3 jit_solution(4705293434322134487)
XLA Ops:
  2.8 8.8 %all-to-all-start = ((bf16[8,512,128]{2,1,0:T(8,128)(2,1)}), bf16[8,512,128]{2,1,0:T(8,128)(2,1)S(1)}, u32[]{:S(2)}, u32[]{:S(2)}) async-start(bf16[8,512,128]{2,1,0:T(8,128)(2,1)} %shard_map.104), calls=%async_computation | async-start | bytes 2097152 | tf_op jit(solution)/shard_map/all_to_all | solution.py:375
  24.2 9.3 %all-to-all-done.refs_3_.column = bf16[8,512,128]{2,1,0:T(8,128)(2,1)S(1)} async-done(((bf16[8,512,128]{2,1,0:T(8,128)(2,1)}), bf16[8,512,128]{2,1,0:T(8,128)(2,1)S(1)}, u32[]{:S(2)}, u32[]{:S(2)}) %all-to-all-start) | async-done | bytes 1048608 | tf_op jit(solution)/shard_map/all_to_all | solution.py:375
  35.2 5.6 %collective-permute-start.4 = (bf16[7,256,128]{2,1,0:T(8,128)(2,1)}, bf16[7,256,128]{2,1,0:T(8,128)(2,1)S(1)}, u32[]{:S(2)}, u32[]{:S(2)}) collective-permute-start(bf16[7,256,128]{2,1,0:T(8,128)(2,1)} %get-tuple-element.15), channel_id=1, source_target_pairs={{0,32},{16,48},{32,0},{48,16},{64,96},{80,112},{96,64},{112,80},{1... | collective-permute-start | bytes 1376264 | tf_op jit(solution)/shard_map/ppermute | solution.py:360
  40.8 3.0 %collective-permute-start.8 = (bf16[7,256,128]{2,1,0:T(8,128)(2,1)}, bf16[7,256,128]{2,1,0:T(8,128)(2,1)S(1)}, u32[]{:S(2)}, u32[]{:S(2)}) collective-permute-start(bf16[7,256,128]{2,1,0:T(8,128)(2,1)} %get-tuple-element.21), channel_id=1, source_target_pairs={{0,48},{16,0},{32,16},{48,32},{64,112},{80,64},{96,80},{112,96},{1... | collective-permute-start | bytes 1376264 | tf_op jit(solution)/shard_map/ppermute | solution.py:360
  49.8 4.5 %collective-permute-start.5 = (bf16[256,128]{1,0:T(8,128)(2,1)S(1)}, bf16[256,128]{1,0:T(8,128)(2,1)S(1)}, u32[]{:S(2)}, u32[]{:S(2)}) collective-permute-start(bf16[256,128]{1,0:T(8,128)(2,1)S(1)} %get-tuple-element.18), channel_id=1, source_target_pairs={{0,16},{16,32},{32,48},{48,0},{64,80},{80,96},{96,112},{112,64},{1... | collective-permute-start | bytes 196616 | tf_op jit(solution)/shard_map/ppermute | solution.py:360
  54.3 6.7 %collective-permute-done.3 = bf16[256,128]{1,0:T(8,128)(2,1)S(1)} collective-permute-done((bf16[256,128]{1,0:T(8,128)(2,1)S(1)}, bf16[256,128]{1,0:T(8,128)(2,1)S(1)}, u32[]{:S(2)}, u32[]{:S(2)}) %collective-permute-start.3) | collective-permute-done | bytes 65568 | tf_op jit(solution)/shard_map/ppermute | solution.py:360
  61.0 4.1 %collective-permute-start.7 = (bf16[256,128]{1,0:T(8,128)(2,1)S(1)}, bf16[256,128]{1,0:T(8,128)(2,1)S(1)}, u32[]{:S(2)}, u32[]{:S(2)}) collective-permute-start(bf16[256,128]{1,0:T(8,128)(2,1)S(1)} %get-tuple-element.20), channel_id=1, source_target_pairs={{0,48},{16,0},{32,16},{48,32},{64,112},{80,64},{96,80},{112,96},{1... | collective-permute-start | bytes 196616 | tf_op jit(solution)/shard_map/ppermute | solution.py:360
  65.8 4.2 %shard_map.103.plan = s32[6,144]{1,0:T(8,128)S(1)} custom-call(s32[1,1]{1,0:T(1,128)} %bitcast.me, s32[1,128]{1,0:T(1,128)S(1)} %bitcast.27, s32[1,1]{1,0:T(1,128)S(6)} %copy.15.live), custom_call_target="tpu_custom_call" | custom-call | tf_op jit(solution)/shard_map/pallas_call | solution.py:403
  70.1 3.3 %shard_map.107 = (f32[33,128,128]{2,1,0:T(8,128)S(1)}, bf16[128,128,128]{2,1,0:T(8,128)(2,1)S(1)}) custom-call(s32[1,1]{1,0:T(1,128)} %bitcast.me, s32[6,144]{1,0:T(8,128)S(1)} %shard_map.103.plan, s32[1,128]{1,0:T(1,128)S(1)} %pad.4.need, bf16[128,128,128]{2,1,0:T(8,128)(2,1)} %bitcast.29, bf16[8,512,128]{2,1,0:T(8,128)(2,1)S(1)} %all-to-all-done.refs_3_.column, ...), custom_call_target="tpu_custom_call" | custom-call | flops 536870912 | bytes 8388608 | tf_op jit(solution)/shard_map/pallas_call | solution.py:413
  73.4 3.6 %shard_map.108 = bf16[16,272,128]{2,1,0:T(8,128)(2,1)} custom-call(s32[6,144]{1,0:T(8,128)S(1)} %shard_map.103.plan, s32[16,2]{1,0:T(8,128)S(1)} %copy.14.row_need, f32[33,128,128]{2,1,0:T(8,128)S(1)} %get-tuple-element.16.early, bf16[128,128,128]{2,1,0:T(8,128)(2,1)S(1)} %get-tuple-element.17.values, bf16[2,128,128]{2,1,0:T(8,128)(2,1)S(1)} %bitcast.24, ...), custom_call_target="tpu_custom_call" | custom-call | flops 268435456 | bytes 8388608 | tf_op jit(solution)/shard_map/pallas_call | solution.py:430
  77.1 40.7 %all_to_all.20.arrived = bf16[16,272,128]{2,1,0:T(8,128)(2,1)S(1)} all-to-all(bf16[16,272,128]{2,1,0:T(8,128)(2,1)} %shard_map.108), channel_id=1, replica_groups=mesh['gr'=32,'gc'=16] {'gc'}, dimensions={0} | all-to-all | bytes 2228224 | tf_op jit(solution)/shard_map/all_to_all | solution.py:346
  120.5 30.8 %all_to_all.21 = bf16[16,256,128]{2,1,0:T(8,128)(2,1)S(1)} all-to-all(bf16[16,256,128]{2,1,0:T(8,128)(2,1)} %get-tuple-element.24), channel_id=1, replica_groups=mesh['gr'=32,'gc'=16] {'gc'}, dimensions={0} | all-to-all | bytes 2097152 | tf_op jit(solution)/shard_map/all_to_all | solution.py:346
  151.2 5.4 %shard_map.110 = bf16[32,256,128]{2,1,0:T(8,128)(2,1)} custom-call(s32[1,128]{1,0:T(1,128)S(1)} %bitcast.28, s32[1,1]{1,0:T(1,128)S(6)} %copy.15.live, bf16[128,128,128]{2,1,0:T(8,128)(2,1)} %bitcast.30, bf16[32,128,128]{2,1,0:T(8,128)(2,1)S(1)} %bitcast.17), custom_call_target="tpu_custom_call" | custom-call | flops 536870912 | bytes 8388608 | tf_op jit(solution)/shard_map/pallas_call | solution.py:485
  156.6 11.0 %all-to-all-start.3 = ((bf16[32,256,128]{2,1,0:T(8,128)(2,1)}), bf16[32,256,128]{2,1,0:T(8,128)(2,1)S(1)}, u32[]{:S(2)}, u32[]{:S(2)}) async-start(bf16[32,256,128]{2,1,0:T(8,128)(2,1)} %shard_map.110), calls=%async_computation.3 | async-start | bytes 4194304 | tf_op jit(solution)/shard_map/all_to_all | solution.py:346
  167.6 3.4 %collective-permute-start.9 = (f32[64,128]{1,0:T(8,128)S(1)}, f32[64,128]{1,0:T(8,128)S(1)}, u32[]{:S(2)}, u32[]{:S(2)}) collective-permute-start(f32[64,128]{1,0:T(8,128)S(1)} %slice_select_fusion), channel_id=1, source_target_pairs={{0,16},{16,0},{32,48},{48,32},{64,80},{80,64},{96,112},{112,96},{1... | collective-permute-start | bytes 98312 | tf_op jit(solution)/shard_map/ppermute | solution.py:350
  171.0 6.5 %collective-permute-done.9 = f32[64,128]{1,0:T(8,128)S(1)} collective-permute-done((f32[64,128]{1,0:T(8,128)S(1)}, f32[64,128]{1,0:T(8,128)S(1)}, u32[]{:S(2)}, u32[]{:S(2)}) %collective-permute-start.9) | collective-permute-done | bytes 32800 | tf_op jit(solution)/shard_map/ppermute | solution.py:350
  177.6 3.5 %collective-permute-start.10 = (f32[32,128]{1,0:T(8,128)S(1)}, f32[32,128]{1,0:T(8,128)S(1)}, u32[]{:S(2)}, u32[]{:S(2)}) collective-permute-start(f32[32,128]{1,0:T(8,128)S(1)} %slice_select_fusion.1), channel_id=1, source_target_pairs={{0,32},{16,48},{32,0},{48,16},{64,96},{80,112},{96,64},{112,80},{1... | collective-permute-start | bytes 49160 | tf_op jit(solution)/shard_map/ppermute | solution.py:350
  181.1 4.0 %collective-permute-done.10 = f32[32,128]{1,0:T(8,128)S(1)} collective-permute-done((f32[32,128]{1,0:T(8,128)S(1)}, f32[32,128]{1,0:T(8,128)S(1)}, u32[]{:S(2)}, u32[]{:S(2)}) %collective-permute-start.10) | collective-permute-done | bytes 16416 | tf_op jit(solution)/shard_map/ppermute | solution.py:350
  185.1 6.1 %collective-permute-start.11 = (f32[32,128]{1,0:T(8,128)S(1)}, f32[32,128]{1,0:T(8,128)S(1)}, u32[]{:S(2)}, u32[]{:S(2)}) collective-permute-start(f32[32,128]{1,0:T(8,128)S(1)} %select_add_fusion.1), channel_id=1, source_target_pairs={{0,64},{16,80},{32,96},{48,112},{64,0},{80,16},{96,32},{112,48},{1... | collective-permute-start | bytes 49160 | tf_op jit(solution)/shard_map/ppermute | solution.py:350
  191.2 24.0 %collective-permute-done.11 = f32[32,128]{1,0:T(8,128)S(1)} collective-permute-done((f32[32,128]{1,0:T(8,128)S(1)}, f32[32,128]{1,0:T(8,128)S(1)}, u32[]{:S(2)}, u32[]{:S(2)}) %collective-permute-start.11) | collective-permute-done | bytes 16416 | tf_op jit(solution)/shard_map/ppermute | solution.py:350
  217.1 4.6 %collective-permute-done.12 = f32[32,128]{1,0:T(8,128)S(1)} collective-permute-done((f32[32,128]{1,0:T(8,128)S(1)}, f32[32,128]{1,0:T(8,128)S(1)}, u32[]{:S(2)}, u32[]{:S(2)}) %collective-permute-start.12) | collective-permute-done | bytes 16416 | tf_op jit(solution)/shard_map/ppermute | solution.py:350
  224.0 7.4 %collective-permute-done.13 = f32[32,128]{1,0:T(8,128)S(1)} collective-permute-done((f32[32,128]{1,0:T(8,128)S(1)}, f32[32,128]{1,0:T(8,128)S(1)}, u32[]{:S(2)}, u32[]{:S(2)}) %collective-permute-start.13) | collective-permute-done | bytes 16416 | tf_op jit(solution)/shard_map/ppermute | solution.py:350
  236.4 3.7 %collective-permute-done.15 = f32[32,128]{1,0:T(8,128)S(1)} collective-permute-done((f32[32,128]{1,0:T(8,128)S(1)}, f32[32,128]{1,0:T(8,128)S(1)}, u32[]{:S(2)}, u32[]{:S(2)}) %collective-permute-start.15) | collective-permute-done | bytes 16416 | tf_op jit(solution)/shard_map/ppermute | solution.py:350
  240.1 3.0 %collective-permute-start.16 = (f32[32,128]{1,0:T(8,128)S(1)}, f32[32,128]{1,0:T(8,128)S(1)}, u32[]{:S(2)}, u32[]{:S(2)}) collective-permute-start(f32[32,128]{1,0:T(8,128)S(1)} %add.35), channel_id=1, source_target_pairs={{0,4},{1,5},{2,6},{3,7},{4,0},{5,1},{6,2},{7,3},{8,12},{9,13},{10,... | collective-permute-start | bytes 49160 | tf_op jit(solution)/shard_map/ppermute | solution.py:350
  243.1 3.5 %collective-permute-done.16 = f32[32,128]{1,0:T(8,128)S(1)} collective-permute-done((f32[32,128]{1,0:T(8,128)S(1)}, f32[32,128]{1,0:T(8,128)S(1)}, u32[]{:S(2)}, u32[]{:S(2)}) %collective-permute-start.16) | collective-permute-done | bytes 16416 | tf_op jit(solution)/shard_map/ppermute | solution.py:350
  246.6 4.5 %collective-permute-start.17 = (f32[32,128]{1,0:T(8,128)S(1)}, f32[32,128]{1,0:T(8,128)S(1)}, u32[]{:S(2)}, u32[]{:S(2)}) collective-permute-start(f32[32,128]{1,0:T(8,128)S(1)} %add.36), channel_id=1, source_target_pairs={{0,8},{1,9},{2,10},{3,11},{4,12},{5,13},{6,14},{7,15},{8,0},{9,1},... | collective-permute-start | bytes 49160 | tf_op jit(solution)/shard_map/ppermute | solution.py:350
  251.1 5.0 %collective-permute-done.17 = f32[32,128]{1,0:T(8,128)S(1)} collective-permute-done((f32[32,128]{1,0:T(8,128)S(1)}, f32[32,128]{1,0:T(8,128)S(1)}, u32[]{:S(2)}, u32[]{:S(2)}) %collective-permute-start.17) | collective-permute-done | bytes 16416 | tf_op jit(solution)/shard_map/ppermute | solution.py:350
  256.2 5.5 %collective-permute-start.18 = (f32[32,128]{1,0:T(8,128)S(1)}, f32[32,128]{1,0:T(8,128)S(1)}, u32[]{:S(2)}, u32[]{:S(2)}) collective-permute-start(f32[32,128]{1,0:T(8,128)S(1)} %add.37), channel_id=1, source_target_pairs={{0,32},{16,48},{32,0},{48,16},{64,96},{80,112},{96,64},{112,80},{1... | collective-permute-start | bytes 49160 | tf_op jit(solution)/shard_map/ppermute | solution.py:350
  263.4 3.9 %collective-permute-start.19 = (f32[64,128]{1,0:T(8,128)S(1)}, f32[64,128]{1,0:T(8,128)S(1)}, u32[]{:S(2)}, u32[]{:S(2)}) collective-permute-start(f32[64,128]{1,0:T(8,128)S(1)} %pad_maximum_fusion), channel_id=1, source_target_pairs={{0,16},{16,0},{32,48},{48,32},{64,80},{80,64},{96,112},{112,96},{1... | collective-permute-start | bytes 98312 | tf_op jit(solution)/shard_map/ppermute | solution.py:350
  269.2 3.6 %collective-permute-done.20 = s32[4,128]{1,0:T(4,128)S(1)} collective-permute-done((s32[4,128]{1,0:T(4,128)S(1)}, s32[4,128]{1,0:T(4,128)S(1)}, u32[]{:S(2)}, u32[]{:S(2)}) %collective-permute-start.20) | collective-permute-done | bytes 2080 | tf_op jit(solution)/shard_map/ppermute | solution.py:350
  275.0 4.2 %collective-permute-done.21 = s32[8,128]{1,0:T(8,128)S(1)} collective-permute-done((s32[8,128]{1,0:T(8,128)S(1)}, s32[8,128]{1,0:T(8,128)S(1)}, u32[]{:S(2)}, u32[]{:S(2)}) %collective-permute-start.21) | collective-permute-done | bytes 4128 | tf_op jit(solution)/shard_map/ppermute | solution.py:350
  281.2 7.5 %collective-permute-done.22 = s32[16,128]{1,0:T(8,128)S(1)} collective-permute-done((s32[16,128]{1,0:T(8,128)S(1)}, s32[16,128]{1,0:T(8,128)S(1)}, u32[]{:S(2)}, u32[]{:S(2)}) %collective-permute-start.22) | collective-permute-done | bytes 8224 | tf_op jit(solution)/shard_map/ppermute | solution.py:350
  (64 shorter events, 44.7 us)
Async XLA Ops:
  0.6 11.1 %copy-start.4 = (s32[1,1,32,2]{2,3,1,0:T(2,128)S(1)}, s32[1,1,32,2]{2,3,1,0:T(2,128)}, u32[]{:S(2)}) copy-start(s32[1,1,32,2]{2,3,1,0:T(2,128)} %param.15) | copy-start | bytes 772
  0.6 46.0 %copy-start = (bf16[1,1,512,128]{3,2,1,0:T(8,128)(2,1)S(1)}, bf16[1,1,512,128]{3,2,1,0:T(8,128)(2,1)}, u32[]{:S(2)}) copy-start(bf16[1,1,512,128]{3,2,1,0:T(8,128)(2,1)} %param.8) | copy-start | bytes 393220
  0.7 65.1 %copy-start.5 = (s32[1,1,16,2]{2,3,1,0:T(2,128)S(1)}, s32[1,1,16,2]{2,3,1,0:T(2,128)}, u32[]{:S(2)}) copy-start(s32[1,1,16,2]{2,3,1,0:T(2,128)} %param.14) | copy-start | bytes 388
  0.7 65.2 %copy-start.3 = (s32[1,1,128]{2,1,0:T(1,128)S(1)}, s32[1,1,128]{2,1,0:T(1,128)}, u32[]{:S(2)}) copy-start(s32[1,1,128]{2,1,0:T(1,128)} %param.12) | copy-start | bytes 1540
  2.8 30.7 %all-to-all-start = ((bf16[8,512,128]{2,1,0:T(8,128)(2,1)}), bf16[8,512,128]{2,1,0:T(8,128)(2,1)S(1)}, u32[]{:S(2)}, u32[]{:S(2)}) async-start(bf16[8,512,128]{2,1,0:T(8,128)(2,1)} %shard_map.104), calls=%async_computation | async-start | bytes 2097152 | tf_op jit(solution)/shard_map/all_to_all | solution.py:375
  11.9 8.5 %collective-permute-start = (s32[1,128]{1,0:T(1,128)S(1)}, s32[1,128]{1,0:T(1,128)S(1)}, u32[]{:S(2)}, u32[]{:S(2)}) collective-permute-start(s32[1,128]{1,0:T(1,128)S(1)} %pad.4.need), channel_id=1, source_target_pairs={{0,48},{16,0},{32,16},{48,32},{64,112},{80,64},{96,80},{112,96},{1... | collective-permute-start | bytes 1544 | tf_op jit(solution)/shard_map/ppermute | solution.py:360
  14.8 7.0 %collective-permute-start.1 = (s32[1,128]{1,0:T(1,128)S(1)}, s32[1,128]{1,0:T(1,128)S(1)}, u32[]{:S(2)}, u32[]{:S(2)}) collective-permute-start(s32[1,128]{1,0:T(1,128)S(1)} %pad.4.need), channel_id=1, source_target_pairs={{0,32},{16,48},{32,0},{48,16},{64,96},{80,112},{96,64},{112,80},{1... | collective-permute-start | bytes 1544 | tf_op jit(solution)/shard_map/ppermute | solution.py:360
  17.6 6.7 %collective-permute-start.2 = (s32[1,128]{1,0:T(1,128)S(1)}, s32[1,128]{1,0:T(1,128)S(1)}, u32[]{:S(2)}, u32[]{:S(2)}) collective-permute-start(s32[1,128]{1,0:T(1,128)S(1)} %pad.4.need), channel_id=1, source_target_pairs={{0,16},{16,32},{32,48},{48,0},{64,80},{80,96},{96,112},{112,64},{1... | collective-permute-start | bytes 1544 | tf_op jit(solution)/shard_map/ppermute | solution.py:360
  35.2 34.9 %collective-permute-start.4 = (bf16[7,256,128]{2,1,0:T(8,128)(2,1)}, bf16[7,256,128]{2,1,0:T(8,128)(2,1)S(1)}, u32[]{:S(2)}, u32[]{:S(2)}) collective-permute-start(bf16[7,256,128]{2,1,0:T(8,128)(2,1)} %get-tuple-element.15), channel_id=1, source_target_pairs={{0,32},{16,48},{32,0},{48,16},{64,96},{80,112},{96,64},{112,80},{1... | collective-permute-start | bytes 1376264 | tf_op jit(solution)/shard_map/ppermute | solution.py:360
  40.8 32.6 %collective-permute-start.8 = (bf16[7,256,128]{2,1,0:T(8,128)(2,1)}, bf16[7,256,128]{2,1,0:T(8,128)(2,1)S(1)}, u32[]{:S(2)}, u32[]{:S(2)}) collective-permute-start(bf16[7,256,128]{2,1,0:T(8,128)(2,1)} %get-tuple-element.21), channel_id=1, source_target_pairs={{0,48},{16,0},{32,16},{48,32},{64,112},{80,64},{96,80},{112,96},{1... | collective-permute-start | bytes 1376264 | tf_op jit(solution)/shard_map/ppermute | solution.py:360
  43.8 29.6 %collective-permute-start.6 = (bf16[7,256,128]{2,1,0:T(8,128)(2,1)S(1)}, bf16[7,256,128]{2,1,0:T(8,128)(2,1)S(1)}, u32[]{:S(2)}, u32[]{:S(2)}) collective-permute-start(bf16[7,256,128]{2,1,0:T(8,128)(2,1)S(1)} %get-tuple-element.19), channel_id=1, source_target_pairs={{0,16},{16,32},{32,48},{48,0},{64,80},{80,96},{96,112},{112,64},{1... | collective-permute-start | bytes 1376264 | tf_op jit(solution)/shard_map/ppermute | solution.py:360
  47.2 13.8 %collective-permute-start.3 = (bf16[256,128]{1,0:T(8,128)(2,1)S(1)}, bf16[256,128]{1,0:T(8,128)(2,1)S(1)}, u32[]{:S(2)}, u32[]{:S(2)}) collective-permute-start(bf16[256,128]{1,0:T(8,128)(2,1)S(1)} %get-tuple-element.14), channel_id=1, source_target_pairs={{0,32},{16,48},{32,0},{48,16},{64,96},{80,112},{96,64},{112,80},{1... | collective-permute-start | bytes 196616 | tf_op jit(solution)/shard_map/ppermute | solution.py:360
  49.8 23.6 %collective-permute-start.5 = (bf16[256,128]{1,0:T(8,128)(2,1)S(1)}, bf16[256,128]{1,0:T(8,128)(2,1)S(1)}, u32[]{:S(2)}, u32[]{:S(2)}) collective-permute-start(bf16[256,128]{1,0:T(8,128)(2,1)S(1)} %get-tuple-element.18), channel_id=1, source_target_pairs={{0,16},{16,32},{32,48},{48,0},{64,80},{80,96},{96,112},{112,64},{1... | collective-permute-start | bytes 196616 | tf_op jit(solution)/shard_map/ppermute | solution.py:360
  61.0 12.4 %collective-permute-start.7 = (bf16[256,128]{1,0:T(8,128)(2,1)S(1)}, bf16[256,128]{1,0:T(8,128)(2,1)S(1)}, u32[]{:S(2)}, u32[]{:S(2)}) collective-permute-start(bf16[256,128]{1,0:T(8,128)(2,1)S(1)} %get-tuple-element.20), channel_id=1, source_target_pairs={{0,48},{16,0},{32,16},{48,32},{64,112},{80,64},{96,80},{112,96},{1... | collective-permute-start | bytes 196616 | tf_op jit(solution)/shard_map/ppermute | solution.py:360
  77.0 40.7 %copy-start.1 = (bf16[1,1,512,128]{3,2,1,0:T(8,128)(2,1)S(1)}, bf16[1,1,512,128]{3,2,1,0:T(8,128)(2,1)}, u32[]{:S(2)}) copy-start(bf16[1,1,512,128]{3,2,1,0:T(8,128)(2,1)} %param.9) | copy-start | bytes 393220
  77.1 40.7 %copy-start.2 = (bf16[128,128]{1,0:T(8,128)(2,1)S(1)}, bf16[128,128]{1,0:T(8,128)(2,1)}, u32[]{:S(2)}) copy-start(bf16[128,128]{1,0:T(8,128)(2,1)} %weight.1) | copy-start | bytes 98308
  156.6 132.8 %all-to-all-start.3 = ((bf16[32,256,128]{2,1,0:T(8,128)(2,1)}), bf16[32,256,128]{2,1,0:T(8,128)(2,1)S(1)}, u32[]{:S(2)}, u32[]{:S(2)}) async-start(bf16[32,256,128]{2,1,0:T(8,128)(2,1)} %shard_map.110), calls=%async_computation.3 | async-start | bytes 4194304 | tf_op jit(solution)/shard_map/all_to_all | solution.py:346
  167.6 9.9 %collective-permute-start.9 = (f32[64,128]{1,0:T(8,128)S(1)}, f32[64,128]{1,0:T(8,128)S(1)}, u32[]{:S(2)}, u32[]{:S(2)}) collective-permute-start(f32[64,128]{1,0:T(8,128)S(1)} %slice_select_fusion), channel_id=1, source_target_pairs={{0,16},{16,0},{32,48},{48,32},{64,80},{80,64},{96,112},{112,96},{1... | collective-permute-start | bytes 98312 | tf_op jit(solution)/shard_map/ppermute | solution.py:350
  177.6 7.5 %collective-permute-start.10 = (f32[32,128]{1,0:T(8,128)S(1)}, f32[32,128]{1,0:T(8,128)S(1)}, u32[]{:S(2)}, u32[]{:S(2)}) collective-permute-start(f32[32,128]{1,0:T(8,128)S(1)} %slice_select_fusion.1), channel_id=1, source_target_pairs={{0,32},{16,48},{32,0},{48,16},{64,96},{80,112},{96,64},{112,80},{1... | collective-permute-start | bytes 49160 | tf_op jit(solution)/shard_map/ppermute | solution.py:350
  185.1 30.1 %collective-permute-start.11 = (f32[32,128]{1,0:T(8,128)S(1)}, f32[32,128]{1,0:T(8,128)S(1)}, u32[]{:S(2)}, u32[]{:S(2)}) collective-permute-start(f32[32,128]{1,0:T(8,128)S(1)} %select_add_fusion.1), channel_id=1, source_target_pairs={{0,64},{16,80},{32,96},{48,112},{64,0},{80,16},{96,32},{112,48},{1... | collective-permute-start | bytes 49160 | tf_op jit(solution)/shard_map/ppermute | solution.py:350
  215.2 6.5 %collective-permute-start.12 = (f32[32,128]{1,0:T(8,128)S(1)}, f32[32,128]{1,0:T(8,128)S(1)}, u32[]{:S(2)}, u32[]{:S(2)}) collective-permute-start(f32[32,128]{1,0:T(8,128)S(1)} %add.31), channel_id=1, source_target_pairs={{0,128},{16,144},{32,160},{48,176},{64,192},{80,208},{96,224},{112... | collective-permute-start | bytes 49160 | tf_op jit(solution)/shard_map/ppermute | solution.py:350
  221.7 9.7 %collective-permute-start.13 = (f32[32,128]{1,0:T(8,128)S(1)}, f32[32,128]{1,0:T(8,128)S(1)}, u32[]{:S(2)}, u32[]{:S(2)}) collective-permute-start(f32[32,128]{1,0:T(8,128)S(1)} %add.32), channel_id=1, source_target_pairs={{0,256},{16,272},{32,288},{48,304},{64,320},{80,336},{96,352},{112... | collective-permute-start | bytes 49160 | tf_op jit(solution)/shard_map/ppermute | solution.py:350
  231.4 3.1 %collective-permute-start.14 = (f32[32,128]{1,0:T(8,128)S(1)}, f32[32,128]{1,0:T(8,128)S(1)}, u32[]{:S(2)}, u32[]{:S(2)}) collective-permute-start(f32[32,128]{1,0:T(8,128)S(1)} %add.33), channel_id=1, source_target_pairs={{0,1},{1,0},{2,3},{3,2},{4,5},{5,4},{6,7},{7,6},{8,9},{9,8},{10,11... | collective-permute-start | bytes 49160 | tf_op jit(solution)/shard_map/ppermute | solution.py:350
  234.5 5.6 %collective-permute-start.15 = (f32[32,128]{1,0:T(8,128)S(1)}, f32[32,128]{1,0:T(8,128)S(1)}, u32[]{:S(2)}, u32[]{:S(2)}) collective-permute-start(f32[32,128]{1,0:T(8,128)S(1)} %add.34), channel_id=1, source_target_pairs={{0,2},{1,3},{2,0},{3,1},{4,6},{5,7},{6,4},{7,5},{8,10},{9,11},{10,... | collective-permute-start | bytes 49160 | tf_op jit(solution)/shard_map/ppermute | solution.py:350
  240.1 6.5 %collective-permute-start.16 = (f32[32,128]{1,0:T(8,128)S(1)}, f32[32,128]{1,0:T(8,128)S(1)}, u32[]{:S(2)}, u32[]{:S(2)}) collective-permute-start(f32[32,128]{1,0:T(8,128)S(1)} %add.35), channel_id=1, source_target_pairs={{0,4},{1,5},{2,6},{3,7},{4,0},{5,1},{6,2},{7,3},{8,12},{9,13},{10,... | collective-permute-start | bytes 49160 | tf_op jit(solution)/shard_map/ppermute | solution.py:350
  246.6 9.5 %collective-permute-start.17 = (f32[32,128]{1,0:T(8,128)S(1)}, f32[32,128]{1,0:T(8,128)S(1)}, u32[]{:S(2)}, u32[]{:S(2)}) collective-permute-start(f32[32,128]{1,0:T(8,128)S(1)} %add.36), channel_id=1, source_target_pairs={{0,8},{1,9},{2,10},{3,11},{4,12},{5,13},{6,14},{7,15},{8,0},{9,1},... | collective-permute-start | bytes 49160 | tf_op jit(solution)/shard_map/ppermute | solution.py:350
  256.2 7.2 %collective-permute-start.18 = (f32[32,128]{1,0:T(8,128)S(1)}, f32[32,128]{1,0:T(8,128)S(1)}, u32[]{:S(2)}, u32[]{:S(2)}) collective-permute-start(f32[32,128]{1,0:T(8,128)S(1)} %add.37), channel_id=1, source_target_pairs={{0,32},{16,48},{32,0},{48,16},{64,96},{80,112},{96,64},{112,80},{1... | collective-permute-start | bytes 49160 | tf_op jit(solution)/shard_map/ppermute | solution.py:350
  263.4 25.3 %collective-permute-start.19 = (f32[64,128]{1,0:T(8,128)S(1)}, f32[64,128]{1,0:T(8,128)S(1)}, u32[]{:S(2)}, u32[]{:S(2)}) collective-permute-start(f32[64,128]{1,0:T(8,128)S(1)} %pad_maximum_fusion), channel_id=1, source_target_pairs={{0,16},{16,0},{32,48},{48,32},{64,80},{80,64},{96,112},{112,96},{1... | collective-permute-start | bytes 98312 | tf_op jit(solution)/shard_map/ppermute | solution.py:350
  267.3 5.5 %collective-permute-start.20 = (s32[4,128]{1,0:T(4,128)S(1)}, s32[4,128]{1,0:T(4,128)S(1)}, u32[]{:S(2)}, u32[]{:S(2)}) collective-permute-start(s32[4,128]{1,0:T(4,128)S(1)} %pad_add_fusion), channel_id=1, source_target_pairs={{0,64},{16,80},{32,96},{48,112},{64,0},{80,16},{96,32},{112,48},{1... | collective-permute-start | bytes 6152 | tf_op jit(solution)/shard_map/ppermute | solution.py:350
  272.8 6.4 %collective-permute-start.21 = (s32[8,128]{1,0:T(8,128)S(1)}, s32[8,128]{1,0:T(8,128)S(1)}, u32[]{:S(2)}, u32[]{:S(2)}) collective-permute-start(s32[8,128]{1,0:T(8,128)S(1)} %concatenate.24), channel_id=1, source_target_pairs={{0,128},{16,144},{32,160},{48,176},{64,192},{80,208},{96,224},{112... | collective-permute-start | bytes 12296 | tf_op jit(solution)/shard_map/ppermute | solution.py:350
  279.2 9.4 %collective-permute-start.22 = (s32[16,128]{1,0:T(8,128)S(1)}, s32[16,128]{1,0:T(8,128)S(1)}, u32[]{:S(2)}, u32[]{:S(2)}) collective-permute-start(s32[16,128]{1,0:T(8,128)S(1)} %concatenate.25), channel_id=1, source_target_pairs={{0,256},{16,272},{32,288},{48,304},{64,320},{80,336},{96,352},{112... | collective-permute-start | bytes 24584 | tf_op jit(solution)/shard_map/ppermute | solution.py:350
